TPU v7x, 32 devices: a whole 2x2x4 slice. The times are simulated.
32 devices in a mesh: seq: 16 (over z, y, core), head: 2 (over x).
Axes of the slice: x: 2, y: 2, z: 4, core: 2. Of those that a mesh axis runs over, the one named last changes fastest.
Arguments:
- queries: bfloat16 [4096, 512], P('seq', 'head'), may hold values from -4 to 4
- values: bfloat16 [4096, 512], P('seq', 'head'), may hold values from -6 to 6
- scales: float32 [4096, 8], P('seq', 'head'), may hold values from 2 to 20
- block_reach: int32 [16], P('seq'), may hold values from 1 to 4
- out_weight: bfloat16 [512, 1024], P('head'), may hold values from -0.25 to 0.25
- out_grad: bfloat16 [4096, 512], P('seq', 'head'), may hold values from -6 to 6
Outputs:
- mixed: bfloat16 [4096, 1024], P(('seq', 'head'))
- value_grad: bfloat16 [4096, 512], P('seq', 'head')
All inputs are finite; a program needn't handle non-finite values.
Results may differ from a plain program's by a relative error of at most 0.0015.
The roundings to bfloat16 on the way count: a program that leaves them out, or rounds other values in their place, can miss the bound.
Values may be sent and summed in bfloat16 or wider, within the bound.
No kernel may reach another device: no remote copies, remote signals or barrier semaphores. Data moves between devices by JAX's collectives and lax.ppermute only.
A program may use at most 64 MiB of HBM per device.

v0:
```python
import jax
import jax.numpy as jnp
from jax import lax
from jax.sharding import PartitionSpec as P

HD = 64
WINDOW = 4


NEGATIVE = -1e30


def from_behind(value, axis, steps):
    count = lax.axis_size(axis)
    initial, last = (max(0, -steps), min(count, count - steps))
    return lax.ppermute(value, axis, [(source, source + steps) for source in range(initial, last)])


def unit_keys(queries, scales):
    as_float = queries.astype(jnp.float32).reshape(queries.shape[0], scales.shape[1], HD)
    direction = as_float * lax.rsqrt(jnp.sum(as_float * as_float, axis=-1, keepdims=True) + 1e-06)
    return (direction * scales[:, :, None]).astype(jnp.bfloat16)


def tile_scores(row_keys, column_keys):
    return jnp.einsum("ihd,jhd->hij", row_keys, column_keys, preferred_element_type=jnp.float32)


def row_part(scores, allowed, column_values):
    tile_top = jnp.max(scores, axis=2)
    exponent = jnp.exp(scores - tile_top[:, :, None]) * allowed
    numerator = jnp.einsum(
        "hij,jhd->ihd",
        exponent.astype(jnp.bfloat16),
        column_values,
        preferred_element_type=jnp.float32,
    )
    return (jnp.where(allowed > 0, tile_top, NEGATIVE), jnp.sum(exponent, axis=2), numerator)


def column_part(scores, allowed, row_values):
    tile_top = jnp.max(scores, axis=1)
    exponent = jnp.exp(scores - tile_top[:, None, :]) * allowed
    numerator = jnp.einsum(
        "hij,ihd->jhd",
        exponent.astype(jnp.bfloat16),
        row_values,
        preferred_element_type=jnp.float32,
    )
    return (jnp.where(allowed > 0, tile_top, NEGATIVE), jnp.sum(exponent, axis=1), numerator)


def merge_stats(former, latter):
    top_one = jnp.where(former[1] > 0, former[0], NEGATIVE)
    top_two = jnp.where(latter[1] > 0, latter[0], NEGATIVE)
    maximum = jnp.maximum(top_one, top_two)
    factor_one = jnp.exp(top_one - maximum)
    factor_two = jnp.exp(top_two - maximum)
    summed = factor_one * former[1] + factor_two * latter[1]
    numerator = former[2] * factor_one.T[:, :, None] + latter[2] * factor_two.T[:, :, None]
    return (maximum, summed, numerator)


def packed(stats):
    return (stats[0], stats[1], stats[2].reshape(stats[2].shape[0], -1))


def unpacked(stats, head_count):
    return (stats[0], stats[1], stats[2].reshape(stats[2].shape[0], head_count, -1))


def shards(queries, values, scales, block_reach, out_weight, out_grad):
    length = queries.shape[0]
    head_count = scales.shape[1]
    key_rows = unit_keys(queries, scales)
    key_flat = key_rows.reshape(length, head_count * HD)
    value_rows = values.reshape(length, head_count, HD)
    diagonal = jnp.eye(length, dtype=bool)
    self_scores = jnp.where(diagonal[None], NEGATIVE, tile_scores(key_rows, key_rows))
    running = row_part(self_scores, 1.0, value_rows)
    partials = []
    visitors = []
    moving = (key_flat, values, block_reach)
    for distance in range(1, WINDOW + 1):
        moving = from_behind((moving[0], moving[1], moving[2]), "seq", 1)
        far_keys = moving[0].reshape(length, head_count, HD)
        far_values = moving[1].reshape(length, head_count, HD)
        allowed = (distance <= jnp.minimum(block_reach[0], moving[2][0])).astype(jnp.float32)
        scores = tile_scores(key_rows, far_keys)
        running = merge_stats(running, row_part(scores, allowed, far_values))
        partials.append(column_part(scores, allowed, value_rows))
        visitors.append((far_keys, allowed))
    for distance in range(1, WINDOW + 1):
        returned = from_behind(packed(partials[distance - 1]), "seq", -distance)
        running = merge_stats(running, unpacked(returned, head_count))
    row_top, totals, numerator = running
    attended = (
        (numerator / totals.T[:, :, None]).astype(jnp.bfloat16).reshape(length, head_count * HD)
    )
    mixed = lax.psum_scatter(
        jnp.dot(attended, out_weight, preferred_element_type=jnp.float32),
        "head",
        scatter_dimension=0,
        tiled=True,
    ).astype(jnp.bfloat16)
    grad_rows = out_grad.reshape(length, head_count, HD)
    own_weights = (jnp.exp(self_scores - row_top[:, :, None]) / totals[:, :, None]).astype(
        jnp.bfloat16
    )
    grad_here = jnp.einsum(
        "hij,ihd->jhd", own_weights, grad_rows, preferred_element_type=jnp.float32
    )
    returns = []
    travel_grad = out_grad
    travel_stats = (row_top, totals)
    for distance in range(1, WINDOW + 1):
        travel_grad = from_behind(travel_grad, "seq", 1)
        travel_stats = from_behind((travel_stats[0], travel_stats[1]), "seq", 1)
        far_keys, allowed = visitors[distance - 1]
        far_grads = travel_grad.reshape(length, head_count, HD)
        far_top = travel_stats[0]
        far_total = travel_stats[1]
        scores = tile_scores(key_rows, far_keys)
        near_weights = jnp.where(
            allowed > 0, jnp.exp(scores - row_top[:, :, None]) / totals[:, :, None], 0.0
        ).astype(jnp.bfloat16)
        returns.append(
            jnp.einsum("hij,ihd->jhd", near_weights, grad_rows, preferred_element_type=jnp.float32)
        )
        far_weights = jnp.where(
            allowed > 0, jnp.exp(scores - far_top[:, None, :]) / far_total[:, None, :], 0.0
        ).astype(jnp.bfloat16)
        grad_here = grad_here + jnp.einsum(
            "hij,jhd->ihd", far_weights, far_grads, preferred_element_type=jnp.float32
        )
    for distance in range(1, WINDOW + 1):
        returned = from_behind(returns[distance - 1].reshape(length, -1), "seq", -distance)
        grad_here = grad_here + returned.reshape(length, head_count, HD)
    value_grad = grad_here.astype(jnp.bfloat16).reshape(length, head_count * HD)
    return (mixed, value_grad)


def solution(mesh):
    return jax.shard_map(
        shards,
        mesh=mesh,
        in_specs=(
            P("seq", "head"),
            P("seq", "head"),
            P("seq", "head"),
            P("seq"),
            P("head", None),
            P("seq", "head"),
        ),
        out_specs=(P(("seq", "head"), None), P("seq", "head")),
        check_vma=False,
    )
```

profile of v0, /device:TPU:8, one launch (start us, length us, event | category | flops | bytes accessed | tf_op | source)
XLA Modules:
  0.0 201.1 jit_solution(973224636411914071)
XLA Ops:
  9.1 2.1 %collective-permute-start = (bf16[256,256]{0,1:T(8,128)(2,1)S(1)}, bf16[256,256]{0,1:T(8,128)(2,1)S(1)}, u32[]{:S(2)}, u32[]{:S(2)}) collective-permute-start(bf16[256,256]{0,1:T(8,128)(2,1)S(1)} %fusion.88), channel_id=1, source_target_pairs={{0,2},{2,4},{4,6},{6,8},{8,10},{10,12},{12,14},{14,16},{16,18},{18... | collective-permute-start | bytes 393224 | tf_op jit(solution)/shard_map/ppermute | solution.py:16
  11.1 3.5 %collective-permute-start.1 = (s32[1]{0:T(128)}, s32[1]{0:T(128)}, u32[]{:S(2)}, u32[]{:S(2)}) collective-permute-start(s32[1]{0:T(128)} %param.9), channel_id=1, source_target_pairs={{0,2},{2,4},{4,6},{6,8},{8,10},{10,12},{12,14},{14,16},{16,18},{18... | collective-permute-start | bytes 20 | tf_op jit(solution)/shard_map/ppermute | solution.py:16
  14.7 1.9 collective-permute-start.2
  16.6 3.5 %collective-permute-start.26 = (bf16[256,256]{1,0:T(8,128)(2,1)S(1)}, bf16[256,256]{1,0:T(8,128)(2,1)}, u32[]{:S(2)}, u32[]{:S(2)}) collective-permute-start(bf16[256,256]{1,0:T(8,128)(2,1)S(1)} %copy-done.13), channel_id=1, source_target_pairs={{0,2},{2,4},{4,6},{6,8},{8,10},{10,12},{12,14},{14,16},{16,18},{18... | collective-permute-start | bytes 393224 | tf_op jit(solution)/shard_map/ppermute | solution.py:16
  23.8 1.9 collective-permute-start.4
  25.8 4.0 %collective-permute-done.4 = s32[1]{0:T(128)} collective-permute-done((s32[1]{0:T(128)}, s32[1]{0:T(128)}, u32[]{:S(2)}, u32[]{:S(2)}) %collective-permute-start.4) | collective-permute-done | bytes 36 | tf_op jit(solution)/shard_map/ppermute | solution.py:16
  30.4 1.9 collective-permute-start.7
  32.4 4.0 %collective-permute-done.7 = s32[1]{0:T(128)} collective-permute-done((s32[1]{0:T(128)}, s32[1]{0:T(128)}, u32[]{:S(2)}, u32[]{:S(2)}) %collective-permute-start.7) | collective-permute-done | bytes 36 | tf_op jit(solution)/shard_map/ppermute | solution.py:16
  37.0 1.9 collective-permute-start.10
  38.9 4.0 %collective-permute-done.10 = s32[1]{0:T(128)} collective-permute-done((s32[1]{0:T(128)}, s32[1]{0:T(128)}, u32[]{:S(2)}, u32[]{:S(2)}) %collective-permute-start.10) | collective-permute-done | bytes 36 | tf_op jit(solution)/shard_map/ppermute | solution.py:16
  44.0 1.3 copy.61
  45.6 1.9 collective-permute-start.14
  48.2 1.9 collective-permute-start.13
  51.1 1.9 collective-permute-start.12
  53.1 2.4 %collective-permute-start.3 = (bf16[256,256]{0,1:T(8,128)(2,1)S(1)}, bf16[256,256]{0,1:T(8,128)(2,1)S(1)}, u32[]{:S(2)}, u32[]{:S(2)}) collective-permute-start(bf16[256,256]{0,1:T(8,128)(2,1)S(1)} %collective-permute-done), channel_id=1, source_target_pairs={{0,2},{2,4},{4,6},{6,8},{8,10},{10,12},{12,14},{14,16},{16,18},{18... | collective-permute-start | bytes 393224 | tf_op jit(solution)/shard_map/ppermute | solution.py:16
  55.6 3.6 %collective-permute-start.5 = (bf16[256,256]{1,0:T(8,128)(2,1)S(1)}, bf16[256,256]{1,0:T(8,128)(2,1)}, u32[]{:S(2)}, u32[]{:S(2)}) collective-permute-start(bf16[256,256]{1,0:T(8,128)(2,1)S(1)} %collective-permute-done.2), channel_id=1, source_target_pairs={{0,2},{2,4},{4,6},{6,8},{8,10},{10,12},{12,14},{14,16},{16,18},{18... | collective-permute-start | bytes 393224 | tf_op jit(solution)/shard_map/ppermute | solution.py:16
  59.2 1.7 copy.62
  61.5 2.4 %collective-permute-start.29 = (bf16[256,256]{1,0:T(8,128)(2,1)}, bf16[256,256]{1,0:T(8,128)(2,1)}, u32[]{:S(2)}, u32[]{:S(2)}) collective-permute-start(bf16[256,256]{1,0:T(8,128)(2,1)} %collective-permute-done.26), channel_id=1, source_target_pairs={{0,2},{2,4},{4,6},{6,8},{8,10},{10,12},{12,14},{14,16},{16,18},{18... | collective-permute-start | bytes 393224 | tf_op jit(solution)/shard_map/ppermute | solution.py:16
  64.4 1.3 copy.64
  66.3 2.7 %collective-permute-start.16 = (f32[4,256]{1,0:T(4,128)}, f32[4,256]{1,0:T(4,128)}, u32[]{:S(2)}, u32[]{:S(2)}) collective-permute-start(f32[4,256]{1,0:T(4,128)} %broadcast_select_fusion.1), channel_id=1, source_target_pairs={{4,0},{6,2},{8,4},{10,6},{12,8},{14,10},{16,12},{18,14},{20,16},{2... | collective-permute-start | bytes 12296 | tf_op jit(solution)/shard_map/ppermute | solution.py:16
  71.1 3.4 %collective-permute-start.6 = (bf16[256,256]{0,1:T(8,128)(2,1)S(1)}, bf16[256,256]{0,1:T(8,128)(2,1)}, u32[]{:S(2)}, u32[]{:S(2)}) collective-permute-start(bf16[256,256]{0,1:T(8,128)(2,1)S(1)} %collective-permute-done.3), channel_id=1, source_target_pairs={{0,2},{2,4},{4,6},{6,8},{8,10},{10,12},{12,14},{14,16},{16,18},{18... | collective-permute-start | bytes 393224 | tf_op jit(solution)/shard_map/ppermute | solution.py:16
  74.4 1.6 copy.65
  77.2 1.2 collective-permute-done.6
  78.3 1.9 collective-permute-start.8
  80.3 2.8 %fusion.121 = (f32[4,256]{1,0:T(4,128)}, f32[4,256]{1,0:T(4,128)S(1)}, f32[4,256,256]{2,1,0:T(8,128)}) fusion(bf16[256,4,64]{0,2,1:T(8,128)(2,1)S(1)} %multiply_convert_fusion, bf16[256,4,64]{0,2,1:T(8,128)(2,1)} %bitcast.19), kind=kOutput, calls=%fused_computation.204 | convolution fusion | flops 34076672 | bytes 1318912 | tf_op jit(solution)/shard_map/ihd,jhd->hij/dot_general | solution.py:26
  83.1 2.5 %copy.67 = f32[4,256,256]{1,2,0:T(8,128)} copy(f32[4,256,256]{2,1,0:T(8,128)} %get-tuple-element.59) | data formatting | bytes 2097152 | tf_op jit(solution)/shard_map/ihd,jhd->hij/dot_general | solution.py:26
  85.6 2.2 %fusion.48 = f32[4,256,64]{1,2,0:T(8,128)} fusion(bf16[256,4,64]{0,2,1:T(8,128)(2,1)S(1)} %bitcast.279, f32[4,256,256]{2,1,0:T(8,128)} %get-tuple-element.59, f32[4,256]{1,0:T(4,128)} %get-tuple-element.18, f32[]{:T(128)} %bitcast.20), kind=kOutput, calls=%fused_computation.75 | convolution fusion | flops 34340864 | bytes 1445892 | tf_op jit(solution)/shard_map/hij,ihd->jhd/dot_general | solution.py:44
  88.5 2.5 %collective-permute-start.32 = (bf16[256,256]{1,0:T(8,128)(2,1)}, bf16[256,256]{1,0:T(8,128)(2,1)}, u32[]{:S(2)}, u32[]{:S(2)}) collective-permute-start(bf16[256,256]{1,0:T(8,128)(2,1)} %collective-permute-done.29), channel_id=1, source_target_pairs={{0,2},{2,4},{4,6},{6,8},{8,10},{10,12},{12,14},{14,16},{16,18},{18... | collective-permute-start | bytes 393224 | tf_op jit(solution)/shard_map/ppermute | solution.py:16
  92.0 1.3 broadcast_select_fusion
  93.3 2.7 %collective-permute-done.32 = bf16[256,256]{1,0:T(8,128)(2,1)} collective-permute-done((bf16[256,256]{1,0:T(8,128)(2,1)}, bf16[256,256]{1,0:T(8,128)(2,1)}, u32[]{:S(2)}, u32[]{:S(2)}) %collective-permute-start.32) | collective-permute-done | bytes 131104 | tf_op jit(solution)/shard_map/ppermute | solution.py:16
  96.0 1.9 collective-permute-start.9
  98.0 1.7 copy.68
  99.6 1.7 fusion.43
  101.3 2.2 %collective-permute-done.9 = bf16[256,256]{0,1:T(8,128)(2,1)} collective-permute-done((bf16[256,256]{0,1:T(8,128)(2,1)}, bf16[256,256]{0,1:T(8,128)(2,1)}, u32[]{:S(2)}, u32[]{:S(2)}) %collective-permute-start.9) | collective-permute-done | bytes 131104 | tf_op jit(solution)/shard_map/ppermute | solution.py:16
  103.5 1.9 collective-permute-start.15
  105.5 1.5 fusion.122
  113.0 1.9 collective-permute-start.19
  115.0 1.9 collective-permute-start.18
  117.7 2.5 %collective-permute-start.11 = (bf16[256,256]{1,0:T(8,128)(2,1)S(1)}, bf16[256,256]{1,0:T(8,128)(2,1)S(1)}, u32[]{:S(2)}, u32[]{:S(2)}) collective-permute-start(bf16[256,256]{1,0:T(8,128)(2,1)S(1)} %copy-done.19), channel_id=1, source_target_pairs={{0,2},{2,4},{4,6},{6,8},{8,10},{10,12},{12,14},{14,16},{16,18},{18... | collective-permute-start | bytes 393224 | tf_op jit(solution)/shard_map/ppermute | solution.py:16
  120.2 3.5 %collective-permute-start.35 = (bf16[256,256]{1,0:T(8,128)(2,1)}, bf16[256,256]{1,0:T(8,128)(2,1)S(1)}, u32[]{:S(2)}, u32[]{:S(2)}) collective-permute-start(bf16[256,256]{1,0:T(8,128)(2,1)} %collective-permute-done.32), channel_id=1, source_target_pairs={{0,2},{2,4},{4,6},{6,8},{8,10},{10,12},{12,14},{14,16},{16,18},{18... | collective-permute-start | bytes 393224 | tf_op jit(solution)/shard_map/ppermute | solution.py:16
  124.4 1.9 collective-permute-start.22
  126.3 1.9 collective-permute-start.21
  129.0 1.6 copy.70
  130.6 2.1 %collective-permute-start.17 = (f32[256,256]{0,1:T(8,128)S(1)}, f32[256,256]{0,1:T(8,128)}, u32[]{:S(2)}, u32[]{:S(2)}) collective-permute-start(f32[256,256]{0,1:T(8,128)S(1)} %bitcast.286), channel_id=1, source_target_pairs={{4,0},{6,2},{8,4},{10,6},{12,8},{14,10},{16,12},{18,14},{20,16},{2... | collective-permute-start | bytes 786440 | tf_op jit(solution)/shard_map/ppermute | solution.py:16
  132.8 2.1 %collective-permute-start.20 = (f32[256,256]{0,1:T(8,128)S(1)}, f32[256,256]{0,1:T(8,128)}, u32[]{:S(2)}, u32[]{:S(2)}) collective-permute-start(f32[256,256]{0,1:T(8,128)S(1)} %bitcast.287), channel_id=1, source_target_pairs={{6,0},{8,2},{10,4},{12,6},{14,8},{16,10},{18,12},{20,14},{22,16},{... | collective-permute-start | bytes 786440 | tf_op jit(solution)/shard_map/ppermute | solution.py:16
  135.0 1.9 collective-permute-start.23
  137.0 2.0 %collective-permute-start.25 = (f32[4,256]{1,0:T(4,128)S(1)}, f32[4,256]{1,0:T(4,128)S(1)}, u32[]{:S(2)}, u32[]{:S(2)}) collective-permute-start(f32[4,256]{1,0:T(4,128)S(1)} %get-tuple-element.48), channel_id=1, source_target_pairs={{0,2},{2,4},{4,6},{6,8},{8,10},{10,12},{12,14},{14,16},{16,18},{18... | collective-permute-start | bytes 12296 | tf_op jit(solution)/shard_map/ppermute | solution.py:16
  140.0 3.9 %collective-permute-start.24 = (f32[4,256]{1,0:T(4,128)S(1)}, f32[4,256]{1,0:T(4,128)S(1)}, u32[]{:S(2)}, u32[]{:S(2)}) collective-permute-start(f32[4,256]{1,0:T(4,128)S(1)} %get-tuple-element.38), channel_id=1, source_target_pairs={{0,2},{2,4},{4,6},{6,8},{8,10},{10,12},{12,14},{14,16},{16,18},{18... | collective-permute-start | bytes 12296 | tf_op jit(solution)/shard_map/ppermute | solution.py:16
  144.0 1.9 collective-permute-start.39
  145.9 7.8 %collective-permute-done.23 = f32[256,256]{0,1:T(8,128)S(1)} collective-permute-done((f32[256,256]{0,1:T(8,128)S(1)}, f32[256,256]{0,1:T(8,128)S(1)}, u32[]{:S(2)}, u32[]{:S(2)}) %collective-permute-start.23) | collective-permute-done | bytes 262176 | tf_op jit(solution)/shard_map/ppermute | solution.py:16
  154.4 1.5 fusion.26
  156.0 1.4 fusion.129
  157.7 2.1 %collective-permute-start.38 = (f32[256,256]{0,1:T(8,128)S(1)}, f32[256,256]{0,1:T(8,128)S(1)}, u32[]{:S(2)}, u32[]{:S(2)}) collective-permute-start(f32[256,256]{0,1:T(8,128)S(1)} %bitcast.307), channel_id=1, source_target_pairs={{6,0},{8,2},{10,4},{12,6},{14,8},{16,10},{18,12},{20,14},{22,16},{... | collective-permute-start | bytes 786440 | tf_op jit(solution)/shard_map/ppermute | solution.py:16
  160.1 2.1 %collective-permute-start.37 = (f32[256,256]{0,1:T(8,128)S(1)}, f32[256,256]{0,1:T(8,128)S(1)}, u32[]{:S(2)}, u32[]{:S(2)}) collective-permute-start(f32[256,256]{0,1:T(8,128)S(1)} %bitcast.308), channel_id=1, source_target_pairs={{4,0},{6,2},{8,4},{10,6},{12,8},{14,10},{16,12},{18,14},{20,16},{2... | collective-permute-start | bytes 786440 | tf_op jit(solution)/shard_map/ppermute | solution.py:16
  162.5 3.0 %collective-permute-start.28 = (f32[4,256]{1,0:T(4,128)S(1)}, f32[4,256]{1,0:T(4,128)S(1)}, u32[]{:S(2)}, u32[]{:S(2)}) collective-permute-start(f32[4,256]{1,0:T(4,128)S(1)} %collective-permute-done.25), channel_id=1, source_target_pairs={{0,2},{2,4},{4,6},{6,8},{8,10},{10,12},{12,14},{14,16},{16,18},{18... | collective-permute-start | bytes 12296 | tf_op jit(solution)/shard_map/ppermute | solution.py:16
  165.8 3.1 %collective-permute-start.27 = (f32[4,256]{1,0:T(4,128)S(1)}, f32[4,256]{1,0:T(4,128)S(1)}, u32[]{:S(2)}, u32[]{:S(2)}) collective-permute-start(f32[4,256]{1,0:T(4,128)S(1)} %collective-permute-done.24), channel_id=1, source_target_pairs={{0,2},{2,4},{4,6},{6,8},{8,10},{10,12},{12,14},{14,16},{16,18},{18... | collective-permute-start | bytes 12296 | tf_op jit(solution)/shard_map/ppermute | solution.py:16
  168.9 2.6 %collective-permute-start.31 = (f32[4,256]{1,0:T(4,128)S(1)}, f32[4,256]{1,0:T(4,128)S(1)}, u32[]{:S(2)}, u32[]{:S(2)}) collective-permute-start(f32[4,256]{1,0:T(4,128)S(1)} %collective-permute-done.28), channel_id=1, source_target_pairs={{0,2},{2,4},{4,6},{6,8},{8,10},{10,12},{12,14},{14,16},{16,18},{18... | collective-permute-start | bytes 12296 | tf_op jit(solution)/shard_map/ppermute | solution.py:16
  172.2 4.2 %collective-permute-start.30 = (f32[4,256]{1,0:T(4,128)S(1)}, f32[4,256]{1,0:T(4,128)S(1)}, u32[]{:S(2)}, u32[]{:S(2)}) collective-permute-start(f32[4,256]{1,0:T(4,128)S(1)} %collective-permute-done.27), channel_id=1, source_target_pairs={{0,2},{2,4},{4,6},{6,8},{8,10},{10,12},{12,14},{14,16},{16,18},{18... | collective-permute-start | bytes 12296 | tf_op jit(solution)/shard_map/ppermute | solution.py:16
  176.5 1.9 collective-permute-start.34
  179.2 4.5 %collective-permute-start.36 = (f32[256,256]{0,1:T(8,128)S(1)}, f32[256,256]{0,1:T(8,128)S(1)}, u32[]{:S(2)}, u32[]{:S(2)}) collective-permute-start(f32[256,256]{0,1:T(8,128)S(1)} %bitcast.309), channel_id=1, source_target_pairs={{2,0},{4,2},{6,4},{8,6},{10,8},{12,10},{14,12},{16,14},{18,16},{20... | collective-permute-start | bytes 786440 | tf_op jit(solution)/shard_map/ppermute | solution.py:16
  183.7 1.9 collective-permute-start.33
  186.4 3.1 %collective-permute-done.33 = f32[4,256]{1,0:T(4,128)S(1)} collective-permute-done((f32[4,256]{1,0:T(4,128)S(1)}, f32[4,256]{1,0:T(4,128)S(1)}, u32[]{:S(2)}, u32[]{:S(2)}) %collective-permute-start.33) | collective-permute-done | bytes 4128 | tf_op jit(solution)/shard_map/ppermute | solution.py:16
  190.3 1.5 fusion.27
  192.5 1.8 convert_element_type.117
  (152 shorter events, 28.4 us)
Async XLA Ops:
  7.2 148.8 %copy-start = (bf16[256,1024]{1,0:T(8,128)(2,1)S(1)}, bf16[256,1024]{1,0:T(8,128)(2,1)}, u32[]{:S(2)}) copy-start(bf16[256,1024]{1,0:T(8,128)(2,1)} %param.10) | copy-start | bytes 1572868
  7.2 185.3 %reduce-scatter.2.cloned.1.call-start = ((), (), s32[]{:S(2)}) async-start(), calls=%async_computation.1 | async-start | bytes 1572864 | tf_op jit(solution)/shard_map/reduce_scatter | solution.py:100
  9.0 5.6 %copy-start.12 = (bf16[256,256]{1,0:T(8,128)(2,1)S(1)}, bf16[256,256]{1,0:T(8,128)(2,1)}, u32[]{:S(2)}) copy-start(bf16[256,256]{1,0:T(8,128)(2,1)} %param.7) | copy-start | bytes 393220
  9.0 7.6 %copy-start.13 = (bf16[256,256]{1,0:T(8,128)(2,1)S(1)}, bf16[256,256]{1,0:T(8,128)(2,1)}, u32[]{:S(2)}) copy-start(bf16[256,256]{1,0:T(8,128)(2,1)} %param.11) | copy-start | bytes 393220
  9.1 34.5 %collective-permute-start = (bf16[256,256]{0,1:T(8,128)(2,1)S(1)}, bf16[256,256]{0,1:T(8,128)(2,1)S(1)}, u32[]{:S(2)}, u32[]{:S(2)}) collective-permute-start(bf16[256,256]{0,1:T(8,128)(2,1)S(1)} %fusion.88), channel_id=1, source_target_pairs={{0,2},{2,4},{4,6},{6,8},{8,10},{10,12},{12,14},{14,16},{16,18},{18... | collective-permute-start | bytes 393224 | tf_op jit(solution)/shard_map/ppermute | solution.py:16
  11.1 12.1 %collective-permute-start.1 = (s32[1]{0:T(128)}, s32[1]{0:T(128)}, u32[]{:S(2)}, u32[]{:S(2)}) collective-permute-start(s32[1]{0:T(128)} %param.9), channel_id=1, source_target_pairs={{0,2},{2,4},{4,6},{6,8},{8,10},{10,12},{12,14},{14,16},{16,18},{18... | collective-permute-start | bytes 20 | tf_op jit(solution)/shard_map/ppermute | solution.py:16
  14.7 38.4 %collective-permute-start.2 = (bf16[256,256]{1,0:T(8,128)(2,1)S(1)}, bf16[256,256]{1,0:T(8,128)(2,1)S(1)}, u32[]{:S(2)}, u32[]{:S(2)}) collective-permute-start(bf16[256,256]{1,0:T(8,128)(2,1)S(1)} %copy-done.12), channel_id=1, source_target_pairs={{0,2},{2,4},{4,6},{6,8},{8,10},{10,12},{12,14},{14,16},{16,18},{18... | collective-permute-start | bytes 393224 | tf_op jit(solution)/shard_map/ppermute | solution.py:16
  16.6 39.0 %collective-permute-start.26 = (bf16[256,256]{1,0:T(8,128)(2,1)S(1)}, bf16[256,256]{1,0:T(8,128)(2,1)}, u32[]{:S(2)}, u32[]{:S(2)}) collective-permute-start(bf16[256,256]{1,0:T(8,128)(2,1)S(1)} %copy-done.13), channel_id=1, source_target_pairs={{0,2},{2,4},{4,6},{6,8},{8,10},{10,12},{12,14},{14,16},{16,18},{18... | collective-permute-start | bytes 393224 | tf_op jit(solution)/shard_map/ppermute | solution.py:16
  23.2 37.7 %copy-start.20 = (f32[4,256]{1,0:T(4,128)}, f32[4,256]{1,0:T(4,128)S(1)}, u32[]{:S(2)}) copy-start(f32[4,256]{1,0:T(4,128)S(1)} %fusion.28) | copy-start | bytes 12292
  23.8 6.0 %collective-permute-start.4 = (s32[1]{0:T(128)}, s32[1]{0:T(128)}, u32[]{:S(2)}, u32[]{:S(2)}) collective-permute-start(s32[1]{0:T(128)} %collective-permute-done.1), channel_id=1, source_target_pairs={{0,2},{2,4},{4,6},{6,8},{8,10},{10,12},{12,14},{14,16},{16,18},{18... | collective-permute-start | bytes 20 | tf_op jit(solution)/shard_map/ppermute | solution.py:16
  30.4 6.0 %collective-permute-start.7 = (s32[1]{0:T(128)}, s32[1]{0:T(128)}, u32[]{:S(2)}, u32[]{:S(2)}) collective-permute-start(s32[1]{0:T(128)} %collective-permute-done.4), channel_id=1, source_target_pairs={{0,2},{2,4},{4,6},{6,8},{8,10},{10,12},{12,14},{14,16},{16,18},{18... | collective-permute-start | bytes 20 | tf_op jit(solution)/shard_map/ppermute | solution.py:16
  37.0 6.0 %collective-permute-start.10 = (s32[1]{0:T(128)}, s32[1]{0:T(128)}, u32[]{:S(2)}, u32[]{:S(2)}) collective-permute-start(s32[1]{0:T(128)} %collective-permute-done.7), channel_id=1, source_target_pairs={{0,2},{2,4},{4,6},{6,8},{8,10},{10,12},{12,14},{14,16},{16,18},{18... | collective-permute-start | bytes 20 | tf_op jit(solution)/shard_map/ppermute | solution.py:16
  45.6 94.4 %collective-permute-start.14 = (f32[256,256]{0,1:T(8,128)S(1)}, f32[256,256]{0,1:T(8,128)}, u32[]{:S(2)}, u32[]{:S(2)}) collective-permute-start(f32[256,256]{0,1:T(8,128)S(1)} %bitcast.285), channel_id=1, source_target_pairs={{2,0},{4,2},{6,4},{8,6},{10,8},{12,10},{14,12},{16,14},{18,16},{20... | collective-permute-start | bytes 786440 | tf_op jit(solution)/shard_map/ppermute | solution.py:16
  48.2 64.5 %collective-permute-start.13 = (f32[4,256]{1,0:T(4,128)}, f32[4,256]{1,0:T(4,128)}, u32[]{:S(2)}, u32[]{:S(2)}) collective-permute-start(f32[4,256]{1,0:T(4,128)} %broadcast_select_fusion.2), channel_id=1, source_target_pairs={{2,0},{4,2},{6,4},{8,6},{10,8},{12,10},{14,12},{16,14},{18,16},{20... | collective-permute-start | bytes 12296 | tf_op jit(solution)/shard_map/ppermute | solution.py:16
  51.1 9.8 %copy-start.22 = (f32[4,256]{1,0:T(4,128)}, f32[4,256]{1,0:T(4,128)S(1)}, u32[]{:S(2)}) copy-start(f32[4,256]{1,0:T(4,128)S(1)} %get-tuple-element.7) | copy-start | bytes 12292
  51.1 63.8 %collective-permute-start.12 = (f32[4,256]{1,0:T(4,128)}, f32[4,256]{1,0:T(4,128)}, u32[]{:S(2)}, u32[]{:S(2)}) collective-permute-start(f32[4,256]{1,0:T(4,128)} %get-tuple-element.6), channel_id=1, source_target_pairs={{2,0},{4,2},{6,4},{8,6},{10,8},{12,10},{14,12},{16,14},{18,16},{20... | collective-permute-start | bytes 12296 | tf_op jit(solution)/shard_map/ppermute | solution.py:16
  53.1 8.5 %collective-permute-start.3 = (bf16[256,256]{0,1:T(8,128)(2,1)S(1)}, bf16[256,256]{0,1:T(8,128)(2,1)S(1)}, u32[]{:S(2)}, u32[]{:S(2)}) collective-permute-start(bf16[256,256]{0,1:T(8,128)(2,1)S(1)} %collective-permute-done), channel_id=1, source_target_pairs={{0,2},{2,4},{4,6},{6,8},{8,10},{10,12},{12,14},{14,16},{16,18},{18... | collective-permute-start | bytes 393224 | tf_op jit(solution)/shard_map/ppermute | solution.py:16
  55.6 10.7 %collective-permute-start.5 = (bf16[256,256]{1,0:T(8,128)(2,1)S(1)}, bf16[256,256]{1,0:T(8,128)(2,1)}, u32[]{:S(2)}, u32[]{:S(2)}) collective-permute-start(bf16[256,256]{1,0:T(8,128)(2,1)S(1)} %collective-permute-done.2), channel_id=1, source_target_pairs={{0,2},{2,4},{4,6},{6,8},{8,10},{10,12},{12,14},{14,16},{16,18},{18... | collective-permute-start | bytes 393224 | tf_op jit(solution)/shard_map/ppermute | solution.py:16
  61.5 9.5 %collective-permute-start.29 = (bf16[256,256]{1,0:T(8,128)(2,1)}, bf16[256,256]{1,0:T(8,128)(2,1)}, u32[]{:S(2)}, u32[]{:S(2)}) collective-permute-start(bf16[256,256]{1,0:T(8,128)(2,1)} %collective-permute-done.26), channel_id=1, source_target_pairs={{0,2},{2,4},{4,6},{6,8},{8,10},{10,12},{12,14},{14,16},{16,18},{18... | collective-permute-start | bytes 393224 | tf_op jit(solution)/shard_map/ppermute | solution.py:16
  66.3 51.3 %collective-permute-start.16 = (f32[4,256]{1,0:T(4,128)}, f32[4,256]{1,0:T(4,128)}, u32[]{:S(2)}, u32[]{:S(2)}) collective-permute-start(f32[4,256]{1,0:T(4,128)} %broadcast_select_fusion.1), channel_id=1, source_target_pairs={{4,0},{6,2},{8,4},{10,6},{12,8},{14,10},{16,12},{18,14},{20,16},{2... | collective-permute-start | bytes 12296 | tf_op jit(solution)/shard_map/ppermute | solution.py:16
  71.1 7.3 %collective-permute-start.6 = (bf16[256,256]{0,1:T(8,128)(2,1)S(1)}, bf16[256,256]{0,1:T(8,128)(2,1)}, u32[]{:S(2)}, u32[]{:S(2)}) collective-permute-start(bf16[256,256]{0,1:T(8,128)(2,1)S(1)} %collective-permute-done.3), channel_id=1, source_target_pairs={{0,2},{2,4},{4,6},{6,8},{8,10},{10,12},{12,14},{14,16},{16,18},{18... | collective-permute-start | bytes 393224 | tf_op jit(solution)/shard_map/ppermute | solution.py:16
  78.3 9.5 %collective-permute-start.8 = (bf16[256,256]{1,0:T(8,128)(2,1)}, bf16[256,256]{1,0:T(8,128)(2,1)S(1)}, u32[]{:S(2)}, u32[]{:S(2)}) collective-permute-start(bf16[256,256]{1,0:T(8,128)(2,1)} %collective-permute-done.5), channel_id=1, source_target_pairs={{0,2},{2,4},{4,6},{6,8},{8,10},{10,12},{12,14},{14,16},{16,18},{18... | collective-permute-start | bytes 393224 | tf_op jit(solution)/shard_map/ppermute | solution.py:16
  88.5 7.5 %collective-permute-start.32 = (bf16[256,256]{1,0:T(8,128)(2,1)}, bf16[256,256]{1,0:T(8,128)(2,1)}, u32[]{:S(2)}, u32[]{:S(2)}) collective-permute-start(bf16[256,256]{1,0:T(8,128)(2,1)} %collective-permute-done.29), channel_id=1, source_target_pairs={{0,2},{2,4},{4,6},{6,8},{8,10},{10,12},{12,14},{14,16},{16,18},{18... | collective-permute-start | bytes 393224 | tf_op jit(solution)/shard_map/ppermute | solution.py:16
  96.0 7.5 %collective-permute-start.9 = (bf16[256,256]{0,1:T(8,128)(2,1)}, bf16[256,256]{0,1:T(8,128)(2,1)}, u32[]{:S(2)}, u32[]{:S(2)}) collective-permute-start(bf16[256,256]{0,1:T(8,128)(2,1)} %collective-permute-done.6), channel_id=1, source_target_pairs={{0,2},{2,4},{4,6},{6,8},{8,10},{10,12},{12,14},{14,16},{16,18},{18... | collective-permute-start | bytes 393224 | tf_op jit(solution)/shard_map/ppermute | solution.py:16
  99.6 3.9 %copy-start.30 = (f32[4,256]{1,0:T(4,128)S(1)}, f32[4,256]{1,0:T(4,128)}, u32[]{:S(2)}) copy-start(f32[4,256]{1,0:T(4,128)} %get-tuple-element.8) | copy-start | bytes 12292
  103.5 16.6 %collective-permute-start.15 = (f32[4,256]{1,0:T(4,128)S(1)}, f32[4,256]{1,0:T(4,128)S(1)}, u32[]{:S(2)}, u32[]{:S(2)}) collective-permute-start(f32[4,256]{1,0:T(4,128)S(1)} %copy-done.30), channel_id=1, source_target_pairs={{4,0},{6,2},{8,4},{10,6},{12,8},{14,10},{16,12},{18,14},{20,16},{2... | collective-permute-start | bytes 12296 | tf_op jit(solution)/shard_map/ppermute | solution.py:16
  105.4 3.9 %copy-start.5 = (f32[4,256,256]{1,2,0:T(8,128)S(1)}, f32[4,256,256]{1,2,0:T(8,128)}, u32[]{:S(2)}) copy-start(f32[4,256,256]{1,2,0:T(8,128)} %copy-done.4) | copy-start | bytes 3145732
  106.9 1.1 copy-start.25
  106.9 5.4 %copy-start.2 = (f32[4,256,256]{2,1,0:T(8,128)}, f32[4,256,256]{2,1,0:T(8,128)S(1)}, u32[]{:S(2)}) copy-start(f32[4,256,256]{2,1,0:T(8,128)S(1)} %get-tuple-element.56) | copy-start | bytes 3145732
  106.9 1.1 copy-start.23
  110.7 1.2 copy-start.1
  112.4 5.3 %copy-start.19 = (bf16[256,256]{1,0:T(8,128)(2,1)S(1)}, bf16[256,256]{1,0:T(8,128)(2,1)}, u32[]{:S(2)}) copy-start(bf16[256,256]{1,0:T(8,128)(2,1)} %copy-done.18) | copy-start | bytes 393220
  113.0 11.3 %collective-permute-start.19 = (f32[4,256]{1,0:T(4,128)S(1)}, f32[4,256]{1,0:T(4,128)S(1)}, u32[]{:S(2)}, u32[]{:S(2)}) collective-permute-start(f32[4,256]{1,0:T(4,128)S(1)} %copy-done.32), channel_id=1, source_target_pairs={{6,0},{8,2},{10,4},{12,6},{14,8},{16,10},{18,12},{20,14},{22,16},{... | collective-permute-start | bytes 12296 | tf_op jit(solution)/shard_map/ppermute | solution.py:16
  115.0 11.3 %collective-permute-start.18 = (f32[4,256]{1,0:T(4,128)S(1)}, f32[4,256]{1,0:T(4,128)S(1)}, u32[]{:S(2)}, u32[]{:S(2)}) collective-permute-start(f32[4,256]{1,0:T(4,128)S(1)} %get-tuple-element.10), channel_id=1, source_target_pairs={{6,0},{8,2},{10,4},{12,6},{14,8},{16,10},{18,12},{20,14},{22,16},{... | collective-permute-start | bytes 12296 | tf_op jit(solution)/shard_map/ppermute | solution.py:16
  117.7 12.9 %collective-permute-start.11 = (bf16[256,256]{1,0:T(8,128)(2,1)S(1)}, bf16[256,256]{1,0:T(8,128)(2,1)S(1)}, u32[]{:S(2)}, u32[]{:S(2)}) collective-permute-start(bf16[256,256]{1,0:T(8,128)(2,1)S(1)} %copy-done.19), channel_id=1, source_target_pairs={{0,2},{2,4},{4,6},{6,8},{8,10},{10,12},{12,14},{14,16},{16,18},{18... | collective-permute-start | bytes 393224 | tf_op jit(solution)/shard_map/ppermute | solution.py:16
  120.2 12.6 %collective-permute-start.35 = (bf16[256,256]{1,0:T(8,128)(2,1)}, bf16[256,256]{1,0:T(8,128)(2,1)S(1)}, u32[]{:S(2)}, u32[]{:S(2)}) collective-permute-start(bf16[256,256]{1,0:T(8,128)(2,1)} %collective-permute-done.32), channel_id=1, source_target_pairs={{0,2},{2,4},{4,6},{6,8},{8,10},{10,12},{12,14},{14,16},{16,18},{18... | collective-permute-start | bytes 393224 | tf_op jit(solution)/shard_map/ppermute | solution.py:16
  124.4 10.6 %collective-permute-start.22 = (f32[4,256]{1,0:T(4,128)S(1)}, f32[4,256]{1,0:T(4,128)S(1)}, u32[]{:S(2)}, u32[]{:S(2)}) collective-permute-start(f32[4,256]{1,0:T(4,128)S(1)} %broadcast_select_fusion.3), channel_id=1, source_target_pairs={{8,0},{10,2},{12,4},{14,6},{16,8},{18,10},{20,12},{22,14},{24,16},... | collective-permute-start | bytes 12296 | tf_op jit(solution)/shard_map/ppermute | solution.py:16
  126.3 10.6 %collective-permute-start.21 = (f32[4,256]{1,0:T(4,128)}, f32[4,256]{1,0:T(4,128)S(1)}, u32[]{:S(2)}, u32[]{:S(2)}) collective-permute-start(f32[4,256]{1,0:T(4,128)} %get-tuple-element.12), channel_id=1, source_target_pairs={{8,0},{10,2},{12,4},{14,6},{16,8},{18,10},{20,12},{22,14},{24,16},... | collective-permute-start | bytes 12296 | tf_op jit(solution)/shard_map/ppermute | solution.py:16
  128.9 1.6 copy-start.10
  130.6 2.2 %copy-start.11 = (f32[4,256,64]{1,2,0:T(8,128)S(1)}, f32[4,256,64]{1,2,0:T(8,128)}, u32[]{:S(2)}) copy-start(f32[4,256,64]{1,2,0:T(8,128)} %fusion.48) | copy-start | bytes 786436
  130.6 13.4 %collective-permute-start.17 = (f32[256,256]{0,1:T(8,128)S(1)}, f32[256,256]{0,1:T(8,128)}, u32[]{:S(2)}, u32[]{:S(2)}) collective-permute-start(f32[256,256]{0,1:T(8,128)S(1)} %bitcast.286), channel_id=1, source_target_pairs={{4,0},{6,2},{8,4},{10,6},{12,8},{14,10},{16,12},{18,14},{20,16},{2... | collective-permute-start | bytes 786440 | tf_op jit(solution)/shard_map/ppermute | solution.py:16
  132.8 6.2 %copy-start.14 = (bf16[256,256]{0,1:T(8,128)(2,1)S(1)}, bf16[256,256]{0,1:T(8,128)(2,1)}, u32[]{:S(2)}) copy-start(bf16[256,256]{0,1:T(8,128)(2,1)} %copy.59) | copy-start | bytes 393220
  132.8 13.1 %collective-permute-start.20 = (f32[256,256]{0,1:T(8,128)S(1)}, f32[256,256]{0,1:T(8,128)}, u32[]{:S(2)}, u32[]{:S(2)}) collective-permute-start(f32[256,256]{0,1:T(8,128)S(1)} %bitcast.287), channel_id=1, source_target_pairs={{6,0},{8,2},{10,4},{12,6},{14,8},{16,10},{18,12},{20,14},{22,16},{... | collective-permute-start | bytes 786440 | tf_op jit(solution)/shard_map/ppermute | solution.py:16
  135.0 18.7 %collective-permute-start.23 = (f32[256,256]{0,1:T(8,128)S(1)}, f32[256,256]{0,1:T(8,128)S(1)}, u32[]{:S(2)}, u32[]{:S(2)}) collective-permute-start(f32[256,256]{0,1:T(8,128)S(1)} %bitcast.288), channel_id=1, source_target_pairs={{8,0},{10,2},{12,4},{14,6},{16,8},{18,10},{20,12},{22,14},{24,16},... | collective-permute-start | bytes 786440 | tf_op jit(solution)/shard_map/ppermute | solution.py:16
  137.0 25.5 %collective-permute-start.25 = (f32[4,256]{1,0:T(4,128)S(1)}, f32[4,256]{1,0:T(4,128)S(1)}, u32[]{:S(2)}, u32[]{:S(2)}) collective-permute-start(f32[4,256]{1,0:T(4,128)S(1)} %get-tuple-element.48), channel_id=1, source_target_pairs={{0,2},{2,4},{4,6},{6,8},{8,10},{10,12},{12,14},{14,16},{16,18},{18... | collective-permute-start | bytes 12296 | tf_op jit(solution)/shard_map/ppermute | solution.py:16
  139.0 14.7 %copy-start.3 = (f32[4,256,256]{2,1,0:T(8,128)S(1)}, f32[4,256,256]{2,1,0:T(8,128)}, u32[]{:S(2)}) copy-start(f32[4,256,256]{2,1,0:T(8,128)} %copy-done.2) | copy-start | bytes 3145732
  140.0 25.7 %collective-permute-start.24 = (f32[4,256]{1,0:T(4,128)S(1)}, f32[4,256]{1,0:T(4,128)S(1)}, u32[]{:S(2)}, u32[]{:S(2)}) collective-permute-start(f32[4,256]{1,0:T(4,128)S(1)} %get-tuple-element.38), channel_id=1, source_target_pairs={{0,2},{2,4},{4,6},{6,8},{8,10},{10,12},{12,14},{14,16},{16,18},{18... | collective-permute-start | bytes 12296 | tf_op jit(solution)/shard_map/ppermute | solution.py:16
  144.0 45.6 %collective-permute-start.39 = (f32[256,256]{0,1:T(8,128)}, f32[256,256]{0,1:T(8,128)S(1)}, u32[]{:S(2)}, u32[]{:S(2)}) collective-permute-start(f32[256,256]{0,1:T(8,128)} %bitcast.68), channel_id=1, source_target_pairs={{8,0},{10,2},{12,4},{14,6},{16,8},{18,10},{20,12},{22,14},{24,16},... | collective-permute-start | bytes 786440 | tf_op jit(solution)/shard_map/ppermute | solution.py:16
  155.9 1.4 copy-start.9
  157.3 2.4 %copy-start.8 = (f32[4,256,256]{1,2,0:T(8,128)S(1)}, f32[4,256,256]{1,2,0:T(8,128)}, u32[]{:S(2)}) copy-start(f32[4,256,256]{1,2,0:T(8,128)} %copy.64) | copy-start | bytes 3145732
  157.7 4.5 %copy-start.7 = (f32[4,256,256]{1,2,0:T(8,128)S(1)}, f32[4,256,256]{1,2,0:T(8,128)}, u32[]{:S(2)}) copy-start(f32[4,256,256]{1,2,0:T(8,128)} %copy.61) | copy-start | bytes 3145732
  157.7 31.9 %collective-permute-start.38 = (f32[256,256]{0,1:T(8,128)S(1)}, f32[256,256]{0,1:T(8,128)S(1)}, u32[]{:S(2)}, u32[]{:S(2)}) collective-permute-start(f32[256,256]{0,1:T(8,128)S(1)} %bitcast.307), channel_id=1, source_target_pairs={{6,0},{8,2},{10,4},{12,6},{14,8},{16,10},{18,12},{20,14},{22,16},{... | collective-permute-start | bytes 786440 | tf_op jit(solution)/shard_map/ppermute | solution.py:16
  160.1 5.4 %copy-start.6 = (f32[4,256,256]{1,2,0:T(8,128)S(1)}, f32[4,256,256]{1,2,0:T(8,128)}, u32[]{:S(2)}) copy-start(f32[4,256,256]{1,2,0:T(8,128)} %copy-done.4) | copy-start | bytes 3145732
  160.1 29.5 %collective-permute-start.37 = (f32[256,256]{0,1:T(8,128)S(1)}, f32[256,256]{0,1:T(8,128)S(1)}, u32[]{:S(2)}, u32[]{:S(2)}) collective-permute-start(f32[256,256]{0,1:T(8,128)S(1)} %bitcast.308), channel_id=1, source_target_pairs={{4,0},{6,2},{8,4},{10,6},{12,8},{14,10},{16,12},{18,14},{20,16},{2... | collective-permute-start | bytes 786440 | tf_op jit(solution)/shard_map/ppermute | solution.py:16
  162.4 9.0 %copy-start.15 = (bf16[256,256]{0,1:T(8,128)(2,1)S(1)}, bf16[256,256]{0,1:T(8,128)(2,1)}, u32[]{:S(2)}) copy-start(bf16[256,256]{0,1:T(8,128)(2,1)} %copy.62) | copy-start | bytes 393220
  162.5 6.4 %collective-permute-start.28 = (f32[4,256]{1,0:T(4,128)S(1)}, f32[4,256]{1,0:T(4,128)S(1)}, u32[]{:S(2)}, u32[]{:S(2)}) collective-permute-start(f32[4,256]{1,0:T(4,128)S(1)} %collective-permute-done.25), channel_id=1, source_target_pairs={{0,2},{2,4},{4,6},{6,8},{8,10},{10,12},{12,14},{14,16},{16,18},{18... | collective-permute-start | bytes 12296 | tf_op jit(solution)/shard_map/ppermute | solution.py:16
  165.8 6.5 %collective-permute-start.27 = (f32[4,256]{1,0:T(4,128)S(1)}, f32[4,256]{1,0:T(4,128)S(1)}, u32[]{:S(2)}, u32[]{:S(2)}) collective-permute-start(f32[4,256]{1,0:T(4,128)S(1)} %collective-permute-done.24), channel_id=1, source_target_pairs={{0,2},{2,4},{4,6},{6,8},{8,10},{10,12},{12,14},{14,16},{16,18},{18... | collective-permute-start | bytes 12296 | tf_op jit(solution)/shard_map/ppermute | solution.py:16
  168.9 7.6 %collective-permute-start.31 = (f32[4,256]{1,0:T(4,128)S(1)}, f32[4,256]{1,0:T(4,128)S(1)}, u32[]{:S(2)}, u32[]{:S(2)}) collective-permute-start(f32[4,256]{1,0:T(4,128)S(1)} %collective-permute-done.28), channel_id=1, source_target_pairs={{0,2},{2,4},{4,6},{6,8},{8,10},{10,12},{12,14},{14,16},{16,18},{18... | collective-permute-start | bytes 12296 | tf_op jit(solution)/shard_map/ppermute | solution.py:16
  171.5 6.9 %copy-start.16 = (bf16[256,256]{0,1:T(8,128)(2,1)S(1)}, bf16[256,256]{0,1:T(8,128)(2,1)}, u32[]{:S(2)}) copy-start(bf16[256,256]{0,1:T(8,128)(2,1)} %copy.65) | copy-start | bytes 393220
  172.2 6.9 %collective-permute-start.30 = (f32[4,256]{1,0:T(4,128)S(1)}, f32[4,256]{1,0:T(4,128)S(1)}, u32[]{:S(2)}, u32[]{:S(2)}) collective-permute-start(f32[4,256]{1,0:T(4,128)S(1)} %collective-permute-done.27), channel_id=1, source_target_pairs={{0,2},{2,4},{4,6},{6,8},{8,10},{10,12},{12,14},{14,16},{16,18},{18... | collective-permute-start | bytes 12296 | tf_op jit(solution)/shard_map/ppermute | solution.py:16
  176.5 7.3 %collective-permute-start.34 = (f32[4,256]{1,0:T(4,128)S(1)}, f32[4,256]{1,0:T(4,128)S(1)}, u32[]{:S(2)}, u32[]{:S(2)}) collective-permute-start(f32[4,256]{1,0:T(4,128)S(1)} %collective-permute-done.31), channel_id=1, source_target_pairs={{0,2},{2,4},{4,6},{6,8},{8,10},{10,12},{12,14},{14,16},{16,18},{18... | collective-permute-start | bytes 12296 | tf_op jit(solution)/shard_map/ppermute | solution.py:16
  178.4 7.3 %copy-start.17 = (bf16[256,256]{0,1:T(8,128)(2,1)S(1)}, bf16[256,256]{0,1:T(8,128)(2,1)}, u32[]{:S(2)}) copy-start(bf16[256,256]{0,1:T(8,128)(2,1)} %copy.68) | copy-start | bytes 393220
  179.2 10.4 %collective-permute-start.36 = (f32[256,256]{0,1:T(8,128)S(1)}, f32[256,256]{0,1:T(8,128)S(1)}, u32[]{:S(2)}, u32[]{:S(2)}) collective-permute-start(f32[256,256]{0,1:T(8,128)S(1)} %bitcast.309), channel_id=1, source_target_pairs={{2,0},{4,2},{6,4},{8,6},{10,8},{12,10},{14,12},{16,14},{18,16},{20... | collective-permute-start | bytes 786440 | tf_op jit(solution)/shard_map/ppermute | solution.py:16
  183.7 5.8 %collective-permute-start.33 = (f32[4,256]{1,0:T(4,128)S(1)}, f32[4,256]{1,0:T(4,128)S(1)}, u32[]{:S(2)}, u32[]{:S(2)}) collective-permute-start(f32[4,256]{1,0:T(4,128)S(1)} %collective-permute-done.30), channel_id=1, source_target_pairs={{0,2},{2,4},{4,6},{6,8},{8,10},{10,12},{12,14},{14,16},{16,18},{18... | collective-permute-start | bytes 12296 | tf_op jit(solution)/shard_map/ppermute | solution.py:16
  (11 other events, 8.5 us)
Sparse Core Ops, SparseCore 0:
  157.5 21.4 reduce-scatter.1
where the time goes:
time: 203 us; the launch traced here: 201 us
  starting transfers between devices  98.1 us (48%)
  waiting for transfers between devices  29.2 us (14%)
  local copies, waits for them, and re-layouts  23 us (11%)
  matrix products  19.7 us (10%)
  between operations  18.2 us (9%)
  other arithmetic  12.9 us (6%)
    ppermute x40, starting transfers between devices, from_behind(): lax.ppermute(value, axis, [(source, source + steps) for source in range(i...  98.1 us
    ppermute x40, waiting for transfers between devices, from_behind(): lax.ppermute(value, axis, [(source, source + steps) for source in range(i...  29.2 us
    unnamed x72, local copies, waits for them, and re-layouts  8.94 us
    ppermute x8, local copies, waits for them, and re-layouts, from_behind(): lax.ppermute(value, axis, [(source, source + steps) for source in range(i...  7.28 us
    dot_general x4, local copies, waits for them, and re-layouts, tile_scores(): jnp.einsum('ihd,jhd->hij', row_keys, column_keys, preferred_element_type=...  6.75 us
    dot_general x5, matrix products, tile_scores(): jnp.einsum('ihd,jhd->hij', row_keys, column_keys, preferred_element_type=...  5.59 us
    reduce_sum x4, other arithmetic, column_part(): jnp.sum(exponent, axis=1)  4.87 us
  transfers between devices with their start and end apart: 41, of which 8 were waited for; matrix products, arithmetic and copies ran while one was open for 23% of the time, Pallas kernels for 0%

commit v1 on v0

v1 whole, which is shorter than its diff:
```python
import jax
import jax.numpy as jnp
from jax import lax
from jax.experimental import pallas as pl
from jax.experimental.pallas import tpu as pltpu
from jax.sharding import PartitionSpec as P

HD = 64
NEGATIVE = -1e30
REACH_ROWS = 16
F32 = jnp.float32
BF16 = jnp.bfloat16


def sibling(value):
    count = lax.axis_size("seq")
    return lax.ppermute(value, "seq", [(i, i ^ 1) for i in range(count)])


def chip_ring(value, step):
    chips = lax.axis_size("seq") // 2
    pairs = []
    for chip in range(chips):
        up, down = chip + step, chip - step
        pairs.append((2 * chip, 2 * up if up < chips else 2 * chip + 1))
        pairs.append((2 * chip + 1, 2 * down + 1 if down >= 0 else 2 * chip))
    return lax.ppermute(value, "seq", pairs)


def other_head(value):
    return lax.ppermute(value, "head", [(0, 1), (1, 0)])


def dot_nt(a, b):
    return lax.dot_general(a, b, (((1,), (1,)), ((), ())), preferred_element_type=F32)


def dot_nn(a, b):
    return lax.dot_general(a, b, (((1,), (0,)), ((), ())), preferred_element_type=F32)


def prepare_body(reach_ref, q_ref, s_ref, v_ref, k_ref, vt_ref):
    length, width = q_ref.shape
    low = lax.broadcasted_iota(jnp.int32, (length, 128), 1) < HD
    for g in range(width // 128):
        lanes = slice(128 * g, 128 * g + 128)
        q = q_ref[:, lanes].astype(F32)
        square = q * q
        sum_low = jnp.sum(jnp.where(low, square, 0.0), axis=1, keepdims=True)
        sum_high = jnp.sum(jnp.where(low, 0.0, square), axis=1, keepdims=True)
        inverse = jnp.where(low, lax.rsqrt(sum_low + 1e-6), lax.rsqrt(sum_high + 1e-6))
        scale = jnp.where(low, s_ref[:, 2 * g : 2 * g + 1], s_ref[:, 2 * g + 1 : 2 * g + 2])
        k_ref[0:length, lanes] = ((q * inverse) * scale).astype(BF16)
    reach = jnp.full((REACH_ROWS, width), reach_ref[0].astype(F32), F32)
    k_ref[length:, :] = reach.astype(BF16)
    vt_ref[...] = jnp.transpose(v_ref[...].astype(F32)).astype(BF16)


def head_keys(k_ref, length, h):
    g = h // 2
    lane = lax.broadcasted_iota(jnp.int32, (length, 128), 1)
    keep = (lane < HD) if h % 2 == 0 else (lane >= HD)
    rows = k_ref[0:length, 128 * g : 128 * g + 128]
    return jnp.where(keep, rows, jnp.zeros_like(rows))


def far_slots(flag_ref, length, sib, one, two, one_s, two_s):
    return [
        (sib, 0, 1, None),
        (one, 0, 2, flag_ref[1]),
        (one, 1, 1, flag_ref[1]),
        (two, 0, 4, flag_ref[2]),
        (two, 1, 3, flag_ref[2]),
        (one_s, 0, 3, flag_ref[3]),
        (one_s, 1, 2, flag_ref[3]),
        (two_s, 1, 4, flag_ref[4]),
    ]


def slot_allowed(flag_ref, slot, length):
    ref, block, distance, valid = slot
    start = block * (length + REACH_ROWS) + length
    far = jnp.max(ref[start : start + REACH_ROWS, 0:128].astype(F32))
    near = flag_ref[0].astype(F32)
    allowed = jnp.minimum(near, far) >= float(distance)
    if valid is not None:
        allowed = jnp.logical_and(allowed, valid > 0)
    return allowed


def diagonal(length):
    row = lax.broadcasted_iota(jnp.int32, (length, length), 0)
    return row == lax.broadcasted_iota(jnp.int32, (length, length), 1)


def stats_body(flag_ref, own, sib, one, two, one_s, two_s, st_ref, m_ref):
    length = own.shape[0] - REACH_ROWS
    heads = own.shape[1] // HD
    keys = [head_keys(own, length, h) for h in range(heads)]

    def tile(slot, ref, row, masked):
        for h in range(heads):
            g = h // 2
            scores = dot_nt(ref[row : row + length, 128 * g : 128 * g + 128], keys[h])
            if masked:
                scores = jnp.where(diagonal(length), NEGATIVE, scores)
            top = jnp.max(scores, axis=0, keepdims=True)
            total = jnp.sum(jnp.exp(scores - top), axis=0, keepdims=True)
            m_ref[2 * heads * slot + h : 2 * heads * slot + h + 1, :] = top
            m_ref[2 * heads * slot + heads + h : 2 * heads * slot + heads + h + 1, :] = total

    tile(0, own, 0, True)
    slots = far_slots(flag_ref, length, sib, one, two, one_s, two_s)
    for index, slot in enumerate(slots):
        at = index + 1
        m_ref[2 * heads * at : 2 * heads * at + heads, :] = jnp.full((heads, length), NEGATIVE, F32)
        m_ref[2 * heads * at + heads : 2 * heads * at + 2 * heads, :] = jnp.zeros((heads, length), F32)

        @pl.when(slot_allowed(flag_ref, slot, length))
        def _():
            tile(at, slot[0], slot[1] * (length + REACH_ROWS), False)

    tops = [m_ref[2 * heads * s : 2 * heads * s + heads, :] for s in range(len(slots) + 1)]
    top = tops[0]
    for other in tops[1:]:
        top = jnp.maximum(top, other)
    total = jnp.zeros((heads, length), F32)
    for s in range(len(slots) + 1):
        total = total + jnp.exp(tops[s] - top) * m_ref[2 * heads * s + heads : 2 * heads * s + 2 * heads, :]
    st_ref[0:heads, :] = top
    st_ref[heads : 2 * heads, :] = total


def attend_body(
    flag_ref, own, sib, one, two, one_s, two_s, v, vsib, vone, vtwo, vone_s, vtwo_s,
    st_ref, m_ref, keep_ref, send_ref, acc, rows_ref,
):
    length = own.shape[0] - REACH_ROWS
    heads = own.shape[1] // HD
    keys = [head_keys(own, length, h) for h in range(heads)]

    def tile(slot, ref, row, vref, vrow, masked):
        for h in range(heads):
            g = h // 2
            scores = dot_nt(ref[row : row + length, 128 * g : 128 * g + 128], keys[h])
            if masked:
                scores = jnp.where(diagonal(length), NEGATIVE, scores)
            top = m_ref[2 * heads * slot + h : 2 * heads * slot + h + 1, :]
            weights = jnp.exp(scores - top).astype(BF16)
            numer = dot_nn(vref[vrow + HD * h : vrow + HD * h + HD, :], weights)
            numer = numer * jnp.exp(top - st_ref[h : h + 1, :])
            if masked:
                acc[HD * h : HD * h + HD, :] = numer
            else:
                acc[HD * h : HD * h + HD, :] += numer

    tile(0, own, 0, v, 0, True)
    vrefs = [vsib, vone, vone, vtwo, vtwo, vone_s, vone_s, vtwo_s]
    slots = far_slots(flag_ref, length, sib, one, two, one_s, two_s)
    for index, slot in enumerate(slots):

        @pl.when(slot_allowed(flag_ref, slot, length))
        def _():
            row = slot[1] * (length + REACH_ROWS)
            tile(index + 1, slot[0], row, vrefs[index], slot[1] * heads * HD, False)

    for h in range(heads):
        part = slice(HD * h, HD * h + HD)
        acc[part, :] = acc[part, :] / st_ref[heads + h : heads + h + 1, :]
    rows_ref[...] = jnp.transpose(acc[...])
    half = length // 2
    mine = flag_ref[5]
    keep_ref[...] = rows_ref[pl.ds(pl.multiple_of(mine * half, half), half), :].astype(BF16)
    send_ref[...] = rows_ref[pl.ds(pl.multiple_of((1 - mine) * half, half), half), :].astype(BF16)


def grad_body(
    flag_ref, own, sib, one, two, one_s, two_s, g0, gsib, gone, gtwo, gone_s, gtwo_s,
    st, ssib, sone, stwo, sone_s, stwo_s, out_ref, acc,
):
    length = own.shape[0] - REACH_ROWS
    heads = own.shape[1] // HD
    keys = [head_keys(own, length, h) for h in range(heads)]
    low = lax.broadcasted_iota(jnp.int32, (length, 128), 1) < HD

    def tile(ref, row, gref, grow, sref, srow, masked):
        for g in range(heads // 2):
            lanes = slice(128 * g, 128 * g + 128)
            grads = gref[grow : grow + length, lanes]
            parts = []
            for h in (2 * g, 2 * g + 1):
                scores = dot_nt(keys[h], ref[row : row + length, lanes])
                if masked:
                    scores = jnp.where(diagonal(length), NEGATIVE, scores)
                top = sref[srow + h : srow + h + 1, :]
                inverse = 1.0 / sref[srow + heads + h : srow + heads + h + 1, :]
                weights = (jnp.exp(scores - top) * inverse).astype(BF16)
                zero = jnp.zeros_like(grads)
                some = jnp.where(low, grads, zero) if h % 2 == 0 else jnp.where(low, zero, grads)
                parts.append(dot_nn(weights, some))
            if masked:
                acc[:, lanes] = parts[0] + parts[1]
            else:
                acc[:, lanes] += parts[0] + parts[1]

    tile(own, 0, g0, 0, st, 0, True)
    grefs = [gsib, gone, gone, gtwo, gtwo, gone_s, gone_s, gtwo_s]
    srefs = [ssib, sone, sone, stwo, stwo, sone_s, sone_s, stwo_s]
    slots = far_slots(flag_ref, length, sib, one, two, one_s, two_s)
    for index, slot in enumerate(slots):

        @pl.when(slot_allowed(flag_ref, slot, length))
        def _():
            block = slot[1]
            row = block * (length + REACH_ROWS)
            tile(slot[0], row, grefs[index], block * length, srefs[index], 2 * heads * block, False)

    out_ref[...] = acc[...].astype(BF16)


def project_body(keep_ref, got_ref, near_ref, far_ref, out_ref):
    total = dot_nn(keep_ref[...], near_ref[...]) + dot_nn(got_ref[...], far_ref[...])
    out_ref[...] = total.astype(BF16)


VMEM = pl.BlockSpec(memory_space=pltpu.VMEM)
SMEM = pl.BlockSpec(memory_space=pltpu.SMEM)


def call(body, name, args, outs, smem=1, scratch=()):
    specs = [SMEM] * smem + [VMEM] * (len(args) - smem)
    return pl.pallas_call(
        body,
        name=name,
        in_specs=specs,
        out_specs=[VMEM] * len(outs),
        out_shape=[jax.ShapeDtypeStruct(shape, dtype) for shape, dtype in outs],
        scratch_shapes=[pltpu.VMEM(shape, dtype) for shape, dtype in scratch],
    )(*args)


def gathered(own):
    sib = sibling(own)
    both = jnp.concatenate([own, sib], axis=0)
    one, two = chip_ring(both, 1), chip_ring(both, 2)
    return [own, sib, one, two, sibling(one), sibling(two)]


def shards(queries, values, scales, block_reach, out_weight, out_grad):
    length, width = queries.shape
    heads = scales.shape[1]
    chips = lax.axis_size("seq") // 2
    place = lax.axis_index("seq")
    chip, toward = place // 2, 2 * (place % 2) - 1
    inside = lambda c: jnp.logical_and(c >= 0, c < chips).astype(jnp.int32)
    flags = jnp.stack(
        [
            block_reach[0],
            inside(chip + toward),
            inside(chip + 2 * toward),
            inside(chip - toward),
            inside(chip - 2 * toward),
            lax.axis_index("head"),
        ]
    ).astype(jnp.int32)
    keys, turned = call(
        prepare_body,
        "prepare",
        [block_reach, queries, scales, values],
        [((length + REACH_ROWS, width), BF16), ((width, length), BF16)],
    )
    key_set = gathered(keys)
    value_set = gathered(turned)
    grad_set = gathered(out_grad)
    far_weight = other_head(out_weight)
    stats, tops = call(
        stats_body,
        "stats",
        [flags, *key_set],
        [((2 * heads, length), F32), ((9 * 2 * heads, length), F32)],
    )
    stat_set = gathered(stats)
    keep, send = call(
        attend_body,
        "attend",
        [flags, *key_set, *value_set, stats, tops],
        [((length // 2, width), BF16), ((length // 2, width), BF16)],
        scratch=[((width, length), F32), ((length, width), F32)],
    )
    got = other_head(send)
    (value_grad,) = call(
        grad_body,
        "value_grad",
        [flags, *key_set, *grad_set, *stat_set],
        [((length, width), BF16)],
        scratch=[((length, width), F32)],
    )
    (mixed,) = call(
        project_body,
        "project",
        [keep, got, out_weight, far_weight],
        [((length // 2, out_weight.shape[1]), BF16)],
        smem=0,
    )
    return (mixed, value_grad)


def solution(mesh):
    return jax.shard_map(
        shards,
        mesh=mesh,
        in_specs=(
            P("seq", "head"),
            P("seq", "head"),
            P("seq", "head"),
            P("seq"),
            P("head", None),
            P("seq", "head"),
        ),
        out_specs=(P(("seq", "head"), None), P("seq", "head")),
        check_vma=False,
    )
```

time: 203 us -> 62.7 us (0.31)
  starting transfers between devices: 98.1 us -> 16.2 us
  Pallas kernels: 0 us -> 24.7 us
  matrix products: 19.7 us -> 0 us
  between operations: 18.2 us -> 1.44 us
  local copies, waits for them, and re-layouts: 23 us -> 6.46 us
  waiting for transfers between devices: 29.2 us -> 13.7 us
  other arithmetic: 12.9 us -> 0 us
    ppermute x40 -> x22, starting transfers between devices: 98.1 us -> 16.2 us  [the longest x8 9.32 us: chip_ring(): return lax.ppermute(value, 'seq', pairs)]
    pallas_call x0 -> x5, Pallas kernels: none -> 24.7 us  [call(): pl.pallas_call(body, name=name, in_specs=specs, out_specs=[VMEM] * len(ou...]
    dot_general x24 -> x0, matrix products: 19.7 us -> none  [the longest x5 5.59 us: tile_scores(): jnp.einsum('ihd,jhd->hij', row_keys, column_keys, preferred_element_type=...]
    ppermute x40 -> x22, waiting for transfers between devices: 29.2 us -> 13.7 us  [the longest x8 12.3 us: chip_ring(): return lax.ppermute(value, 'seq', pairs)]
    ppermute x8 -> x0, local copies, waits for them, and re-layouts: 7.28 us -> none  [from_behind(): lax.ppermute(value, axis, [(source, source + steps) for source in range(i...]
    dot_general x4 -> x0, local copies, waits for them, and re-layouts: 6.75 us -> none  [tile_scores(): jnp.einsum('ihd,jhd->hij', row_keys, column_keys, preferred_element_type=...]
    reduce_sum x6 -> x0, other arithmetic: 5.08 us -> none  [the longest x4 4.87 us: column_part(): jnp.sum(exponent, axis=1)]
    unnamed x72 -> x47, local copies, waits for them, and re-layouts: 8.94 us -> 5.8 us
  transfers between devices with their start and end apart: 41 -> 22, of which waited for: 8 -> 8; matrix products, arithmetic and copies ran while one was open for 23% -> 4% of each run, Pallas kernels for 0% -> 32%
where the time goes in v1:
time: 62.7 us; the launch traced here: 62.5 us
  Pallas kernels  24.7 us (39%)
  starting transfers between devices  16.2 us (26%)
  waiting for transfers between devices  13.7 us (22%)
  local copies, waits for them, and re-layouts  6.46 us (10%)
  between operations  1.44 us (2%)
    pallas_call x5, Pallas kernels, call(): pl.pallas_call(body, name=name, in_specs=specs, out_specs=[VMEM] * len(ou...  24.7 us
    ppermute x8, waiting for transfers between devices, chip_ring(): return lax.ppermute(value, 'seq', pairs)  12.3 us
    ppermute x8, starting transfers between devices, chip_ring(): return lax.ppermute(value, 'seq', pairs)  9.32 us
    unnamed x47, local copies, waits for them, and re-layouts  5.8 us
    ppermute x12, starting transfers between devices, sibling(): return lax.ppermute(value, 'seq', [(i, i ^ 1) for i in range(count)])  3.77 us
    ppermute x2, starting transfers between devices, other_head(): return lax.ppermute(value, 'head', [(0, 1), (1, 0)])  3.11 us
    ppermute x12, waiting for transfers between devices, sibling(): return lax.ppermute(value, 'seq', [(i, i ^ 1) for i in range(count)])  1.4 us
  transfers between devices with their start and end apart: 22, of which 8 were waited for; matrix products, arithmetic and copies ran while one was open for 4% of the time, Pallas kernels for 32%

profile of v1, /device:TPU:8, one launch (start us, length us, event | category | flops | bytes accessed | tf_op | source)
XLA Modules:
  0.0 62.5 jit_solution(16022514723434960267)
XLA Ops:
  1.3 1.5 %copy.8.s_ref = f32[256,4]{1,0:T(8,128)} copy(f32[256,4]{0,1:T(4,128)} %param.8) | data formatting | bytes 8192 | tf_op args[2]
  2.8 2.2 %prepare.1 = (bf16[272,256]{1,0:T(8,128)(2,1)}, bf16[256,256]{1,0:T(8,128)(2,1)}) custom-call(s32[1]{0:T(128)S(6)} %copy.13.reach_ref, bf16[256,256]{1,0:T(8,128)(2,1)} %q_ref.1, f32[256,4]{1,0:T(8,128)} %copy.8.s_ref, bf16[256,256]{1,0:T(8,128)(2,1)} %v_ref.1), custom_call_target="tpu_custom_call" | custom-call | tf_op jit(solution)/shard_map/prepare/pallas_call | solution.py:232
  5.0 0.0 collective-permute-start
  5.0 0.5 collective-permute-start.5
  5.5 0.0 copy-done.5
  5.5 0.1 collective-permute-start.12
  5.6 0.9 %constant_dynamic-update-slice_fusion.1 = bf16[544,256]{1,0:T(8,128)(2,1)S(1)} fusion(bf16[272,256]{1,0:T(8,128)(2,1)} %get-tuple-element.8.own), kind=kLoop, calls=%fused_computation.1 | loop fusion | bytes 278528
  6.5 0.0 copy-start.9
  6.5 0.2 collective-permute-done.5.vsib
  6.7 1.6 %collective-permute-start.6 = (bf16[512,256]{1,0:T(8,128)(2,1)S(1)}, bf16[512,256]{1,0:T(8,128)(2,1)S(1)}, u32[]{:S(2)}, u32[]{:S(2)}) collective-permute-start(bf16[512,256]{1,0:T(8,128)(2,1)S(1)} %constant_dynamic-update-slice_fusion.2), channel_id=1, source_target_pairs={{0,4},{2,0},{4,8},{6,2},{8,12},{10,6},{12,16},{14,10},{16,20},{18,... | collective-permute-start | bytes 786440 | tf_op jit(solution)/shard_map/ppermute | solution.py:27
  8.3 1.6 %collective-permute-start.7 = (bf16[512,256]{1,0:T(8,128)(2,1)S(1)}, bf16[512,256]{1,0:T(8,128)(2,1)S(1)}, u32[]{:S(2)}, u32[]{:S(2)}) collective-permute-start(bf16[512,256]{1,0:T(8,128)(2,1)S(1)} %constant_dynamic-update-slice_fusion.2), channel_id=1, source_target_pairs={{0,8},{2,0},{4,12},{6,4},{8,16},{10,2},{12,20},{14,6},{16,24},{18,... | collective-permute-start | bytes 786440 | tf_op jit(solution)/shard_map/ppermute | solution.py:27
  9.9 0.0 collective-permute-done.sib
  9.9 1.6 %collective-permute-start.1 = (bf16[544,256]{1,0:T(8,128)(2,1)S(1)}, bf16[544,256]{1,0:T(8,128)(2,1)S(1)}, u32[]{:S(2)}, u32[]{:S(2)}) collective-permute-start(bf16[544,256]{1,0:T(8,128)(2,1)S(1)} %constant_dynamic-update-slice_fusion), channel_id=1, source_target_pairs={{0,4},{2,0},{4,8},{6,2},{8,12},{10,6},{12,16},{14,10},{16,20},{18,... | collective-permute-start | bytes 835592 | tf_op jit(solution)/shard_map/ppermute | solution.py:27
  11.5 0.4 collective-permute-start.2
  11.9 0.0 collective-permute-done.12.gsib
  11.9 0.6 %copy-done.6 = bf16[256,256]{1,0:T(8,128)(2,1)} copy-done((bf16[256,256]{1,0:T(8,128)(2,1)}, bf16[256,256]{1,0:T(8,128)(2,1)S(1)}, u32[]{:S(2)}) %copy-start.6) | copy-done | bytes 131096
  12.5 1.2 %collective-permute-start.13 = (bf16[512,256]{1,0:T(8,128)(2,1)S(1)}, bf16[512,256]{1,0:T(8,128)(2,1)S(1)}, u32[]{:S(2)}, u32[]{:S(2)}) collective-permute-start(bf16[512,256]{1,0:T(8,128)(2,1)S(1)} %constant_dynamic-update-slice_fusion.4), channel_id=1, source_target_pairs={{0,4},{2,0},{4,8},{6,2},{8,12},{10,6},{12,16},{14,10},{16,20},{18,... | collective-permute-start | bytes 786440 | tf_op jit(solution)/shard_map/ppermute | solution.py:27
  13.7 1.3 %collective-permute-done.6.vone = bf16[512,256]{1,0:T(8,128)(2,1)S(1)} collective-permute-done((bf16[512,256]{1,0:T(8,128)(2,1)S(1)}, bf16[512,256]{1,0:T(8,128)(2,1)S(1)}, u32[]{:S(2)}, u32[]{:S(2)}) %collective-permute-start.6) | collective-permute-done | bytes 262176 | tf_op jit(solution)/shard_map/ppermute | solution.py:27
  15.0 1.6 %collective-permute-start.14 = (bf16[512,256]{1,0:T(8,128)(2,1)S(1)}, bf16[512,256]{1,0:T(8,128)(2,1)S(1)}, u32[]{:S(2)}, u32[]{:S(2)}) collective-permute-start(bf16[512,256]{1,0:T(8,128)(2,1)S(1)} %constant_dynamic-update-slice_fusion.4), channel_id=1, source_target_pairs={{0,8},{2,0},{4,12},{6,4},{8,16},{10,2},{12,20},{14,6},{16,24},{18,... | collective-permute-start | bytes 786440 | tf_op jit(solution)/shard_map/ppermute | solution.py:27
  16.6 4.4 %collective-permute-done.1.one = bf16[544,256]{1,0:T(8,128)(2,1)S(1)} collective-permute-done((bf16[544,256]{1,0:T(8,128)(2,1)S(1)}, bf16[544,256]{1,0:T(8,128)(2,1)S(1)}, u32[]{:S(2)}, u32[]{:S(2)}) %collective-permute-start.1) | collective-permute-done | bytes 278560 | tf_op jit(solution)/shard_map/ppermute | solution.py:27
  21.0 0.4 collective-permute-start.3
  21.4 0.0 collective-permute-done.2.two
  21.4 0.7 %collective-permute-start.4 = (bf16[544,256]{1,0:T(8,128)(2,1)S(1)}, bf16[544,256]{1,0:T(8,128)(2,1)S(1)}, u32[]{:S(2)}, u32[]{:S(2)}) collective-permute-start(bf16[544,256]{1,0:T(8,128)(2,1)S(1)} %collective-permute-done.2.two), channel_id=1, source_target_pairs={{0,2},{2,0},{4,6},{6,4},{8,10},{10,8},{12,14},{14,12},{16,18},{18,... | collective-permute-start | bytes 835592 | tf_op jit(solution)/shard_map/ppermute | solution.py:17
  22.2 0.0 collective-permute-done.7.vtwo
  22.2 0.0 copy-done.9
  22.2 1.6 %collective-permute-start.11 = (bf16[256,1024]{1,0:T(8,128)(2,1)S(1)}, bf16[256,1024]{1,0:T(8,128)(2,1)S(1)}, u32[]{:S(2)}, u32[]{:S(2)}) collective-permute-start(bf16[256,1024]{1,0:T(8,128)(2,1)S(1)} %copy-done.9), channel_id=1, source_target_pairs={{0,1},{1,0},{2,3},{3,2},{4,5},{5,4},{6,7},{7,6},{8,9},{9,8},{10,11... | collective-permute-start | bytes 1572872 | tf_op jit(solution)/shard_map/ppermute | solution.py:31
  23.7 2.9 %collective-permute-done.13.gone = bf16[512,256]{1,0:T(8,128)(2,1)S(1)} collective-permute-done((bf16[512,256]{1,0:T(8,128)(2,1)S(1)}, bf16[512,256]{1,0:T(8,128)(2,1)S(1)}, u32[]{:S(2)}, u32[]{:S(2)}) %collective-permute-start.13) | collective-permute-done | bytes 262176 | tf_op jit(solution)/shard_map/ppermute | solution.py:27
  26.6 0.4 collective-permute-start.8
  27.0 0.0 collective-permute-done.14.gtwo
  27.0 1.1 %collective-permute-start.9 = (bf16[512,256]{1,0:T(8,128)(2,1)S(1)}, bf16[512,256]{1,0:T(8,128)(2,1)}, u32[]{:S(2)}, u32[]{:S(2)}) collective-permute-start(bf16[512,256]{1,0:T(8,128)(2,1)S(1)} %collective-permute-done.7.vtwo), channel_id=1, source_target_pairs={{0,2},{2,0},{4,6},{6,4},{8,10},{10,8},{12,14},{14,12},{16,18},{18,... | collective-permute-start | bytes 786440 | tf_op jit(solution)/shard_map/ppermute | solution.py:17
  28.1 0.0 collective-permute-done.3.one_s
  28.1 0.1 collective-permute-start.15
  28.2 0.0 collective-permute-done.4.two_s
  28.2 0.4 collective-permute-start.16
  28.6 0.6 %stack.39.flag_ref = s32[6]{0:T(128)} concatenate(s32[1]{0:T(128)S(6)} %copy.13.reach_ref, s32[1]{0:T(128)} %bitcast, s32[1]{0:T(128)} %bitcast.1, s32[1]{0:T(128)} %bitcast.2, s32[1]{0:T(128)} %bitcast.3, s32[1]{0:T(128)} %bitcast.4), dimensions={0} | concatenate | bytes 48 | tf_op jit(solution)/shard_map/stack | solution.py:256
  29.3 0.0 copy-done
  29.3 0.0 copy-done.2
  29.3 5.1 %stats.1 = (f32[8,256]{1,0:T(8,128)}, f32[72,256]{1,0:T(8,128)}) custom-call(s32[6]{0:T(128)} %stack.39.flag_ref, bf16[272,256]{1,0:T(8,128)(2,1)} %get-tuple-element.8.own, bf16[272,256]{1,0:T(8,128)(2,1)} %copy-done.4, bf16[544,256]{1,0:T(8,128)(2,1)} %copy-done, bf16[544,256]{1,0:T(8,128)(2,1)} %copy-done.1, bf16[544,256]{1,0:T(8,128)(2,1)} %copy-done.2, ...), custom_call_target="tpu_custom_call" | custom-call | tf_op jit(solution)/shard_map/stats/pallas_call | solution.py:232
  34.4 0.0 collective-permute-done.8.vone_s
  34.4 0.0 collective-permute-start.17
  34.4 0.7 %constant_dynamic-update-slice_fusion.7 = f32[16,256]{1,0:T(8,128)S(1)} fusion(f32[8,256]{1,0:T(8,128)} %get-tuple-element.10.st_ref.st), kind=kLoop, calls=%fused_computation.7 | loop fusion | bytes 16384
  35.1 0.0 collective-permute-done.9.vtwo_s
  35.1 8.6 %attend.1 = (bf16[128,256]{1,0:T(8,128)(2,1)}, bf16[128,256]{1,0:T(8,128)(2,1)}) custom-call(s32[6]{0:T(128)} %stack.39.flag_ref, bf16[272,256]{1,0:T(8,128)(2,1)} %get-tuple-element.8.own, bf16[272,256]{1,0:T(8,128)(2,1)} %copy-done.4, bf16[544,256]{1,0:T(8,128)(2,1)} %copy-done, bf16[544,256]{1,0:T(8,128)(2,1)} %copy-done.1, bf16[544,256]{1,0:T(8,128)(2,1)} %copy-done.2, ...), custom_call_target="tpu_custom_call" | custom-call | tf_op jit(solution)/shard_map/attend/pallas_call | solution.py:232
  43.7 1.6 %collective-permute-start.10 = (bf16[128,256]{1,0:T(8,128)(2,1)}, bf16[128,256]{1,0:T(8,128)(2,1)S(1)}, u32[]{:S(2)}, u32[]{:S(2)}) collective-permute-start(bf16[128,256]{1,0:T(8,128)(2,1)} %get-tuple-element.13), channel_id=1, source_target_pairs={{0,1},{1,0},{2,3},{3,2},{4,5},{5,4},{6,7},{7,6},{8,9},{9,8},{10,11... | collective-permute-start | bytes 196616 | tf_op jit(solution)/shard_map/ppermute | solution.py:31
  45.3 0.0 collective-permute-done.17.ssib
  45.3 0.6 copy-done.16
  45.9 1.5 %collective-permute-start.18 = (f32[16,256]{1,0:T(8,128)S(1)}, f32[16,256]{1,0:T(8,128)S(1)}, u32[]{:S(2)}, u32[]{:S(2)}) collective-permute-start(f32[16,256]{1,0:T(8,128)S(1)} %constant_dynamic-update-slice_fusion.6), channel_id=1, source_target_pairs={{0,4},{2,0},{4,8},{6,2},{8,12},{10,6},{12,16},{14,10},{16,20},{18,... | collective-permute-start | bytes 49160 | tf_op jit(solution)/shard_map/ppermute | solution.py:27
  47.4 0.0 collective-permute-done.15.gone_s
  47.4 0.0 collective-permute-start.19
  47.4 3.1 %collective-permute-done.18.sone = f32[16,256]{1,0:T(8,128)S(1)} collective-permute-done((f32[16,256]{1,0:T(8,128)S(1)}, f32[16,256]{1,0:T(8,128)S(1)}, u32[]{:S(2)}, u32[]{:S(2)}) %collective-permute-start.18) | collective-permute-done | bytes 16416 | tf_op jit(solution)/shard_map/ppermute | solution.py:27
  50.5 0.0 collective-permute-start.20
  50.5 0.6 collective-permute-done.19.stwo
  51.1 0.0 collective-permute-start.21
  51.1 0.0 collective-permute-done.16.gtwo_s
  51.1 0.6 collective-permute-done.20.sone_s
  51.7 0.6 collective-permute-done.21.stwo_s
  52.3 0.0 copy-done.19
  52.3 0.6 copy-done.20
  52.9 6.5 %value_grad.1 = bf16[256,256]{1,0:T(8,128)(2,1)} custom-call(s32[6]{0:T(128)} %stack.39.flag_ref, bf16[272,256]{1,0:T(8,128)(2,1)} %get-tuple-element.8.own, bf16[272,256]{1,0:T(8,128)(2,1)} %copy-done.4, bf16[544,256]{1,0:T(8,128)(2,1)} %copy-done, bf16[544,256]{1,0:T(8,128)(2,1)} %copy-done.1, bf16[544,256]{1,0:T(8,128)(2,1)} %copy-done.2, ...), custom_call_target="tpu_custom_call" | custom-call | tf_op jit(solution)/shard_map/value_grad/pallas_call | solution.py:232
  59.4 0.0 collective-permute-done.11.far_ref
  59.4 0.0 collective-permute-done.10.got_ref
  59.4 0.8 %copy-done.10 = bf16[256,1024]{1,0:T(8,128)(2,1)} copy-done((bf16[256,1024]{1,0:T(8,128)(2,1)}, bf16[256,1024]{1,0:T(8,128)(2,1)S(1)}, u32[]{:S(2)}) %copy-start.10) | copy-done | bytes 524312
  60.2 0.0 copy-done.15
  60.2 2.3 %project.1 = bf16[128,1024]{1,0:T(8,128)(2,1)} custom-call(bf16[128,256]{1,0:T(8,128)(2,1)} %get-tuple-element.12.keep_ref, bf16[128,256]{1,0:T(8,128)(2,1)} %copy-done.15, bf16[256,1024]{1,0:T(8,128)(2,1)} %near_ref.1, bf16[256,1024]{1,0:T(8,128)(2,1)} %copy-done.10), custom_call_target="tpu_custom_call" | custom-call | tf_op jit(solution)/shard_map/project/pallas_call | solution.py:232
  (37 shorter events, 0.1 us)
Async XLA Ops:
  2.8 2.7 %copy-start.5 = (bf16[256,256]{1,0:T(8,128)(2,1)S(1)}, bf16[256,256]{1,0:T(8,128)(2,1)}, u32[]{:S(2)}) copy-start(bf16[256,256]{1,0:T(8,128)(2,1)} %g0.1) | copy-start | bytes 393220
  5.0 4.9 %collective-permute-start = (bf16[272,256]{1,0:T(8,128)(2,1)}, bf16[272,256]{1,0:T(8,128)(2,1)S(1)}, u32[]{:S(2)}, u32[]{:S(2)}) collective-permute-start(bf16[272,256]{1,0:T(8,128)(2,1)} %get-tuple-element.8.own), channel_id=1, source_target_pairs={{0,2},{2,0},{4,6},{6,4},{8,10},{10,8},{12,14},{14,12},{16,18},{18,... | collective-permute-start | bytes 417800 | tf_op jit(solution)/shard_map/ppermute | solution.py:17
  5.0 1.5 %copy-start.7 = (bf16[256,256]{1,0:T(8,128)(2,1)S(1)}, bf16[256,256]{1,0:T(8,128)(2,1)}, u32[]{:S(2)}) copy-start(bf16[256,256]{1,0:T(8,128)(2,1)} %get-tuple-element.9.v) | copy-start | bytes 393220
  5.0 1.8 %collective-permute-start.5 = (bf16[256,256]{1,0:T(8,128)(2,1)}, bf16[256,256]{1,0:T(8,128)(2,1)S(1)}, u32[]{:S(2)}, u32[]{:S(2)}) collective-permute-start(bf16[256,256]{1,0:T(8,128)(2,1)} %get-tuple-element.9.v), channel_id=1, source_target_pairs={{0,2},{2,0},{4,6},{6,4},{8,10},{10,8},{12,14},{14,12},{16,18},{18,... | collective-permute-start | bytes 393224 | tf_op jit(solution)/shard_map/ppermute | solution.py:17
  5.5 6.4 %collective-permute-start.12 = (bf16[256,256]{1,0:T(8,128)(2,1)S(1)}, bf16[256,256]{1,0:T(8,128)(2,1)S(1)}, u32[]{:S(2)}, u32[]{:S(2)}) collective-permute-start(bf16[256,256]{1,0:T(8,128)(2,1)S(1)} %copy-done.5), channel_id=1, source_target_pairs={{0,2},{2,0},{4,6},{6,4},{8,10},{10,8},{12,14},{14,12},{16,18},{18,... | collective-permute-start | bytes 393224 | tf_op jit(solution)/shard_map/ppermute | solution.py:17
  6.5 15.7 %copy-start.9 = (bf16[256,1024]{1,0:T(8,128)(2,1)S(1)}, bf16[256,1024]{1,0:T(8,128)(2,1)}, u32[]{:S(2)}) copy-start(bf16[256,1024]{1,0:T(8,128)(2,1)} %near_ref.1) | copy-start | bytes 1572868
  6.7 3.2 %copy-start.8 = (bf16[256,256]{1,0:T(8,128)(2,1)}, bf16[256,256]{1,0:T(8,128)(2,1)S(1)}, u32[]{:S(2)}) copy-start(bf16[256,256]{1,0:T(8,128)(2,1)S(1)} %collective-permute-done.5.vsib) | copy-start | bytes 393220
  6.7 8.3 %collective-permute-start.6 = (bf16[512,256]{1,0:T(8,128)(2,1)S(1)}, bf16[512,256]{1,0:T(8,128)(2,1)S(1)}, u32[]{:S(2)}, u32[]{:S(2)}) collective-permute-start(bf16[512,256]{1,0:T(8,128)(2,1)S(1)} %constant_dynamic-update-slice_fusion.2), channel_id=1, source_target_pairs={{0,4},{2,0},{4,8},{6,2},{8,12},{10,6},{12,16},{14,10},{16,20},{18,... | collective-permute-start | bytes 786440 | tf_op jit(solution)/shard_map/ppermute | solution.py:27
  8.3 13.8 %collective-permute-start.7 = (bf16[512,256]{1,0:T(8,128)(2,1)S(1)}, bf16[512,256]{1,0:T(8,128)(2,1)S(1)}, u32[]{:S(2)}, u32[]{:S(2)}) collective-permute-start(bf16[512,256]{1,0:T(8,128)(2,1)S(1)} %constant_dynamic-update-slice_fusion.2), channel_id=1, source_target_pairs={{0,8},{2,0},{4,12},{6,4},{8,16},{10,2},{12,20},{14,6},{16,24},{18,... | collective-permute-start | bytes 786440 | tf_op jit(solution)/shard_map/ppermute | solution.py:27
  9.9 2.0 %copy-start.4 = (bf16[272,256]{1,0:T(8,128)(2,1)}, bf16[272,256]{1,0:T(8,128)(2,1)S(1)}, u32[]{:S(2)}) copy-start(bf16[272,256]{1,0:T(8,128)(2,1)S(1)} %collective-permute-done.sib) | copy-start | bytes 417796
  9.9 11.1 %collective-permute-start.1 = (bf16[544,256]{1,0:T(8,128)(2,1)S(1)}, bf16[544,256]{1,0:T(8,128)(2,1)S(1)}, u32[]{:S(2)}, u32[]{:S(2)}) collective-permute-start(bf16[544,256]{1,0:T(8,128)(2,1)S(1)} %constant_dynamic-update-slice_fusion), channel_id=1, source_target_pairs={{0,4},{2,0},{4,8},{6,2},{8,12},{10,6},{12,16},{14,10},{16,20},{18,... | collective-permute-start | bytes 835592 | tf_op jit(solution)/shard_map/ppermute | solution.py:27
  11.5 9.9 %collective-permute-start.2 = (bf16[544,256]{1,0:T(8,128)(2,1)S(1)}, bf16[544,256]{1,0:T(8,128)(2,1)S(1)}, u32[]{:S(2)}, u32[]{:S(2)}) collective-permute-start(bf16[544,256]{1,0:T(8,128)(2,1)S(1)} %constant_dynamic-update-slice_fusion), channel_id=1, source_target_pairs={{0,8},{2,0},{4,12},{6,4},{8,16},{10,2},{12,20},{14,6},{16,24},{18,... | collective-permute-start | bytes 835592 | tf_op jit(solution)/shard_map/ppermute | solution.py:27
  11.9 0.7 %copy-start.6 = (bf16[256,256]{1,0:T(8,128)(2,1)}, bf16[256,256]{1,0:T(8,128)(2,1)S(1)}, u32[]{:S(2)}) copy-start(bf16[256,256]{1,0:T(8,128)(2,1)S(1)} %collective-permute-done.12.gsib) | copy-start | bytes 393220
  12.5 14.1 %collective-permute-start.13 = (bf16[512,256]{1,0:T(8,128)(2,1)S(1)}, bf16[512,256]{1,0:T(8,128)(2,1)S(1)}, u32[]{:S(2)}, u32[]{:S(2)}) collective-permute-start(bf16[512,256]{1,0:T(8,128)(2,1)S(1)} %constant_dynamic-update-slice_fusion.4), channel_id=1, source_target_pairs={{0,4},{2,0},{4,8},{6,2},{8,12},{10,6},{12,16},{14,10},{16,20},{18,... | collective-permute-start | bytes 786440 | tf_op jit(solution)/shard_map/ppermute | solution.py:27
  15.0 20.1 %copy-start.13 = (bf16[512,256]{1,0:T(8,128)(2,1)}, bf16[512,256]{1,0:T(8,128)(2,1)S(1)}, u32[]{:S(2)}) copy-start(bf16[512,256]{1,0:T(8,128)(2,1)S(1)} %collective-permute-done.6.vone) | copy-start | bytes 786436
  15.0 12.0 %collective-permute-start.14 = (bf16[512,256]{1,0:T(8,128)(2,1)S(1)}, bf16[512,256]{1,0:T(8,128)(2,1)S(1)}, u32[]{:S(2)}, u32[]{:S(2)}) collective-permute-start(bf16[512,256]{1,0:T(8,128)(2,1)S(1)} %constant_dynamic-update-slice_fusion.4), channel_id=1, source_target_pairs={{0,8},{2,0},{4,12},{6,4},{8,16},{10,2},{12,20},{14,6},{16,24},{18,... | collective-permute-start | bytes 786440 | tf_op jit(solution)/shard_map/ppermute | solution.py:27
  21.0 8.3 %copy-start = (bf16[544,256]{1,0:T(8,128)(2,1)}, bf16[544,256]{1,0:T(8,128)(2,1)S(1)}, u32[]{:S(2)}) copy-start(bf16[544,256]{1,0:T(8,128)(2,1)S(1)} %collective-permute-done.1.one) | copy-start | bytes 835588
  21.0 7.1 %collective-permute-start.3 = (bf16[544,256]{1,0:T(8,128)(2,1)S(1)}, bf16[544,256]{1,0:T(8,128)(2,1)S(1)}, u32[]{:S(2)}, u32[]{:S(2)}) collective-permute-start(bf16[544,256]{1,0:T(8,128)(2,1)S(1)} %collective-permute-done.1.one), channel_id=1, source_target_pairs={{0,2},{2,0},{4,6},{6,4},{8,10},{10,8},{12,14},{14,12},{16,18},{18,... | collective-permute-start | bytes 835592 | tf_op jit(solution)/shard_map/ppermute | solution.py:17
  21.4 7.9 %copy-start.1 = (bf16[544,256]{1,0:T(8,128)(2,1)}, bf16[544,256]{1,0:T(8,128)(2,1)S(1)}, u32[]{:S(2)}) copy-start(bf16[544,256]{1,0:T(8,128)(2,1)S(1)} %collective-permute-done.2.two) | copy-start | bytes 835588
  21.4 6.8 %collective-permute-start.4 = (bf16[544,256]{1,0:T(8,128)(2,1)S(1)}, bf16[544,256]{1,0:T(8,128)(2,1)S(1)}, u32[]{:S(2)}, u32[]{:S(2)}) collective-permute-start(bf16[544,256]{1,0:T(8,128)(2,1)S(1)} %collective-permute-done.2.two), channel_id=1, source_target_pairs={{0,2},{2,0},{4,6},{6,4},{8,10},{10,8},{12,14},{14,12},{16,18},{18,... | collective-permute-start | bytes 835592 | tf_op jit(solution)/shard_map/ppermute | solution.py:17
  22.2 12.9 %copy-start.14 = (bf16[512,256]{1,0:T(8,128)(2,1)}, bf16[512,256]{1,0:T(8,128)(2,1)S(1)}, u32[]{:S(2)}) copy-start(bf16[512,256]{1,0:T(8,128)(2,1)S(1)} %collective-permute-done.7.vtwo) | copy-start | bytes 786436
  22.2 37.2 %collective-permute-start.11 = (bf16[256,1024]{1,0:T(8,128)(2,1)S(1)}, bf16[256,1024]{1,0:T(8,128)(2,1)S(1)}, u32[]{:S(2)}, u32[]{:S(2)}) collective-permute-start(bf16[256,1024]{1,0:T(8,128)(2,1)S(1)} %copy-done.9), channel_id=1, source_target_pairs={{0,1},{1,0},{2,3},{3,2},{4,5},{5,4},{6,7},{7,6},{8,9},{9,8},{10,11... | collective-permute-start | bytes 1572872 | tf_op jit(solution)/shard_map/ppermute | solution.py:31
  26.6 17.1 %copy-start.11 = (bf16[512,256]{1,0:T(8,128)(2,1)}, bf16[512,256]{1,0:T(8,128)(2,1)S(1)}, u32[]{:S(2)}) copy-start(bf16[512,256]{1,0:T(8,128)(2,1)S(1)} %collective-permute-done.13.gone) | copy-start | bytes 786436
  26.6 7.8 %collective-permute-start.8 = (bf16[512,256]{1,0:T(8,128)(2,1)S(1)}, bf16[512,256]{1,0:T(8,128)(2,1)}, u32[]{:S(2)}, u32[]{:S(2)}) collective-permute-start(bf16[512,256]{1,0:T(8,128)(2,1)S(1)} %collective-permute-done.6.vone), channel_id=1, source_target_pairs={{0,2},{2,0},{4,6},{6,4},{8,10},{10,8},{12,14},{14,12},{16,18},{18,... | collective-permute-start | bytes 786440 | tf_op jit(solution)/shard_map/ppermute | solution.py:17
  27.0 16.7 %copy-start.12 = (bf16[512,256]{1,0:T(8,128)(2,1)}, bf16[512,256]{1,0:T(8,128)(2,1)S(1)}, u32[]{:S(2)}) copy-start(bf16[512,256]{1,0:T(8,128)(2,1)S(1)} %collective-permute-done.14.gtwo) | copy-start | bytes 786436
  27.0 8.1 %collective-permute-start.9 = (bf16[512,256]{1,0:T(8,128)(2,1)S(1)}, bf16[512,256]{1,0:T(8,128)(2,1)}, u32[]{:S(2)}, u32[]{:S(2)}) collective-permute-start(bf16[512,256]{1,0:T(8,128)(2,1)S(1)} %collective-permute-done.7.vtwo), channel_id=1, source_target_pairs={{0,2},{2,0},{4,6},{6,4},{8,10},{10,8},{12,14},{14,12},{16,18},{18,... | collective-permute-start | bytes 786440 | tf_op jit(solution)/shard_map/ppermute | solution.py:17
  28.1 1.2 %copy-start.2 = (bf16[544,256]{1,0:T(8,128)(2,1)}, bf16[544,256]{1,0:T(8,128)(2,1)S(1)}, u32[]{:S(2)}) copy-start(bf16[544,256]{1,0:T(8,128)(2,1)S(1)} %collective-permute-done.3.one_s) | copy-start | bytes 835588
  28.1 19.2 %collective-permute-start.15 = (bf16[512,256]{1,0:T(8,128)(2,1)S(1)}, bf16[512,256]{1,0:T(8,128)(2,1)}, u32[]{:S(2)}, u32[]{:S(2)}) collective-permute-start(bf16[512,256]{1,0:T(8,128)(2,1)S(1)} %collective-permute-done.13.gone), channel_id=1, source_target_pairs={{0,2},{2,0},{4,6},{6,4},{8,10},{10,8},{12,14},{14,12},{16,18},{18,... | collective-permute-start | bytes 786440 | tf_op jit(solution)/shard_map/ppermute | solution.py:17
  28.2 1.1 %copy-start.3 = (bf16[544,256]{1,0:T(8,128)(2,1)}, bf16[544,256]{1,0:T(8,128)(2,1)S(1)}, u32[]{:S(2)}) copy-start(bf16[544,256]{1,0:T(8,128)(2,1)S(1)} %collective-permute-done.4.two_s) | copy-start | bytes 835588
  28.2 22.9 %collective-permute-start.16 = (bf16[512,256]{1,0:T(8,128)(2,1)S(1)}, bf16[512,256]{1,0:T(8,128)(2,1)}, u32[]{:S(2)}, u32[]{:S(2)}) collective-permute-start(bf16[512,256]{1,0:T(8,128)(2,1)S(1)} %collective-permute-done.14.gtwo), channel_id=1, source_target_pairs={{0,2},{2,0},{4,6},{6,4},{8,10},{10,8},{12,14},{14,12},{16,18},{18,... | collective-permute-start | bytes 786440 | tf_op jit(solution)/shard_map/ppermute | solution.py:17
  34.4 10.9 %collective-permute-start.17 = (f32[8,256]{1,0:T(8,128)}, f32[8,256]{1,0:T(8,128)S(1)}, u32[]{:S(2)}, u32[]{:S(2)}) collective-permute-start(f32[8,256]{1,0:T(8,128)} %get-tuple-element.10.st_ref.st), channel_id=1, source_target_pairs={{0,2},{2,0},{4,6},{6,4},{8,10},{10,8},{12,14},{14,12},{16,18},{18,... | collective-permute-start | bytes 24584 | tf_op jit(solution)/shard_map/ppermute | solution.py:17
  43.7 15.7 %collective-permute-start.10 = (bf16[128,256]{1,0:T(8,128)(2,1)}, bf16[128,256]{1,0:T(8,128)(2,1)S(1)}, u32[]{:S(2)}, u32[]{:S(2)}) collective-permute-start(bf16[128,256]{1,0:T(8,128)(2,1)} %get-tuple-element.13), channel_id=1, source_target_pairs={{0,1},{1,0},{2,3},{3,2},{4,5},{5,4},{6,7},{7,6},{8,9},{9,8},{10,11... | collective-permute-start | bytes 196616 | tf_op jit(solution)/shard_map/ppermute | solution.py:31
  45.3 0.6 copy-start.16
  45.9 4.6 %collective-permute-start.18 = (f32[16,256]{1,0:T(8,128)S(1)}, f32[16,256]{1,0:T(8,128)S(1)}, u32[]{:S(2)}, u32[]{:S(2)}) collective-permute-start(f32[16,256]{1,0:T(8,128)S(1)} %constant_dynamic-update-slice_fusion.6), channel_id=1, source_target_pairs={{0,4},{2,0},{4,8},{6,2},{8,12},{10,6},{12,16},{14,10},{16,20},{18,... | collective-permute-start | bytes 49160 | tf_op jit(solution)/shard_map/ppermute | solution.py:27
  47.4 3.7 %collective-permute-start.19 = (f32[16,256]{1,0:T(8,128)S(1)}, f32[16,256]{1,0:T(8,128)S(1)}, u32[]{:S(2)}, u32[]{:S(2)}) collective-permute-start(f32[16,256]{1,0:T(8,128)S(1)} %constant_dynamic-update-slice_fusion.6), channel_id=1, source_target_pairs={{0,8},{2,0},{4,12},{6,4},{8,16},{10,2},{12,20},{14,6},{16,24},{18,... | collective-permute-start | bytes 49160 | tf_op jit(solution)/shard_map/ppermute | solution.py:27
  50.5 1.8 %copy-start.17 = (f32[16,256]{1,0:T(8,128)}, f32[16,256]{1,0:T(8,128)S(1)}, u32[]{:S(2)}) copy-start(f32[16,256]{1,0:T(8,128)S(1)} %collective-permute-done.18.sone) | copy-start | bytes 49156
  50.5 1.2 %collective-permute-start.20 = (f32[16,256]{1,0:T(8,128)S(1)}, f32[16,256]{1,0:T(8,128)S(1)}, u32[]{:S(2)}, u32[]{:S(2)}) collective-permute-start(f32[16,256]{1,0:T(8,128)S(1)} %collective-permute-done.18.sone), channel_id=1, source_target_pairs={{0,2},{2,0},{4,6},{6,4},{8,10},{10,8},{12,14},{14,12},{16,18},{18,... | collective-permute-start | bytes 49160 | tf_op jit(solution)/shard_map/ppermute | solution.py:17
  51.1 1.2 %copy-start.18 = (f32[16,256]{1,0:T(8,128)}, f32[16,256]{1,0:T(8,128)S(1)}, u32[]{:S(2)}) copy-start(f32[16,256]{1,0:T(8,128)S(1)} %collective-permute-done.19.stwo) | copy-start | bytes 49156
  51.1 1.2 %collective-permute-start.21 = (f32[16,256]{1,0:T(8,128)S(1)}, f32[16,256]{1,0:T(8,128)S(1)}, u32[]{:S(2)}, u32[]{:S(2)}) collective-permute-start(f32[16,256]{1,0:T(8,128)S(1)} %collective-permute-done.19.stwo), channel_id=1, source_target_pairs={{0,2},{2,0},{4,6},{6,4},{8,10},{10,8},{12,14},{14,12},{16,18},{18,... | collective-permute-start | bytes 49160 | tf_op jit(solution)/shard_map/ppermute | solution.py:17
  51.7 0.6 copy-start.19
  52.3 0.6 copy-start.20
  59.4 0.8 %copy-start.10 = (bf16[256,1024]{1,0:T(8,128)(2,1)}, bf16[256,1024]{1,0:T(8,128)(2,1)S(1)}, u32[]{:S(2)}) copy-start(bf16[256,1024]{1,0:T(8,128)(2,1)S(1)} %collective-permute-done.11.far_ref) | copy-start | bytes 1572868
  59.4 0.8 %copy-start.15 = (bf16[128,256]{1,0:T(8,128)(2,1)}, bf16[128,256]{1,0:T(8,128)(2,1)S(1)}, u32[]{:S(2)}) copy-start(bf16[128,256]{1,0:T(8,128)(2,1)S(1)} %collective-permute-done.10.got_ref) | copy-start | bytes 196612

commit v2 on v1

v2 whole, which is shorter than its diff:
```python
from functools import partial

import jax
import jax.numpy as jnp
from jax import lax
from jax.experimental import pallas as pl
from jax.experimental.pallas import tpu as pltpu
from jax.sharding import PartitionSpec as P


HD = 64
NEGATIVE = -1e30
REACH_ROWS = 16
F32 = jnp.float32
BF16 = jnp.bfloat16


def sibling(value):
    count = lax.axis_size("seq")
    return lax.ppermute(value, "seq", [(i, i ^ 1) for i in range(count)])


def chip_ring(value, step):
    chips = lax.axis_size("seq") // 2
    pairs = []
    for chip in range(chips):
        up, down = chip + step, chip - step
        pairs.append((2 * chip, 2 * up if up < chips else 2 * chip + 1))
        pairs.append((2 * chip + 1, 2 * down + 1 if down >= 0 else 2 * chip))
    return lax.ppermute(value, "seq", pairs)


def other_head(value):
    return lax.ppermute(value, "head", [(0, 1), (1, 0)])


def dot_nt(a, b):
    return lax.dot_general(a, b, (((1,), (1,)), ((), ())), preferred_element_type=F32)


def dot_nn(a, b):
    return lax.dot_general(a, b, (((1,), (0,)), ((), ())), preferred_element_type=F32)


def prepare_body(
    reach_ref, q_in, s_in, v_in, g_in, k_ref, vt_ref, g_ref, q_ref, s_ref, v_ref, sems
):
    length, width = q_ref.shape
    pairs = ((q_in, q_ref), (s_in, s_ref), (v_in, v_ref), (g_in, g_ref))
    copies = [pltpu.make_async_copy(a, b, sems.at[i]) for i, (a, b) in enumerate(pairs)]
    for copy in copies:
        copy.start()
    copies[0].wait()
    copies[1].wait()
    low = lax.broadcasted_iota(jnp.int32, (length, 128), 1) < HD
    scales = jnp.transpose(s_ref[...])
    for g in range(width // 128):
        lanes = slice(128 * g, 128 * g + 128)
        q = q_ref[:, lanes].astype(F32)
        square = q * q
        sum_low = jnp.sum(jnp.where(low, square, 0.0), axis=1, keepdims=True)
        sum_high = jnp.sum(jnp.where(low, 0.0, square), axis=1, keepdims=True)
        inverse = jnp.where(low, lax.rsqrt(sum_low + 1e-6), lax.rsqrt(sum_high + 1e-6))
        scale = jnp.where(low, scales[:, 2 * g : 2 * g + 1], scales[:, 2 * g + 1 : 2 * g + 2])
        k_ref[0:length, lanes] = ((q * inverse) * scale).astype(BF16)
    reach = jnp.full((REACH_ROWS, width), reach_ref[0].astype(F32), F32)
    k_ref[length:, :] = reach.astype(BF16)
    copies[2].wait()
    vt_ref[...] = jnp.transpose(v_ref[...].astype(F32)).astype(BF16)
    copies[3].wait()


def head_keys(k_ref, length, h):
    g = h // 2
    lane = lax.broadcasted_iota(jnp.int32, (length, 128), 1)
    keep = (lane < HD) if h % 2 == 0 else (lane >= HD)
    rows = k_ref[0:length, 128 * g : 128 * g + 128]
    return jnp.where(keep, rows, jnp.zeros_like(rows))


def far_slots(chips, sib, one, two, one_s, two_s):
    place = lax.axis_index("seq")
    odd = lax.rem(place, 2)
    chip, toward = lax.div(place, 2), 2 * odd - 1

    def inside(step):
        far = chip + step * toward
        return jnp.logical_and(far >= 0, far < chips)

    return [
        (sib, 0, 1, None),
        (one, 0, 2, inside(1)),
        (one, 1, 1, inside(1)),
        (two, 0, 4, inside(2)),
        (two, 1, 3, inside(2)),
        (one_s, 0, 3, inside(-1)),
        (one_s, 1, 2, inside(-1)),
        (two_s, 1, 4, inside(-2)),
    ]


def allowed_slots(reach_ref, slots, length):
    near = reach_ref[0].astype(F32)
    result = []
    for ref, block, distance, valid in slots:
        start = block * (length + REACH_ROWS) + length
        far = jnp.max(ref[start : start + REACH_ROWS, 0:128].astype(F32))
        allowed = jnp.minimum(near, far) >= float(distance)
        if valid is not None:
            allowed = jnp.logical_and(allowed, valid)
        result.append(allowed)
    return result


def off_diagonal(scores, row, column):
    rows = lax.broadcasted_iota(jnp.int32, scores.shape, 0) + row
    columns = lax.broadcasted_iota(jnp.int32, scores.shape, 1) + column
    return jnp.where(rows == columns, NEGATIVE, scores)


def stats_body(chips, reach_ref, own, sib, one, two, one_s, two_s, st_ref, m_ref, w_ref):
    length = own.shape[0] - REACH_ROWS
    heads = own.shape[1] // HD
    keys = [head_keys(own, length, h) for h in range(heads)]

    def tile(slot, ref, row, masked):
        for h in range(heads):
            g = h // 2
            rows = ref[row : row + length, 128 * g : 128 * g + 128]
            for part in range(0, length, 128):
                scores = dot_nt(rows, keys[h][part : part + 128, :])
                if masked:
                    scores = off_diagonal(scores, 0, part)
                top = jnp.max(scores, axis=0, keepdims=True)
                exponent = jnp.exp(scores - top)
                total = jnp.sum(exponent, axis=0, keepdims=True)
                lanes = slice(part, part + 128)
                at = 2 * heads * slot + h
                m_ref[at : at + 1, lanes] = top
                m_ref[at + heads : at + heads + 1, lanes] = total
                at = (slot * heads + h) * length
                w_ref[at : at + length, lanes] = exponent.astype(BF16)

    slots = far_slots(chips, sib, one, two, one_s, two_s)
    allowed = allowed_slots(reach_ref, slots, length)
    tile(0, own, 0, True)
    for index, slot in enumerate(slots):
        at = 2 * heads * (index + 1)
        m_ref[at : at + heads, :] = jnp.full((heads, length), NEGATIVE, F32)
        m_ref[at + heads : at + 2 * heads, :] = jnp.zeros((heads, length), F32)

        @pl.when(allowed[index])
        def _():
            tile(index + 1, slot[0], slot[1] * (length + REACH_ROWS), False)

    count = len(slots) + 1
    tops = [m_ref[2 * heads * s : 2 * heads * s + heads, :] for s in range(count)]
    top = tops[0]
    for other in tops[1:]:
        top = jnp.maximum(top, other)
    total = jnp.zeros((heads, length), F32)
    for s in range(count):
        at = 2 * heads * s
        factor = jnp.exp(tops[s] - top)
        total = total + factor * m_ref[at + heads : at + 2 * heads, :]
        m_ref[at : at + heads, :] = factor
    st_ref[0:heads, :] = top + jnp.log(total)
    st_ref[heads : 2 * heads, :] = total


def attend_body(
    chips, reach_ref, own, sib, one, two, one_s, two_s, v, vsib, vone, vtwo, vone_s, vtwo_s,
    st_ref, m_ref, w_ref, keep_ref, send_ref, acc, rows_ref,
):
    length = own.shape[0] - REACH_ROWS
    heads = own.shape[1] // HD

    def tile(slot, vref, vrow):
        for h in range(heads):
            at = (slot * heads + h) * length
            part = slice(HD * h, HD * h + HD)
            numer = dot_nn(vref[vrow + HD * h : vrow + HD * h + HD, :], w_ref[at : at + length, :])
            numer = numer * m_ref[2 * heads * slot + h : 2 * heads * slot + h + 1, :]
            if slot == 0:
                acc[part, :] = numer
            else:
                acc[part, :] += numer

    slots = far_slots(chips, sib, one, two, one_s, two_s)
    allowed = allowed_slots(reach_ref, slots, length)
    tile(0, v, 0)
    vrefs = [vsib, vone, vone, vtwo, vtwo, vone_s, vone_s, vtwo_s]
    for index, slot in enumerate(slots):

        @pl.when(allowed[index])
        def _():
            tile(index + 1, vrefs[index], slot[1] * heads * HD)

    for h in range(heads):
        part = slice(HD * h, HD * h + HD)
        acc[part, :] = acc[part, :] / st_ref[heads + h : heads + h + 1, :]
    rows_ref[...] = jnp.transpose(acc[...])
    half = length // 2
    mine = lax.axis_index("head")
    keep_ref[...] = rows_ref[pl.ds(pl.multiple_of(mine * half, half), half), :].astype(BF16)
    send_ref[...] = rows_ref[pl.ds(pl.multiple_of((1 - mine) * half, half), half), :].astype(BF16)


def grad_body(
    chips, reach_ref, own, sib, one, two, one_s, two_s, g0, gsib, gone, gtwo, gone_s, gtwo_s,
    st, ssib, sone, stwo, sone_s, stwo_s, out_ref, acc,
):
    length = own.shape[0] - REACH_ROWS
    heads = own.shape[1] // HD
    keys = [head_keys(own, length, h) for h in range(heads)]
    low = lax.broadcasted_iota(jnp.int32, (length, 128), 1) < HD

    def tile(ref, row, gref, grow, sref, srow, masked):
        for g in range(heads // 2):
            lanes = slice(128 * g, 128 * g + 128)
            grads = gref[grow : grow + length, lanes]
            far = ref[row : row + length, lanes]
            parts = []
            for h in (2 * g, 2 * g + 1):
                scores = dot_nt(keys[h], far)
                if masked:
                    scores = off_diagonal(scores, 0, 0)
                weights = jnp.exp(scores - sref[srow + h : srow + h + 1, :]).astype(BF16)
                zero = jnp.zeros_like(grads)
                some = jnp.where(low, grads, zero) if h % 2 == 0 else jnp.where(low, zero, grads)
                parts.append(dot_nn(weights, some))
            if masked:
                acc[:, lanes] = parts[0] + parts[1]
            else:
                acc[:, lanes] += parts[0] + parts[1]

    slots = far_slots(chips, sib, one, two, one_s, two_s)
    allowed = allowed_slots(reach_ref, slots, length)
    tile(own, 0, g0, 0, st, 0, True)
    grefs = [gsib, gone, gone, gtwo, gtwo, gone_s, gone_s, gtwo_s]
    srefs = [ssib, sone, sone, stwo, stwo, sone_s, sone_s, stwo_s]
    for index, slot in enumerate(slots):

        @pl.when(allowed[index])
        def _():
            block = slot[1]
            row = block * (length + REACH_ROWS)
            tile(slot[0], row, grefs[index], block * length, srefs[index], 2 * heads * block, False)

    out_ref[...] = acc[...].astype(BF16)


def join_body(own_ref, sib_ref, out_ref):
    rows = own_ref.shape[0]
    out_ref[0:rows, :] = own_ref[...]
    out_ref[rows:, :] = sib_ref[...]


def final_body(chips, reach_ref, keep_ref, got_ref, near_ref, far_ref, *refs):
    *grad_refs, mixed_out, grad_out, acc, mixed, grad, sems = refs
    total = dot_nn(keep_ref[...], near_ref[...]) + dot_nn(got_ref[...], far_ref[...])
    mixed[...] = total.astype(BF16)
    first = pltpu.make_async_copy(mixed, mixed_out, sems.at[0])
    first.start()
    grad_body(chips, reach_ref, *grad_refs, grad, acc)
    second = pltpu.make_async_copy(grad, grad_out, sems.at[1])
    second.start()
    first.wait()
    second.wait()


VMEM = pl.BlockSpec(memory_space=pltpu.VMEM)
SMEM = pl.BlockSpec(memory_space=pltpu.SMEM)


def call(body, args, outs, smem=1, scratch=()):
    specs = [SMEM] * smem + [VMEM] * (len(args) - smem)
    args = [*args[:smem], *(pltpu.with_memory_space_constraint(a, pltpu.VMEM) for a in args[smem:])]
    return pl.pallas_call(
        body,
        in_specs=specs,
        out_specs=[VMEM] * len(outs),
        out_shape=[pltpu.VMEM(shape, dtype) for shape, dtype in outs],
        compiler_params=pltpu.CompilerParams(vmem_limit_bytes=8 * 1024 * 1024),
        scratch_shapes=[pltpu.VMEM(shape, dtype) for shape, dtype in scratch],
    )(*args)


def gathered(own):
    sib = sibling(own)
    rows, width = own.shape
    (both,) = call(join_body, [own, sib], [((2 * rows, width), own.dtype)], smem=0)
    one, two = chip_ring(both, 1), chip_ring(both, 2)
    one, two = lax.optimization_barrier((one, two))
    return [own, sib, one, two, sibling(one), sibling(two)]


def compute(queries, values, scales, block_reach, out_weight, out_grad):
    length, width = queries.shape
    heads = scales.shape[1]
    chips = lax.axis_size("seq") // 2
    keys, turned, grads = pl.pallas_call(
        prepare_body,
        name="prepare",
        in_specs=[SMEM] + [pl.BlockSpec(memory_space=pltpu.HBM)] * 4,
        out_specs=[VMEM] * 3,
        out_shape=[
            pltpu.VMEM((length + REACH_ROWS, width), BF16),
            pltpu.VMEM((width, length), BF16),
            pltpu.VMEM((length, width), BF16),
        ],
        compiler_params=pltpu.CompilerParams(vmem_limit_bytes=8 * 1024 * 1024),
        scratch_shapes=[
            pltpu.VMEM((length, width), BF16),
            pltpu.VMEM((heads, length), F32),
            pltpu.VMEM((length, width), BF16),
            pltpu.SemaphoreType.DMA((4,)),
        ],
    )(block_reach, *(pltpu.with_memory_space_constraint(a, pltpu.HBM) for a in (queries, scales.T, values, out_grad)))
    key_set = gathered(keys)
    value_set = gathered(turned)
    grad_set = gathered(grads)
    far_weight = other_head(out_weight)
    stats, tops, weights = call(
        partial(stats_body, chips),
        [block_reach, *key_set],
        [((2 * heads, length), F32), ((9 * 2 * heads, length), F32), ((9 * heads * length, length), BF16)],
    )
    stat_set = gathered(stats)
    keep, send = call(
        partial(attend_body, chips),
        [block_reach, *key_set, *value_set, stats, tops, weights],
        [((length // 2, width), BF16), ((length // 2, width), BF16)],
        scratch=[((width, length), F32), ((length, width), F32)],
    )
    got = other_head(send)
    half, full = length // 2, out_weight.shape[1]
    inputs = [keep, got, out_weight, far_weight, *key_set, *grad_set, *stat_set]
    inputs = [pltpu.with_memory_space_constraint(a, pltpu.VMEM) for a in inputs]
    mixed, value_grad = pl.pallas_call(
        partial(final_body, chips),
        name="final",
        in_specs=[SMEM] + [VMEM] * len(inputs),
        out_specs=[pl.BlockSpec(memory_space=pltpu.HBM)] * 2,
        out_shape=[
            jax.ShapeDtypeStruct((half, full), BF16),
            jax.ShapeDtypeStruct((length, width), BF16),
        ],
        compiler_params=pltpu.CompilerParams(vmem_limit_bytes=8 * 1024 * 1024),
        scratch_shapes=[
            pltpu.VMEM((length, width), F32),
            pltpu.VMEM((half, full), BF16),
            pltpu.VMEM((length, width), BF16),
            pltpu.SemaphoreType.DMA((2,)),
        ],
    )(block_reach, *inputs)
    return (mixed, value_grad)


def solution(mesh):
    return jax.shard_map(
        compute,
        mesh=mesh,
        in_specs=(
            P("seq", "head"),
            P("seq", "head"),
            P("seq", "head"),
            P("seq"),
            P("head", None),
            P("seq", "head"),
        ),
        out_specs=(P(("seq", "head"), None), P("seq", "head")),
        check_vma=False,
    )
```

time: 62.7 us -> 47.4 us (0.76)
  the two profiles are of different devices: /device:TPU:8 before, /device:TPU:17 now
where the time goes in v2:
time: 47.4 us; the launch traced here: 47.2 us
  waiting for transfers between devices  19.5 us (41%)
  starting transfers between devices  16 us (34%)
  Pallas kernels  10.4 us (22%)
  between operations  1.36 us (3%)
    ppermute x8, waiting for transfers between devices, chip_ring(): return lax.ppermute(value, 'seq', pairs)  15.3 us
    ppermute x8, starting transfers between devices, chip_ring(): return lax.ppermute(value, 'seq', pairs)  7.84 us
    ppermute x12, starting transfers between devices, sibling(): return lax.ppermute(value, 'seq', [(i, i ^ 1) for i in range(count)])  5.7 us
    pallas_call x1, Pallas kernels, compute(): pl.pallas_call(partial(final_body, chips), name='final', in_specs=[SMEM]...  4.45 us
    pallas_call x6, Pallas kernels, call(): pl.pallas_call(body, in_specs=specs, out_specs=[VMEM] * len(outs), out_sh...  4.36 us
    ppermute x12, waiting for transfers between devices, sibling(): return lax.ppermute(value, 'seq', [(i, i ^ 1) for i in range(count)])  4.2 us
    ppermute x2, starting transfers between devices, other_head(): return lax.ppermute(value, 'head', [(0, 1), (1, 0)])  2.48 us
    pallas_call x1, Pallas kernels, compute(): pl.pallas_call(prepare_body, name='prepare', in_specs=[SMEM] + [pl.BlockS...  1.54 us
  transfers between devices with their start and end apart: 22, of which 13 were waited for; matrix products, arithmetic and copies ran while one was open for 0% of the time, Pallas kernels for 9%

profile of v2, /device:TPU:17, one launch (start us, length us, event | category | flops | bytes accessed | tf_op | source)
XLA Modules:
  0.0 47.2 jit_solution(7413874615949655180)
XLA Ops:
  1.3 1.5 %prepare.1 = (bf16[272,256]{1,0:T(8,128)(2,1)S(1)}, bf16[256,256]{1,0:T(8,128)(2,1)S(1)}, bf16[256,256]{1,0:T(8,128)(2,1)S(1)}) custom-call(s32[1]{0:T(128)S(6)} %copy.8.reach_ref, bf16[256,256]{1,0:T(8,128)(2,1)} %q_in.1, f32[4,256]{1,0:T(4,128)} %bitcast.1, bf16[256,256]{1,0:T(8,128)(2,1)} %v_in.1, bf16[256,256]{1,0:T(8,128)(2,1)} %g_in.1), custom_call_target="tpu_custom_call" | custom-call | tf_op jit(solution)/shard_map/prepare/pallas_call | solution.py:302
  2.8 0.7 %collective-permute-start = (bf16[272,256]{1,0:T(8,128)(2,1)S(1)}, bf16[272,256]{1,0:T(8,128)(2,1)S(1)}, u32[]{:S(2)}, u32[]{:S(2)}) collective-permute-start(bf16[272,256]{1,0:T(8,128)(2,1)S(1)} %get-tuple-element.18.own_ref.own.refs_0_), channel_id=1, source_target_pairs={{0,2},{2,0},{4,6},{6,4},{8,10},{10,8},{12,14},{14,12},{16,18},{18,... | collective-permute-start | bytes 417800 | tf_op jit(solution)/shard_map/ppermute | solution.py:20
  3.6 0.1 collective-permute-start.5
  3.6 0.9 %collective-permute-done.sib_ref.sib.refs_1_ = bf16[272,256]{1,0:T(8,128)(2,1)S(1)} collective-permute-done((bf16[272,256]{1,0:T(8,128)(2,1)S(1)}, bf16[272,256]{1,0:T(8,128)(2,1)S(1)}, u32[]{:S(2)}, u32[]{:S(2)}) %collective-permute-start) | collective-permute-done | bytes 139296 | tf_op jit(solution)/shard_map/ppermute | solution.py:20
  4.6 1.2 %collective-permute-start.1 = (bf16[544,256]{1,0:T(8,128)(2,1)S(1)}, bf16[544,256]{1,0:T(8,128)(2,1)S(1)}, u32[]{:S(2)}, u32[]{:S(2)}) collective-permute-start(bf16[544,256]{1,0:T(8,128)(2,1)S(1)} %shard_map.77), channel_id=1, source_target_pairs={{0,4},{2,0},{4,8},{6,2},{8,12},{10,6},{12,16},{14,10},{16,20},{18,... | collective-permute-start | bytes 835592 | tf_op jit(solution)/shard_map/ppermute | solution.py:30
  5.8 0.2 collective-permute-start.2
  5.9 0.0 collective-permute-done.5.sib_ref.vsib
  6.0 0.2 collective-permute-start.6
  6.1 1.8 %collective-permute-start.7 = (bf16[512,256]{1,0:T(8,128)(2,1)S(1)}, bf16[512,256]{1,0:T(8,128)(2,1)S(1)}, u32[]{:S(2)}, u32[]{:S(2)}) collective-permute-start(bf16[512,256]{1,0:T(8,128)(2,1)S(1)} %shard_map.78), channel_id=1, source_target_pairs={{0,8},{2,0},{4,12},{6,4},{8,16},{10,2},{12,20},{14,6},{16,24},{18,... | collective-permute-start | bytes 786440 | tf_op jit(solution)/shard_map/ppermute | solution.py:30
  7.9 0.0 copy-start
  7.9 0.7 %collective-permute-start.12 = (bf16[256,256]{1,0:T(8,128)(2,1)S(1)}, bf16[256,256]{1,0:T(8,128)(2,1)S(1)}, u32[]{:S(2)}, u32[]{:S(2)}) collective-permute-start(bf16[256,256]{1,0:T(8,128)(2,1)S(1)} %get-tuple-element.29.own_ref.refs_6_), channel_id=1, source_target_pairs={{0,2},{2,0},{4,6},{6,4},{8,10},{10,8},{12,14},{14,12},{16,18},{18,... | collective-permute-start | bytes 393224 | tf_op jit(solution)/shard_map/ppermute | solution.py:20
  8.6 1.0 %collective-permute-done.12.sib_ref.refs_7_ = bf16[256,256]{1,0:T(8,128)(2,1)S(1)} collective-permute-done((bf16[256,256]{1,0:T(8,128)(2,1)S(1)}, bf16[256,256]{1,0:T(8,128)(2,1)S(1)}, u32[]{:S(2)}, u32[]{:S(2)}) %collective-permute-start.12) | collective-permute-done | bytes 131104 | tf_op jit(solution)/shard_map/ppermute | solution.py:20
  9.6 2.3 %collective-permute-start.13 = (bf16[512,256]{1,0:T(8,128)(2,1)S(1)}, bf16[512,256]{1,0:T(8,128)(2,1)S(1)}, u32[]{:S(2)}, u32[]{:S(2)}) collective-permute-start(bf16[512,256]{1,0:T(8,128)(2,1)S(1)} %shard_map.81), channel_id=1, source_target_pairs={{0,4},{2,0},{4,8},{6,2},{8,12},{10,6},{12,16},{14,10},{16,20},{18,... | collective-permute-start | bytes 786440 | tf_op jit(solution)/shard_map/ppermute | solution.py:30
  11.9 1.4 %collective-permute-done.1.one.refs_2_ = bf16[544,256]{1,0:T(8,128)(2,1)S(1)} collective-permute-done((bf16[544,256]{1,0:T(8,128)(2,1)S(1)}, bf16[544,256]{1,0:T(8,128)(2,1)S(1)}, u32[]{:S(2)}, u32[]{:S(2)}) %collective-permute-start.1) | collective-permute-done | bytes 278560 | tf_op jit(solution)/shard_map/ppermute | solution.py:30
  13.3 0.3 collective-permute-start.14
  13.6 0.7 %collective-permute-done.2.two.refs_3_ = bf16[544,256]{1,0:T(8,128)(2,1)S(1)} collective-permute-done((bf16[544,256]{1,0:T(8,128)(2,1)S(1)}, bf16[544,256]{1,0:T(8,128)(2,1)S(1)}, u32[]{:S(2)}, u32[]{:S(2)}) %collective-permute-start.2) | collective-permute-done | bytes 278560 | tf_op jit(solution)/shard_map/ppermute | solution.py:30
  14.3 0.0 collective-permute-start.3
  14.3 4.6 %collective-permute-done.6.vone = bf16[512,256]{1,0:T(8,128)(2,1)S(1)} collective-permute-done((bf16[512,256]{1,0:T(8,128)(2,1)S(1)}, bf16[512,256]{1,0:T(8,128)(2,1)S(1)}, u32[]{:S(2)}, u32[]{:S(2)}) %collective-permute-start.6) | collective-permute-done | bytes 262176 | tf_op jit(solution)/shard_map/ppermute | solution.py:30
  18.9 0.3 collective-permute-start.4
  19.2 0.5 %collective-permute-done.7.vtwo = bf16[512,256]{1,0:T(8,128)(2,1)S(1)} collective-permute-done((bf16[512,256]{1,0:T(8,128)(2,1)S(1)}, bf16[512,256]{1,0:T(8,128)(2,1)S(1)}, u32[]{:S(2)}, u32[]{:S(2)}) %collective-permute-start.7) | collective-permute-done | bytes 262176 | tf_op jit(solution)/shard_map/ppermute | solution.py:30
  19.7 1.2 %collective-permute-start.11 = (bf16[256,1024]{1,0:T(8,128)(2,1)}, bf16[256,1024]{1,0:T(8,128)(2,1)S(1)}, u32[]{:S(2)}, u32[]{:S(2)}) collective-permute-start(bf16[256,1024]{1,0:T(8,128)(2,1)} %near_ref.1), channel_id=1, source_target_pairs={{0,1},{1,0},{2,3},{3,2},{4,5},{5,4},{6,7},{7,6},{8,9},{9,8},{10,11... | collective-permute-start | bytes 1572872 | tf_op jit(solution)/shard_map/ppermute | solution.py:34
  20.9 3.7 %collective-permute-done.13.refs_8_ = bf16[512,256]{1,0:T(8,128)(2,1)S(1)} collective-permute-done((bf16[512,256]{1,0:T(8,128)(2,1)S(1)}, bf16[512,256]{1,0:T(8,128)(2,1)S(1)}, u32[]{:S(2)}, u32[]{:S(2)}) %collective-permute-start.13) | collective-permute-done | bytes 262176 | tf_op jit(solution)/shard_map/ppermute | solution.py:30
  24.6 0.3 collective-permute-start.8
  24.8 0.8 %collective-permute-done.14.refs_9_ = bf16[512,256]{1,0:T(8,128)(2,1)S(1)} collective-permute-done((bf16[512,256]{1,0:T(8,128)(2,1)S(1)}, bf16[512,256]{1,0:T(8,128)(2,1)S(1)}, u32[]{:S(2)}, u32[]{:S(2)}) %collective-permute-start.14) | collective-permute-done | bytes 262176 | tf_op jit(solution)/shard_map/ppermute | solution.py:30
  25.6 0.0 collective-permute-start.9
  25.6 0.0 collective-permute-done.3.one_s.refs_4_
  25.6 0.5 %collective-permute-start.15 = (bf16[512,256]{1,0:T(8,128)(2,1)S(1)}, bf16[512,256]{1,0:T(8,128)(2,1)S(1)}, u32[]{:S(2)}, u32[]{:S(2)}) collective-permute-start(bf16[512,256]{1,0:T(8,128)(2,1)S(1)} %collective-permute-done.13.refs_8_), channel_id=1, source_target_pairs={{0,2},{2,0},{4,6},{6,4},{8,10},{10,8},{12,14},{14,12},{16,18},{18,... | collective-permute-start | bytes 786440 | tf_op jit(solution)/shard_map/ppermute | solution.py:20
  26.2 0.0 collective-permute-done.4.two_s.refs_5_
  26.2 0.1 collective-permute-start.16
  26.2 2.9 %shard_map.79 = (f32[8,256]{1,0:T(8,128)S(1)}, f32[72,256]{1,0:T(8,128)S(1)}, bf16[9216,256]{1,0:T(8,128)(2,1)S(1)}) custom-call(s32[1]{0:T(128)S(6)} %copy.8.reach_ref, bf16[272,256]{1,0:T(8,128)(2,1)S(1)} %get-tuple-element.18.own_ref.own.refs_0_, bf16[272,256]{1,0:T(8,128)(2,1)S(1)} %collective-permute-done.sib_ref.sib.refs_1_, ...), custom_call_target="tpu_custom_call" | custom-call | tf_op jit(solution)/shard_map/pallas_call | solution.py:279
  29.1 0.0 collective-permute-done.8.vone_s
  29.1 0.0 collective-permute-done.9.vtwo_s
  29.1 1.4 %shard_map.80 = (bf16[128,256]{1,0:T(8,128)(2,1)S(1)}, bf16[128,256]{1,0:T(8,128)(2,1)S(1)}) custom-call(s32[1]{0:T(128)S(6)} %copy.8.reach_ref, bf16[272,256]{1,0:T(8,128)(2,1)S(1)} %get-tuple-element.18.own_ref.own.refs_0_, bf16[272,256]{1,0:T(8,128)(2,1)S(1)} %collective-permute-done.sib_ref.sib.refs_1_, ...), custom_call_target="tpu_custom_call" | custom-call | tf_op jit(solution)/shard_map/pallas_call | solution.py:279
  30.6 1.3 %collective-permute-start.10 = (bf16[128,256]{1,0:T(8,128)(2,1)S(1)}, bf16[128,256]{1,0:T(8,128)(2,1)S(1)}, u32[]{:S(2)}, u32[]{:S(2)}) collective-permute-start(bf16[128,256]{1,0:T(8,128)(2,1)S(1)} %get-tuple-element.28), channel_id=1, source_target_pairs={{0,1},{1,0},{2,3},{3,2},{4,5},{5,4},{6,7},{7,6},{8,9},{9,8},{10,11... | collective-permute-start | bytes 196616 | tf_op jit(solution)/shard_map/ppermute | solution.py:34
  31.8 0.1 collective-permute-start.17
  31.9 1.1 %collective-permute-done.17.sib_ref.refs_13_ = f32[8,256]{1,0:T(8,128)S(1)} collective-permute-done((f32[8,256]{1,0:T(8,128)S(1)}, f32[8,256]{1,0:T(8,128)S(1)}, u32[]{:S(2)}, u32[]{:S(2)}) %collective-permute-start.17) | collective-permute-done | bytes 8224 | tf_op jit(solution)/shard_map/ppermute | solution.py:20
  33.0 1.6 %collective-permute-start.18 = (f32[16,256]{1,0:T(8,128)S(1)}, f32[16,256]{1,0:T(8,128)S(1)}, u32[]{:S(2)}, u32[]{:S(2)}) collective-permute-start(f32[16,256]{1,0:T(8,128)S(1)} %shard_map.82), channel_id=1, source_target_pairs={{0,4},{2,0},{4,8},{6,2},{8,12},{10,6},{12,16},{14,10},{16,20},{18,... | collective-permute-start | bytes 49160 | tf_op jit(solution)/shard_map/ppermute | solution.py:30
  34.7 1.2 %collective-permute-done.18.refs_14_ = f32[16,256]{1,0:T(8,128)S(1)} collective-permute-done((f32[16,256]{1,0:T(8,128)S(1)}, f32[16,256]{1,0:T(8,128)S(1)}, u32[]{:S(2)}, u32[]{:S(2)}) %collective-permute-start.18) | collective-permute-done | bytes 16416 | tf_op jit(solution)/shard_map/ppermute | solution.py:30
  35.9 0.3 collective-permute-start.19
  36.2 2.3 %collective-permute-done.19.refs_15_ = f32[16,256]{1,0:T(8,128)S(1)} collective-permute-done((f32[16,256]{1,0:T(8,128)S(1)}, f32[16,256]{1,0:T(8,128)S(1)}, u32[]{:S(2)}, u32[]{:S(2)}) %collective-permute-start.19) | collective-permute-done | bytes 16416 | tf_op jit(solution)/shard_map/ppermute | solution.py:30
  38.5 3.1 %collective-permute-start.20 = (f32[16,256]{1,0:T(8,128)S(1)}, f32[16,256]{1,0:T(8,128)S(1)}, u32[]{:S(2)}, u32[]{:S(2)}) collective-permute-start(f32[16,256]{1,0:T(8,128)S(1)} %collective-permute-done.18.refs_14_), channel_id=1, source_target_pairs={{0,2},{2,0},{4,6},{6,4},{8,10},{10,8},{12,14},{14,12},{16,18},{18,... | collective-permute-start | bytes 49160 | tf_op jit(solution)/shard_map/ppermute | solution.py:20
  41.6 0.0 collective-permute-done.11.far_ref
  41.6 0.0 collective-permute-start.21
  41.6 0.0 collective-permute-done.15.refs_10_
  41.6 0.0 collective-permute-done.16.refs_11_
  41.6 0.8 %collective-permute-done.20.refs_16_ = f32[16,256]{1,0:T(8,128)S(1)} collective-permute-done((f32[16,256]{1,0:T(8,128)S(1)}, f32[16,256]{1,0:T(8,128)S(1)}, u32[]{:S(2)}, u32[]{:S(2)}) %collective-permute-start.20) | collective-permute-done | bytes 16416 | tf_op jit(solution)/shard_map/ppermute | solution.py:20
  42.4 0.3 collective-permute-done.21.refs_17_
  42.8 0.0 collective-permute-done.10.got_ref
  42.8 0.0 copy-done
  42.8 4.5 %final.1 = (bf16[128,1024]{1,0:T(8,128)(2,1)}, bf16[256,256]{1,0:T(8,128)(2,1)}) custom-call(s32[1]{0:T(128)S(6)} %copy.8.reach_ref, bf16[128,256]{1,0:T(8,128)(2,1)S(1)} %get-tuple-element.27.keep_ref, bf16[128,256]{1,0:T(8,128)(2,1)S(1)} %collective-permute-done.10.got_ref, bf16[256,1024]{1,0:T(8,128)(2,1)S(1)} %copy-done, ...), custom_call_target="tpu_custom_call" | custom-call | tf_op jit(solution)/shard_map/final/pallas_call | solution.py:340
  (4 shorter events, 0.1 us)
Async XLA Ops:
  2.8 1.7 %collective-permute-start = (bf16[272,256]{1,0:T(8,128)(2,1)S(1)}, bf16[272,256]{1,0:T(8,128)(2,1)S(1)}, u32[]{:S(2)}, u32[]{:S(2)}) collective-permute-start(bf16[272,256]{1,0:T(8,128)(2,1)S(1)} %get-tuple-element.18.own_ref.own.refs_0_), channel_id=1, source_target_pairs={{0,2},{2,0},{4,6},{6,4},{8,10},{10,8},{12,14},{14,12},{16,18},{18,... | collective-permute-start | bytes 417800 | tf_op jit(solution)/shard_map/ppermute | solution.py:20
  3.6 2.4 %collective-permute-start.5 = (bf16[256,256]{1,0:T(8,128)(2,1)S(1)}, bf16[256,256]{1,0:T(8,128)(2,1)S(1)}, u32[]{:S(2)}, u32[]{:S(2)}) collective-permute-start(bf16[256,256]{1,0:T(8,128)(2,1)S(1)} %get-tuple-element.21.own_ref.v), channel_id=1, source_target_pairs={{0,2},{2,0},{4,6},{6,4},{8,10},{10,8},{12,14},{14,12},{16,18},{18,... | collective-permute-start | bytes 393224 | tf_op jit(solution)/shard_map/ppermute | solution.py:20
  4.6 8.7 %collective-permute-start.1 = (bf16[544,256]{1,0:T(8,128)(2,1)S(1)}, bf16[544,256]{1,0:T(8,128)(2,1)S(1)}, u32[]{:S(2)}, u32[]{:S(2)}) collective-permute-start(bf16[544,256]{1,0:T(8,128)(2,1)S(1)} %shard_map.77), channel_id=1, source_target_pairs={{0,4},{2,0},{4,8},{6,2},{8,12},{10,6},{12,16},{14,10},{16,20},{18,... | collective-permute-start | bytes 835592 | tf_op jit(solution)/shard_map/ppermute | solution.py:30
  5.8 8.6 %collective-permute-start.2 = (bf16[544,256]{1,0:T(8,128)(2,1)S(1)}, bf16[544,256]{1,0:T(8,128)(2,1)S(1)}, u32[]{:S(2)}, u32[]{:S(2)}) collective-permute-start(bf16[544,256]{1,0:T(8,128)(2,1)S(1)} %shard_map.77), channel_id=1, source_target_pairs={{0,8},{2,0},{4,12},{6,4},{8,16},{10,2},{12,20},{14,6},{16,24},{18,... | collective-permute-start | bytes 835592 | tf_op jit(solution)/shard_map/ppermute | solution.py:30
  6.0 13.0 %collective-permute-start.6 = (bf16[512,256]{1,0:T(8,128)(2,1)S(1)}, bf16[512,256]{1,0:T(8,128)(2,1)S(1)}, u32[]{:S(2)}, u32[]{:S(2)}) collective-permute-start(bf16[512,256]{1,0:T(8,128)(2,1)S(1)} %shard_map.78), channel_id=1, source_target_pairs={{0,4},{2,0},{4,8},{6,2},{8,12},{10,6},{12,16},{14,10},{16,20},{18,... | collective-permute-start | bytes 786440 | tf_op jit(solution)/shard_map/ppermute | solution.py:30
  6.1 13.6 %collective-permute-start.7 = (bf16[512,256]{1,0:T(8,128)(2,1)S(1)}, bf16[512,256]{1,0:T(8,128)(2,1)S(1)}, u32[]{:S(2)}, u32[]{:S(2)}) collective-permute-start(bf16[512,256]{1,0:T(8,128)(2,1)S(1)} %shard_map.78), channel_id=1, source_target_pairs={{0,8},{2,0},{4,12},{6,4},{8,16},{10,2},{12,20},{14,6},{16,24},{18,... | collective-permute-start | bytes 786440 | tf_op jit(solution)/shard_map/ppermute | solution.py:30
  7.9 34.9 %copy-start = (bf16[256,1024]{1,0:T(8,128)(2,1)S(1)}, bf16[256,1024]{1,0:T(8,128)(2,1)}, u32[]{:S(2)}) copy-start(bf16[256,1024]{1,0:T(8,128)(2,1)} %near_ref.1) | copy-start | bytes 1572868
  7.9 1.6 %collective-permute-start.12 = (bf16[256,256]{1,0:T(8,128)(2,1)S(1)}, bf16[256,256]{1,0:T(8,128)(2,1)S(1)}, u32[]{:S(2)}, u32[]{:S(2)}) collective-permute-start(bf16[256,256]{1,0:T(8,128)(2,1)S(1)} %get-tuple-element.29.own_ref.refs_6_), channel_id=1, source_target_pairs={{0,2},{2,0},{4,6},{6,4},{8,10},{10,8},{12,14},{14,12},{16,18},{18,... | collective-permute-start | bytes 393224 | tf_op jit(solution)/shard_map/ppermute | solution.py:20
  9.6 15.0 %collective-permute-start.13 = (bf16[512,256]{1,0:T(8,128)(2,1)S(1)}, bf16[512,256]{1,0:T(8,128)(2,1)S(1)}, u32[]{:S(2)}, u32[]{:S(2)}) collective-permute-start(bf16[512,256]{1,0:T(8,128)(2,1)S(1)} %shard_map.81), channel_id=1, source_target_pairs={{0,4},{2,0},{4,8},{6,2},{8,12},{10,6},{12,16},{14,10},{16,20},{18,... | collective-permute-start | bytes 786440 | tf_op jit(solution)/shard_map/ppermute | solution.py:30
  13.3 12.3 %collective-permute-start.14 = (bf16[512,256]{1,0:T(8,128)(2,1)S(1)}, bf16[512,256]{1,0:T(8,128)(2,1)S(1)}, u32[]{:S(2)}, u32[]{:S(2)}) collective-permute-start(bf16[512,256]{1,0:T(8,128)(2,1)S(1)} %shard_map.81), channel_id=1, source_target_pairs={{0,8},{2,0},{4,12},{6,4},{8,16},{10,2},{12,20},{14,6},{16,24},{18,... | collective-permute-start | bytes 786440 | tf_op jit(solution)/shard_map/ppermute | solution.py:30
  14.3 11.3 %collective-permute-start.3 = (bf16[544,256]{1,0:T(8,128)(2,1)S(1)}, bf16[544,256]{1,0:T(8,128)(2,1)S(1)}, u32[]{:S(2)}, u32[]{:S(2)}) collective-permute-start(bf16[544,256]{1,0:T(8,128)(2,1)S(1)} %collective-permute-done.1.one.refs_2_), channel_id=1, source_target_pairs={{0,2},{2,0},{4,6},{6,4},{8,10},{10,8},{12,14},{14,12},{16,18},{18,... | collective-permute-start | bytes 835592 | tf_op jit(solution)/shard_map/ppermute | solution.py:20
  18.9 7.2 %collective-permute-start.4 = (bf16[544,256]{1,0:T(8,128)(2,1)S(1)}, bf16[544,256]{1,0:T(8,128)(2,1)S(1)}, u32[]{:S(2)}, u32[]{:S(2)}) collective-permute-start(bf16[544,256]{1,0:T(8,128)(2,1)S(1)} %collective-permute-done.2.two.refs_3_), channel_id=1, source_target_pairs={{0,2},{2,0},{4,6},{6,4},{8,10},{10,8},{12,14},{14,12},{16,18},{18,... | collective-permute-start | bytes 835592 | tf_op jit(solution)/shard_map/ppermute | solution.py:20
  19.7 21.9 %collective-permute-start.11 = (bf16[256,1024]{1,0:T(8,128)(2,1)}, bf16[256,1024]{1,0:T(8,128)(2,1)S(1)}, u32[]{:S(2)}, u32[]{:S(2)}) collective-permute-start(bf16[256,1024]{1,0:T(8,128)(2,1)} %near_ref.1), channel_id=1, source_target_pairs={{0,1},{1,0},{2,3},{3,2},{4,5},{5,4},{6,7},{7,6},{8,9},{9,8},{10,11... | collective-permute-start | bytes 1572872 | tf_op jit(solution)/shard_map/ppermute | solution.py:34
  24.6 4.5 %collective-permute-start.8 = (bf16[512,256]{1,0:T(8,128)(2,1)S(1)}, bf16[512,256]{1,0:T(8,128)(2,1)S(1)}, u32[]{:S(2)}, u32[]{:S(2)}) collective-permute-start(bf16[512,256]{1,0:T(8,128)(2,1)S(1)} %collective-permute-done.6.vone), channel_id=1, source_target_pairs={{0,2},{2,0},{4,6},{6,4},{8,10},{10,8},{12,14},{14,12},{16,18},{18,... | collective-permute-start | bytes 786440 | tf_op jit(solution)/shard_map/ppermute | solution.py:20
  25.6 3.5 %collective-permute-start.9 = (bf16[512,256]{1,0:T(8,128)(2,1)S(1)}, bf16[512,256]{1,0:T(8,128)(2,1)S(1)}, u32[]{:S(2)}, u32[]{:S(2)}) collective-permute-start(bf16[512,256]{1,0:T(8,128)(2,1)S(1)} %collective-permute-done.7.vtwo), channel_id=1, source_target_pairs={{0,2},{2,0},{4,6},{6,4},{8,10},{10,8},{12,14},{14,12},{16,18},{18,... | collective-permute-start | bytes 786440 | tf_op jit(solution)/shard_map/ppermute | solution.py:20
  25.6 15.9 %collective-permute-start.15 = (bf16[512,256]{1,0:T(8,128)(2,1)S(1)}, bf16[512,256]{1,0:T(8,128)(2,1)S(1)}, u32[]{:S(2)}, u32[]{:S(2)}) collective-permute-start(bf16[512,256]{1,0:T(8,128)(2,1)S(1)} %collective-permute-done.13.refs_8_), channel_id=1, source_target_pairs={{0,2},{2,0},{4,6},{6,4},{8,10},{10,8},{12,14},{14,12},{16,18},{18,... | collective-permute-start | bytes 786440 | tf_op jit(solution)/shard_map/ppermute | solution.py:20
  26.2 15.4 %collective-permute-start.16 = (bf16[512,256]{1,0:T(8,128)(2,1)S(1)}, bf16[512,256]{1,0:T(8,128)(2,1)S(1)}, u32[]{:S(2)}, u32[]{:S(2)}) collective-permute-start(bf16[512,256]{1,0:T(8,128)(2,1)S(1)} %collective-permute-done.14.refs_9_), channel_id=1, source_target_pairs={{0,2},{2,0},{4,6},{6,4},{8,10},{10,8},{12,14},{14,12},{16,18},{18,... | collective-permute-start | bytes 786440 | tf_op jit(solution)/shard_map/ppermute | solution.py:20
  30.6 12.2 %collective-permute-start.10 = (bf16[128,256]{1,0:T(8,128)(2,1)S(1)}, bf16[128,256]{1,0:T(8,128)(2,1)S(1)}, u32[]{:S(2)}, u32[]{:S(2)}) collective-permute-start(bf16[128,256]{1,0:T(8,128)(2,1)S(1)} %get-tuple-element.28), channel_id=1, source_target_pairs={{0,1},{1,0},{2,3},{3,2},{4,5},{5,4},{6,7},{7,6},{8,9},{9,8},{10,11... | collective-permute-start | bytes 196616 | tf_op jit(solution)/shard_map/ppermute | solution.py:34
  31.8 1.2 %collective-permute-start.17 = (f32[8,256]{1,0:T(8,128)S(1)}, f32[8,256]{1,0:T(8,128)S(1)}, u32[]{:S(2)}, u32[]{:S(2)}) collective-permute-start(f32[8,256]{1,0:T(8,128)S(1)} %get-tuple-element.24.st_ref.own_ref.refs_12_), channel_id=1, source_target_pairs={{0,2},{2,0},{4,6},{6,4},{8,10},{10,8},{12,14},{14,12},{16,18},{18,... | collective-permute-start | bytes 24584 | tf_op jit(solution)/shard_map/ppermute | solution.py:20
  33.0 2.9 %collective-permute-start.18 = (f32[16,256]{1,0:T(8,128)S(1)}, f32[16,256]{1,0:T(8,128)S(1)}, u32[]{:S(2)}, u32[]{:S(2)}) collective-permute-start(f32[16,256]{1,0:T(8,128)S(1)} %shard_map.82), channel_id=1, source_target_pairs={{0,4},{2,0},{4,8},{6,2},{8,12},{10,6},{12,16},{14,10},{16,20},{18,... | collective-permute-start | bytes 49160 | tf_op jit(solution)/shard_map/ppermute | solution.py:30
  35.9 2.6 %collective-permute-start.19 = (f32[16,256]{1,0:T(8,128)S(1)}, f32[16,256]{1,0:T(8,128)S(1)}, u32[]{:S(2)}, u32[]{:S(2)}) collective-permute-start(f32[16,256]{1,0:T(8,128)S(1)} %shard_map.82), channel_id=1, source_target_pairs={{0,8},{2,0},{4,12},{6,4},{8,16},{10,2},{12,20},{14,6},{16,24},{18,... | collective-permute-start | bytes 49160 | tf_op jit(solution)/shard_map/ppermute | solution.py:30
  38.5 3.9 %collective-permute-start.20 = (f32[16,256]{1,0:T(8,128)S(1)}, f32[16,256]{1,0:T(8,128)S(1)}, u32[]{:S(2)}, u32[]{:S(2)}) collective-permute-start(f32[16,256]{1,0:T(8,128)S(1)} %collective-permute-done.18.refs_14_), channel_id=1, source_target_pairs={{0,2},{2,0},{4,6},{6,4},{8,10},{10,8},{12,14},{14,12},{16,18},{18,... | collective-permute-start | bytes 49160 | tf_op jit(solution)/shard_map/ppermute | solution.py:20
  41.6 1.2 %collective-permute-start.21 = (f32[16,256]{1,0:T(8,128)S(1)}, f32[16,256]{1,0:T(8,128)S(1)}, u32[]{:S(2)}, u32[]{:S(2)}) collective-permute-start(f32[16,256]{1,0:T(8,128)S(1)} %collective-permute-done.19.refs_15_), channel_id=1, source_target_pairs={{0,2},{2,0},{4,6},{6,4},{8,10},{10,8},{12,14},{14,12},{16,18},{18,... | collective-permute-start | bytes 49160 | tf_op jit(solution)/shard_map/ppermute | solution.py:20

commit v3 on v2

v3 whole, which is shorter than its diff:
```python
from functools import partial

import jax
import jax.numpy as jnp
from jax import lax
from jax.experimental import pallas as pl
from jax.experimental.pallas import tpu as pltpu
from jax.sharding import PartitionSpec as P


HD = 64
NEGATIVE = -1e30
REACH_ROWS = 16
SHIFT_ROWS = 16
LANES = 128
F32 = jnp.float32
BF16 = jnp.bfloat16


def sibling(value):
    count = lax.axis_size("seq")
    return lax.ppermute(value, "seq", [(i, i ^ 1) for i in range(count)])


def chip_ring(value, step):
    chips = lax.axis_size("seq") // 2
    pairs = []
    for chip in range(chips):
        up, down = chip + step, chip - step
        pairs.append((2 * chip, 2 * up if up < chips else 2 * chip + 1))
        pairs.append((2 * chip + 1, 2 * down + 1 if down >= 0 else 2 * chip))
    return lax.ppermute(value, "seq", pairs)


def other_head(value):
    return lax.ppermute(value, "head", [(0, 1), (1, 0)])


def dot_nt(a, b):
    return lax.dot_general(a, b, (((1,), (1,)), ((), ())), preferred_element_type=F32)


def dot_nn(a, b):
    return lax.dot_general(a, b, (((1,), (0,)), ((), ())), preferred_element_type=F32)


def prepare_body(
    reach_ref, q_in, s_in, v_in, g_in, k_ref, vt_ref, gt_ref, q_ref, s_ref, v_ref, g_ref, sems
):
    length, width = q_ref.shape
    pairs = ((q_in, q_ref), (s_in, s_ref), (v_in, v_ref), (g_in, g_ref))
    copies = [pltpu.make_async_copy(a, b, sems.at[i]) for i, (a, b) in enumerate(pairs)]
    for copy in copies:
        copy.start()
    copies[0].wait()
    copies[1].wait()
    low = lax.broadcasted_iota(jnp.int32, (length, LANES), 1) < HD
    scales = jnp.transpose(s_ref[...])
    for g in range(width // LANES):
        lanes = slice(LANES * g, LANES * g + LANES)
        q = q_ref[:, lanes].astype(F32)
        square = q * q
        sum_low = jnp.sum(jnp.where(low, square, 0.0), axis=1, keepdims=True)
        sum_high = jnp.sum(jnp.where(low, 0.0, square), axis=1, keepdims=True)
        inverse = jnp.where(low, lax.rsqrt(sum_low + 1e-6), lax.rsqrt(sum_high + 1e-6))
        scale = jnp.where(low, scales[:, 2 * g : 2 * g + 1], scales[:, 2 * g + 1 : 2 * g + 2])
        k_ref[0:length, lanes] = ((q * inverse) * scale).astype(BF16)
    reach = jnp.full((REACH_ROWS, width), reach_ref[0].astype(F32), F32)
    k_ref[length:, :] = reach.astype(BF16)
    copies[2].wait()
    vt_ref[...] = jnp.transpose(v_ref[...].astype(F32)).astype(BF16)
    copies[3].wait()
    gt_ref[...] = jnp.transpose(g_ref[...].astype(F32)).astype(BF16)


def join_body(*refs):
    *parts, out_ref = refs
    at = 0
    for ref in parts:
        out_ref[at : at + ref.shape[0], :] = ref[...]
        at += ref.shape[0]


def head_keys(k_ref, length, h):
    g = h // 2
    lane = lax.broadcasted_iota(jnp.int32, (length, LANES), 1)
    keep = (lane < HD) if h % 2 == 0 else (lane >= HD)
    rows = k_ref[0:length, LANES * g : LANES * g + LANES]
    return jnp.where(keep, rows, jnp.zeros_like(rows))


NEAR = ((0, 0, 0, None), (1, 0, 1, None))
DIRECT = ((0, 0, 2, 1), (0, 1, 1, 1), (1, 0, 4, 2), (1, 1, 3, 2))
PASSED = ((0, 0, 3, -1), (0, 1, 2, -1), (1, 1, 4, -2))


def allowed_slots(chips, reach_ref, slots, keys, length):
    place = lax.axis_index("seq")
    chip, toward = lax.div(place, 2), 2 * lax.rem(place, 2) - 1
    near = reach_ref[0].astype(F32)
    result = []
    for index, block, distance, away in slots:
        if distance == 0:
            result.append(None)
            continue
        start = block * (length + REACH_ROWS) + length
        far = jnp.max(keys[index][start : start + REACH_ROWS, 0:LANES].astype(F32))
        allowed = jnp.minimum(near, far) >= float(distance)
        if away is not None:
            other = chip + away * toward
            allowed = jnp.logical_and(allowed, jnp.logical_and(other >= 0, other < chips))
        result.append(allowed)
    return result


def off_diagonal(scores, row, column):
    rows = lax.broadcasted_iota(jnp.int32, scores.shape, 0) + row
    columns = lax.broadcasted_iota(jnp.int32, scores.shape, 1) + column
    return jnp.where(rows == columns, NEGATIVE, scores)


def stats_body(chips, slots, reach_ref, own, *refs):
    count = len({slot[0] for slot in slots})
    keys, rest = refs[:count], refs[count:]
    length = own.shape[0] - REACH_ROWS
    heads = own.shape[1] // HD
    last = slots is PASSED
    if last:
        near_ref, direct_ref, m_ref, w_ref, total_ref, f_ref, shift_ref = rest
    else:
        m_ref, w_ref = rest
    mine = [head_keys(own, length, h) for h in range(heads)]

    def tile(index):
        array, block, distance, _ = slots[index]
        row = block * (length + REACH_ROWS)
        products = []
        for g in range(heads // 2):
            rows = keys[array][row : row + length, LANES * g : LANES * g + LANES]
            for part in range(0, length, LANES):
                pair = [mine[h][part : part + LANES, :] for h in (2 * g, 2 * g + 1)]
                products.append((g, part, dot_nt(rows, jnp.concatenate(pair, axis=0))))
        for g, part, product in products:
            for h in (2 * g, 2 * g + 1):
                scores = product[:, LANES * (h % 2) : LANES * (h % 2) + LANES]
                if distance == 0:
                    scores = off_diagonal(scores, 0, part)
                top = jnp.max(scores, axis=0, keepdims=True)
                exponent = jnp.exp(scores - top)
                total = jnp.sum(exponent, axis=0, keepdims=True)
                lanes = slice(part, part + LANES)
                at = 2 * heads * index + h
                m_ref[at : at + 1, lanes] = top
                m_ref[at + heads : at + heads + 1, lanes] = total
                at = (index * heads + h) * length * (length // LANES) + part // LANES * length
                w_ref[at : at + length, :] = exponent.astype(BF16)

    allowed = allowed_slots(chips, reach_ref, slots, keys, length)
    for index, ok in enumerate(allowed):
        if ok is None:
            tile(index)
            continue
        at = 2 * heads * index
        m_ref[at : at + heads, :] = jnp.full((heads, length), NEGATIVE, F32)
        m_ref[at + heads : at + 2 * heads, :] = jnp.zeros((heads, length), F32)
        pl.when(ok)(partial(tile, index))

    if last:
        parts = []
        for ref, part in ((near_ref, NEAR), (direct_ref, DIRECT), (m_ref, PASSED)):
            parts += [(ref, 2 * heads * s) for s in range(len(part))]
        tops = [ref[at : at + heads, :] for ref, at in parts]
        top = tops[0]
        for other in tops[1:]:
            top = jnp.maximum(top, other)
        total = jnp.zeros((heads, length), F32)
        for index, (ref, at) in enumerate(parts):
            factor = jnp.exp(tops[index] - top)
            total = total + factor * ref[at + heads : at + 2 * heads, :]
            f_ref[2 * heads * index : 2 * heads * index + heads, :] = factor
        left = top + jnp.log(total)
        terms = []
        for _ in range(3):
            term = left.astype(BF16).astype(F32)
            terms.append(term)
            left = left - term
        terms.append(jnp.zeros((SHIFT_ROWS - 3 * heads, length), F32))
        shift_ref[...] = jnp.concatenate(terms, axis=0).astype(BF16)
        total_ref[...] = total


def attend_body(chips, slots, reach_ref, *refs):
    count = len({slot[0] for slot in slots})
    keys, values, rest = refs[:count], refs[count : 2 * count], refs[2 * count :]
    first, last = slots is NEAR, slots is PASSED
    before = {NEAR: 0, DIRECT: len(NEAR), PASSED: len(NEAR) + len(DIRECT)}[slots]
    if first:
        w_ref, f_ref, acc = rest
    elif last:
        w_ref, f_ref, total_ref, acc_in, keep_ref, send_ref, acc, rows_ref = rest
    else:
        w_ref, f_ref, acc_in, acc = rest
    length = acc.shape[1]
    heads = acc.shape[0] // HD
    if not first:
        acc[...] = acc_in[...]

    def tile(index):
        array, block, distance, _ = slots[index]
        for h in range(heads):
            at = (index * heads + h) * length * (length // LANES)
            starts = range(at, at + length * (length // LANES), length)
            weights = [w_ref[start : start + length, :] for start in starts]
            row = (block * heads + h) * HD
            numer = dot_nn(values[array][row : row + HD, :], jnp.concatenate(weights, axis=1))
            at = 2 * heads * (before + index) + h
            numer = numer * f_ref[at : at + 1, :]
            part = slice(HD * h, HD * h + HD)
            if distance == 0:
                acc[part, :] = numer
            else:
                acc[part, :] += numer

    for index, ok in enumerate(allowed_slots(chips, reach_ref, slots, keys, length)):
        if ok is None:
            tile(index)
        else:
            pl.when(ok)(partial(tile, index))

    if last:
        for h in range(heads):
            part = slice(HD * h, HD * h + HD)
            acc[part, :] = acc[part, :] / total_ref[h : h + 1, :]
        rows_ref[...] = jnp.transpose(acc[...])
        half = length // 2
        mine = lax.axis_index("head")
        keep_ref[...] = rows_ref[pl.ds(pl.multiple_of(mine * half, half), half), :].astype(BF16)
        other = pl.multiple_of((1 - mine) * half, half)
        send_ref[...] = rows_ref[pl.ds(other, half), :].astype(BF16)


def grad_tiles(chips, slots, reach_ref, own, keys, grads, shifts, acc):
    length = own.shape[0] - REACH_ROWS
    heads = own.shape[1] // HD
    lane = lax.broadcasted_iota(jnp.int32, (length, LANES), 1)
    low = lane < HD
    mine = []
    for h in range(heads):
        base = HD if h % 2 == 0 else 0
        term = lane - (base + h)
        one = jnp.logical_or(term == 0, jnp.logical_or(term == heads, term == 2 * heads))
        minus = jnp.where(one, -1.0, 0.0).astype(BF16)
        rows = own[0:length, LANES * (h // 2) : LANES * (h // 2) + LANES]
        mine.append(jnp.where(low if h % 2 == 0 else ~low, rows, minus))

    def tile(index):
        array, block, distance, _ = slots[index]
        row = block * (length + REACH_ROWS)
        ref, grow, srow = grads[array], block * heads * HD, block * SHIFT_ROWS
        terms = shifts[array][srow : srow + SHIFT_ROWS, :].astype(F32)
        rest = jnp.zeros((HD - SHIFT_ROWS, length), F32)
        terms = jnp.transpose(jnp.concatenate([terms, rest, terms, rest], axis=0)).astype(BF16)
        products = []
        for h in range(heads):
            g = h // 2
            far = keys[array][row : row + length, LANES * g : LANES * g + LANES]
            far = jnp.where(low if h % 2 == 0 else ~low, far, terms)
            products.append(dot_nt(far, mine[h]))
        weights = []
        for h in range(heads):
            scores = products[h]
            if distance == 0:
                scores = off_diagonal(scores, 0, 0)
            weights.append(jnp.exp(scores).astype(BF16))
        for h in range(heads):
            part = slice(HD * h, HD * h + HD)
            share = dot_nn(ref[grow + HD * h : grow + HD * h + HD, :], weights[h])
            if distance == 0:
                acc[part, :] = share
            else:
                acc[part, :] += share

    for index, ok in enumerate(allowed_slots(chips, reach_ref, slots, keys, length)):
        if ok is None:
            tile(index)
        else:
            pl.when(ok)(partial(tile, index))


def grad_body(chips, slots, reach_ref, own, *refs):
    keys, grads, shifts, rest = refs[0:2], refs[2:4], refs[4:6], refs[6:]
    acc = rest[-1]
    if slots is not NEAR:
        acc[...] = rest[0][...]
    grad_tiles(chips, slots, reach_ref, own, keys, grads, shifts, acc)


def final_body(chips, reach_ref, keep_ref, got_ref, near_ref, far_ref, *refs):
    own, acc_in, *refs = refs
    keys, grads, shifts, rest = refs[0:2], refs[2:4], refs[4:6], refs[6:]
    mixed_out, grad_out, acc, mixed, grad, sems = rest
    total = dot_nn(keep_ref[...], near_ref[...]) + dot_nn(got_ref[...], far_ref[...])
    mixed[...] = total.astype(BF16)
    first = pltpu.make_async_copy(mixed, mixed_out, sems.at[0])
    first.start()
    acc[...] = acc_in[...]
    grad_tiles(chips, PASSED, reach_ref, own, keys, grads, shifts, acc)
    grad[...] = jnp.transpose(acc[...]).astype(BF16)
    second = pltpu.make_async_copy(grad, grad_out, sems.at[1])
    second.start()
    first.wait()
    second.wait()


VMEM = pl.BlockSpec(memory_space=pltpu.VMEM)
SMEM = pl.BlockSpec(memory_space=pltpu.SMEM)
HBM = pl.BlockSpec(memory_space=pltpu.HBM)
PARAMS = pltpu.CompilerParams(vmem_limit_bytes=8 * 1024 * 1024)


def call(body, scalars, args, outs, scratch=()):
    args = [pltpu.with_memory_space_constraint(a, pltpu.VMEM) for a in args]
    run = pl.pallas_call(
        body,
        in_specs=[SMEM] * len(scalars) + [VMEM] * len(args),
        out_specs=[VMEM] * len(outs),
        out_shape=[pltpu.VMEM(shape, dtype) for shape, dtype in outs],
        compiler_params=PARAMS,
        scratch_shapes=[pltpu.VMEM(shape, dtype) for shape, dtype in scratch],
    )
    return list(run(*scalars, *args))


def joined(parts):
    rows, width = sum(part.shape[0] for part in parts), parts[0].shape[1]
    (both,) = call(join_body, [], parts, [((rows, width), BF16)])
    return both


def gathered(own):
    sib = sibling(own)
    return [own, sib], *rings(joined([own, sib]))


def rings(both):
    one, two = chip_ring(both, 1), chip_ring(both, 2)
    one, two = lax.optimization_barrier((one, two))
    return [one, two], [sibling(one), sibling(two)]


def compute(queries, values, scales, block_reach, out_weight, out_grad):
    length, width = queries.shape
    heads = scales.shape[1]
    chips = lax.axis_size("seq") // 2
    inputs = [queries, scales.T, values, out_grad]
    keys, turned, grads = pl.pallas_call(
        prepare_body,
        name="prepare",
        in_specs=[SMEM] + [HBM] * 4,
        out_specs=[VMEM] * 3,
        out_shape=[
            pltpu.VMEM((length + REACH_ROWS, width), BF16),
            pltpu.VMEM((width, length), BF16),
            pltpu.VMEM((width, length), BF16),
        ],
        compiler_params=PARAMS,
        scratch_shapes=[
            pltpu.VMEM((length, width), BF16),
            pltpu.VMEM((heads, length), F32),
            pltpu.VMEM((length, width), BF16),
            pltpu.VMEM((length, width), BF16),
            pltpu.SemaphoreType.DMA((4,)),
        ],
    )(block_reach, *(pltpu.with_memory_space_constraint(a, pltpu.HBM) for a in inputs))
    stages = (NEAR, DIRECT, PASSED)
    key_set = gathered(keys)
    value_set = gathered(turned)
    grad_set = gathered(grads)
    far_weight = other_head(out_weight)

    tops, weights = [], []
    for index, slots in enumerate(stages):
        last = slots is PASSED
        outs = [
            ((2 * heads * len(slots), length), F32),
            ((heads * len(slots) * length * length // LANES, LANES), BF16),
        ]
        if last:
            total = sum(len(part) for part in stages)
            outs += [((heads, length), F32), ((2 * heads * total, length), F32)]
            outs += [((SHIFT_ROWS, length), BF16)]
        args = [keys, *key_set[index], *(tops if last else [])]
        body = partial(stats_body, chips, slots)
        top, weight, *rest = call(body, [block_reach], args, outs)
        tops.append(top)
        weights.append(weight)
    totals, factors, shifts = rest
    shift_set = gathered(shifts)

    running = []
    for index, slots in enumerate(stages):
        args = [*key_set[index], *value_set[index], weights[index], factors]
        body = partial(attend_body, chips, slots)
        if slots is PASSED:
            args += [totals, *running]
            outs = [((length // 2, width), BF16)] * 2
            scratch = [((width, length), F32), ((length, width), F32)]
            keep, send = call(body, [block_reach], args, outs, scratch)
        else:
            running = call(body, [block_reach], args + running, [((width, length), F32)])
    got = other_head(send)

    running = []
    for index, slots in enumerate(stages[:2]):
        args = [keys, *key_set[index], *grad_set[index], *shift_set[index], *running]
        body = partial(grad_body, chips, slots)
        running = call(body, [block_reach], args, [((width, length), F32)])
    half, full = length // 2, out_weight.shape[1]
    inputs = [keep, got, out_weight, far_weight, keys, *running]
    inputs += [*key_set[2], *grad_set[2], *shift_set[2]]
    inputs = [pltpu.with_memory_space_constraint(a, pltpu.VMEM) for a in inputs]
    mixed, value_grad = pl.pallas_call(
        partial(final_body, chips),
        name="final",
        in_specs=[SMEM] + [VMEM] * len(inputs),
        out_specs=[HBM] * 2,
        out_shape=[
            jax.ShapeDtypeStruct((half, full), BF16),
            jax.ShapeDtypeStruct((length, width), BF16),
        ],
        compiler_params=PARAMS,
        scratch_shapes=[
            pltpu.VMEM((width, length), F32),
            pltpu.VMEM((half, full), BF16),
            pltpu.VMEM((length, width), BF16),
            pltpu.SemaphoreType.DMA((2,)),
        ],
    )(block_reach, *inputs)
    return (mixed, value_grad)


def solution(mesh):
    return jax.shard_map(
        compute,
        mesh=mesh,
        in_specs=(
            P("seq", "head"),
            P("seq", "head"),
            P("seq", "head"),
            P("seq"),
            P("head", None),
            P("seq", "head"),
        ),
        out_specs=(P(("seq", "head"), None), P("seq", "head")),
        check_vma=False,
    )
```

time: 47.4 us -> 47.2 us (level)
  waiting for transfers between devices: 19.5 us -> 18.3 us
  Pallas kernels: 10.4 us -> 11.3 us
    pallas_call x7 -> x13, Pallas kernels: 5.9 us -> 9.71 us  [the longest x12 8.07 us: call(): return list(run(*scalars, *args))]
    pallas_call x1, Pallas kernels: 4.45 us -> 1.61 us  [compute(): pl.pallas_call(partial(final_body, chips), name='final', in_specs=[SMEM]...]
    ppermute x12, waiting for transfers between devices: 4.2 us -> 3.04 us  [sibling(): return lax.ppermute(value, 'seq', [(i, i ^ 1) for i in range(count)])]
  transfers between devices with their start and end apart: 22 -> 22, of which waited for: 13 -> 11; matrix products, arithmetic and copies ran while one was open for 0% -> 0% of each run, Pallas kernels for 9% -> 17%
where the time goes in v3:
time: 47.2 us; the launch traced here: 47.1 us
  waiting for transfers between devices  18.3 us (39%)
  starting transfers between devices  16 us (34%)
  Pallas kernels  11.3 us (24%)
  between operations  1.41 us (3%)
    ppermute x8, waiting for transfers between devices, chip_ring(): return lax.ppermute(value, 'seq', pairs)  15.3 us
    pallas_call x12, Pallas kernels, call(): return list(run(*scalars, *args))  8.07 us
    ppermute x8, starting transfers between devices, chip_ring(): return lax.ppermute(value, 'seq', pairs)  7.82 us
    ppermute x12, starting transfers between devices, sibling(): return lax.ppermute(value, 'seq', [(i, i ^ 1) for i in range(count)])  5.7 us
    ppermute x12, waiting for transfers between devices, sibling(): return lax.ppermute(value, 'seq', [(i, i ^ 1) for i in range(count)])  3.04 us
    ppermute x2, starting transfers between devices, other_head(): return lax.ppermute(value, 'head', [(0, 1), (1, 0)])  2.48 us
    pallas_call x1, Pallas kernels, compute(): pl.pallas_call(prepare_body, name='prepare', in_specs=[SMEM] + [HBM] * 4,...  1.64 us
    pallas_call x1, Pallas kernels, compute(): pl.pallas_call(partial(final_body, chips), name='final', in_specs=[SMEM]...  1.61 us
  transfers between devices with their start and end apart: 22, of which 11 were waited for; matrix products, arithmetic and copies ran while one was open for 0% of the time, Pallas kernels for 17%

profile of v3, /device:TPU:17, one launch (start us, length us, event | category | flops | bytes accessed | tf_op | source)
XLA Modules:
  0.0 47.1 jit_solution(7122673062964769778)
XLA Ops:
  1.3 1.6 %prepare.1 = (bf16[272,256]{1,0:T(8,128)(2,1)S(1)}, bf16[256,256]{1,0:T(8,128)(2,1)S(1)}, bf16[256,256]{1,0:T(8,128)(2,1)S(1)}) custom-call(s32[1]{0:T(128)S(6)} %copy.8.reach_ref, bf16[256,256]{1,0:T(8,128)(2,1)} %q_in.1, f32[4,256]{1,0:T(4,128)} %bitcast.1, bf16[256,256]{1,0:T(8,128)(2,1)} %v_in.1, bf16[256,256]{1,0:T(8,128)(2,1)} %g_in.1), custom_call_target="tpu_custom_call" | custom-call | tf_op jit(solution)/shard_map/prepare/pallas_call | solution.py:356
  2.9 0.7 %collective-permute-start = (bf16[272,256]{1,0:T(8,128)(2,1)S(1)}, bf16[272,256]{1,0:T(8,128)(2,1)S(1)}, u32[]{:S(2)}, u32[]{:S(2)}) collective-permute-start(bf16[272,256]{1,0:T(8,128)(2,1)S(1)} %get-tuple-element.23.refs_0_.own), channel_id=1, source_target_pairs={{0,2},{2,0},{4,6},{6,4},{8,10},{10,8},{12,14},{14,12},{16,18},{18,... | collective-permute-start | bytes 417800 | tf_op jit(solution)/shard_map/ppermute | solution.py:22
  3.7 0.1 collective-permute-start.5
  3.7 0.9 %collective-permute-done.refs_1_ = bf16[272,256]{1,0:T(8,128)(2,1)S(1)} collective-permute-done((bf16[272,256]{1,0:T(8,128)(2,1)S(1)}, bf16[272,256]{1,0:T(8,128)(2,1)S(1)}, u32[]{:S(2)}, u32[]{:S(2)}) %collective-permute-start) | collective-permute-done | bytes 139296 | tf_op jit(solution)/shard_map/ppermute | solution.py:22
  4.7 1.2 %collective-permute-start.1 = (bf16[544,256]{1,0:T(8,128)(2,1)S(1)}, bf16[544,256]{1,0:T(8,128)(2,1)S(1)}, u32[]{:S(2)}, u32[]{:S(2)}) collective-permute-start(bf16[544,256]{1,0:T(8,128)(2,1)S(1)} %shard_map.77), channel_id=1, source_target_pairs={{0,4},{2,0},{4,8},{6,2},{8,12},{10,6},{12,16},{14,10},{16,20},{18,... | collective-permute-start | bytes 835592 | tf_op jit(solution)/shard_map/ppermute | solution.py:32
  5.9 0.2 collective-permute-start.2
  6.0 0.0 collective-permute-done.5.refs_1_.refs_3_
  6.1 0.2 collective-permute-start.6
  6.2 1.8 %collective-permute-start.7 = (bf16[512,256]{1,0:T(8,128)(2,1)S(1)}, bf16[512,256]{1,0:T(8,128)(2,1)S(1)}, u32[]{:S(2)}, u32[]{:S(2)}) collective-permute-start(bf16[512,256]{1,0:T(8,128)(2,1)S(1)} %shard_map.78), channel_id=1, source_target_pairs={{0,8},{2,0},{4,12},{6,4},{8,16},{10,2},{12,20},{14,6},{16,24},{18,... | collective-permute-start | bytes 786440 | tf_op jit(solution)/shard_map/ppermute | solution.py:32
  8.0 0.7 %collective-permute-start.12 = (bf16[256,256]{1,0:T(8,128)(2,1)S(1)}, bf16[256,256]{1,0:T(8,128)(2,1)S(1)}, u32[]{:S(2)}, u32[]{:S(2)}) collective-permute-start(bf16[256,256]{1,0:T(8,128)(2,1)S(1)} %get-tuple-element.38.refs_0_.refs_2_), channel_id=1, source_target_pairs={{0,2},{2,0},{4,6},{6,4},{8,10},{10,8},{12,14},{14,12},{16,18},{18,... | collective-permute-start | bytes 393224 | tf_op jit(solution)/shard_map/ppermute | solution.py:22
  8.7 1.0 %collective-permute-done.12.refs_1_.refs_3_ = bf16[256,256]{1,0:T(8,128)(2,1)S(1)} collective-permute-done((bf16[256,256]{1,0:T(8,128)(2,1)S(1)}, bf16[256,256]{1,0:T(8,128)(2,1)S(1)}, u32[]{:S(2)}, u32[]{:S(2)}) %collective-permute-start.12) | collective-permute-done | bytes 131104 | tf_op jit(solution)/shard_map/ppermute | solution.py:22
  9.7 2.3 %collective-permute-start.13 = (bf16[512,256]{1,0:T(8,128)(2,1)S(1)}, bf16[512,256]{1,0:T(8,128)(2,1)S(1)}, u32[]{:S(2)}, u32[]{:S(2)}) collective-permute-start(bf16[512,256]{1,0:T(8,128)(2,1)S(1)} %shard_map.85), channel_id=1, source_target_pairs={{0,4},{2,0},{4,8},{6,2},{8,12},{10,6},{12,16},{14,10},{16,20},{18,... | collective-permute-start | bytes 786440 | tf_op jit(solution)/shard_map/ppermute | solution.py:32
  12.0 1.4 %collective-permute-done.1.refs_0_ = bf16[544,256]{1,0:T(8,128)(2,1)S(1)} collective-permute-done((bf16[544,256]{1,0:T(8,128)(2,1)S(1)}, bf16[544,256]{1,0:T(8,128)(2,1)S(1)}, u32[]{:S(2)}, u32[]{:S(2)}) %collective-permute-start.1) | collective-permute-done | bytes 278560 | tf_op jit(solution)/shard_map/ppermute | solution.py:32
  13.4 0.3 collective-permute-start.14
  13.7 0.7 %collective-permute-done.2.refs_1_ = bf16[544,256]{1,0:T(8,128)(2,1)S(1)} collective-permute-done((bf16[544,256]{1,0:T(8,128)(2,1)S(1)}, bf16[544,256]{1,0:T(8,128)(2,1)S(1)}, u32[]{:S(2)}, u32[]{:S(2)}) %collective-permute-start.2) | collective-permute-done | bytes 278560 | tf_op jit(solution)/shard_map/ppermute | solution.py:32
  14.4 0.0 collective-permute-start.3
  14.4 4.6 %collective-permute-done.6.refs_2_ = bf16[512,256]{1,0:T(8,128)(2,1)S(1)} collective-permute-done((bf16[512,256]{1,0:T(8,128)(2,1)S(1)}, bf16[512,256]{1,0:T(8,128)(2,1)S(1)}, u32[]{:S(2)}, u32[]{:S(2)}) %collective-permute-start.6) | collective-permute-done | bytes 262176 | tf_op jit(solution)/shard_map/ppermute | solution.py:32
  19.0 0.3 collective-permute-start.4
  19.3 0.5 %collective-permute-done.7.refs_3_ = bf16[512,256]{1,0:T(8,128)(2,1)S(1)} collective-permute-done((bf16[512,256]{1,0:T(8,128)(2,1)S(1)}, bf16[512,256]{1,0:T(8,128)(2,1)S(1)}, u32[]{:S(2)}, u32[]{:S(2)}) %collective-permute-start.7) | collective-permute-done | bytes 262176 | tf_op jit(solution)/shard_map/ppermute | solution.py:32
  19.8 1.2 %collective-permute-start.11 = (bf16[256,1024]{1,0:T(8,128)(2,1)}, bf16[256,1024]{1,0:T(8,128)(2,1)S(1)}, u32[]{:S(2)}, u32[]{:S(2)}) collective-permute-start(bf16[256,1024]{1,0:T(8,128)(2,1)} %near_ref.1), channel_id=1, source_target_pairs={{0,1},{1,0},{2,3},{3,2},{4,5},{5,4},{6,7},{7,6},{8,9},{9,8},{10,11... | collective-permute-start | bytes 1572872 | tf_op jit(solution)/shard_map/ppermute | solution.py:36
  21.0 3.7 %collective-permute-done.13.refs_2_ = bf16[512,256]{1,0:T(8,128)(2,1)S(1)} collective-permute-done((bf16[512,256]{1,0:T(8,128)(2,1)S(1)}, bf16[512,256]{1,0:T(8,128)(2,1)S(1)}, u32[]{:S(2)}, u32[]{:S(2)}) %collective-permute-start.13) | collective-permute-done | bytes 262176 | tf_op jit(solution)/shard_map/ppermute | solution.py:32
  24.7 0.3 collective-permute-start.8
  24.9 0.8 %collective-permute-done.14.refs_3_ = bf16[512,256]{1,0:T(8,128)(2,1)S(1)} collective-permute-done((bf16[512,256]{1,0:T(8,128)(2,1)S(1)}, bf16[512,256]{1,0:T(8,128)(2,1)S(1)}, u32[]{:S(2)}, u32[]{:S(2)}) %collective-permute-start.14) | collective-permute-done | bytes 262176 | tf_op jit(solution)/shard_map/ppermute | solution.py:32
  25.7 0.0 collective-permute-start.9
  25.8 0.0 collective-permute-done.3.refs_0_.refs_2_
  25.8 0.5 %collective-permute-start.18 = (bf16[512,256]{1,0:T(8,128)(2,1)S(1)}, bf16[512,256]{1,0:T(8,128)(2,1)S(1)}, u32[]{:S(2)}, u32[]{:S(2)}) collective-permute-start(bf16[512,256]{1,0:T(8,128)(2,1)S(1)} %collective-permute-done.13.refs_2_), channel_id=1, source_target_pairs={{0,2},{2,0},{4,6},{6,4},{8,10},{10,8},{12,14},{14,12},{16,18},{18,... | collective-permute-start | bytes 786440 | tf_op jit(solution)/shard_map/ppermute | solution.py:22
  26.3 0.0 collective-permute-done.4.refs_1_.refs_3_
  26.3 0.1 collective-permute-start.19
  26.3 1.0 %shard_map.79 = (f32[16,256]{1,0:T(8,128)S(1)}, bf16[4096,128]{1,0:T(8,128)(2,1)S(1)}) custom-call(s32[1]{0:T(128)S(6)} %copy.8.reach_ref, bf16[272,256]{1,0:T(8,128)(2,1)S(1)} %get-tuple-element.23.refs_0_.own, bf16[272,256]{1,0:T(8,128)(2,1)S(1)} %get-tuple-element.23.refs_0_.own, bf16[272,256]{1,0:T(8,128)(2,1)S(1)} %collective-permute-done.refs_1_), custom_call_target="tpu_custom_call" | custom-call | tf_op jit(solution)/shard_map/pallas_call | solution.py:331
  27.3 1.5 %shard_map.80 = (f32[32,256]{1,0:T(8,128)S(1)}, bf16[8192,128]{1,0:T(8,128)(2,1)S(1)}) custom-call(s32[1]{0:T(128)S(6)} %copy.8.reach_ref, bf16[272,256]{1,0:T(8,128)(2,1)S(1)} %get-tuple-element.23.refs_0_.own, bf16[544,256]{1,0:T(8,128)(2,1)S(1)} %collective-permute-done.1.refs_0_, bf16[544,256]{1,0:T(8,128)(2,1)S(1)} %collective-permute-done.2.refs_1_), custom_call_target="tpu_custom_call" | custom-call | tf_op jit(solution)/shard_map/pallas_call | solution.py:331
  28.8 1.2 %shard_map.81 = (f32[24,256]{1,0:T(8,128)}, bf16[6144,128]{1,0:T(8,128)(2,1)S(1)}, f32[4,256]{1,0:T(4,128)S(1)}, f32[72,256]{1,0:T(8,128)S(1)}, bf16[16,256]{1,0:T(8,128)(2,1)S(1)}) custom-call(s32[1]{0:T(128)S(6)} %copy.8.reach_ref, bf16[272,256]{1,0:T(8,128)(2,1)S(1)} %get-tuple-element.23.refs_0_.own, ...), custom_call_target="tpu_custom_call" | custom-call | tf_op jit(solution)/shard_map/pallas_call | solution.py:331
  30.0 0.4 shard_map.82.refs_6_
  30.4 0.8 %shard_map.83.refs_7_ = f32[256,256]{1,0:T(8,128)S(1)} custom-call(s32[1]{0:T(128)S(6)} %copy.8.reach_ref, bf16[544,256]{1,0:T(8,128)(2,1)S(1)} %collective-permute-done.1.refs_0_, bf16[544,256]{1,0:T(8,128)(2,1)S(1)} %collective-permute-done.2.refs_1_, bf16[512,256]{1,0:T(8,128)(2,1)S(1)} %collective-permute-done.6.refs_2_, ...), custom_call_target="tpu_custom_call" | custom-call | tf_op jit(solution)/shard_map/pallas_call | solution.py:331
  31.2 0.0 collective-permute-done.8.refs_2_
  31.2 0.0 collective-permute-done.9.refs_3_
  31.2 0.5 %shard_map.84 = (bf16[128,256]{1,0:T(8,128)(2,1)S(1)}, bf16[128,256]{1,0:T(8,128)(2,1)S(1)}) custom-call(s32[1]{0:T(128)S(6)} %copy.8.reach_ref, bf16[544,256]{1,0:T(8,128)(2,1)S(1)} %collective-permute-done.3.refs_0_.refs_2_, bf16[544,256]{1,0:T(8,128)(2,1)S(1)} %collective-permute-done.4.refs_1_.refs_3_, ...), custom_call_target="tpu_custom_call" | custom-call | tf_op jit(solution)/shard_map/pallas_call | solution.py:331
  31.7 0.0 copy-start
  31.8 1.3 %collective-permute-start.10 = (bf16[128,256]{1,0:T(8,128)(2,1)S(1)}, bf16[128,256]{1,0:T(8,128)(2,1)S(1)}, u32[]{:S(2)}, u32[]{:S(2)}) collective-permute-start(bf16[128,256]{1,0:T(8,128)(2,1)S(1)} %get-tuple-element.37), channel_id=1, source_target_pairs={{0,1},{1,0},{2,3},{3,2},{4,5},{5,4},{6,7},{7,6},{8,9},{9,8},{10,11... | collective-permute-start | bytes 196616 | tf_op jit(solution)/shard_map/ppermute | solution.py:36
  33.0 0.1 collective-permute-start.15
  33.1 1.1 %collective-permute-done.15.refs_1_.refs_5_ = bf16[16,256]{1,0:T(8,128)(2,1)S(1)} collective-permute-done((bf16[16,256]{1,0:T(8,128)(2,1)S(1)}, bf16[16,256]{1,0:T(8,128)(2,1)S(1)}, u32[]{:S(2)}, u32[]{:S(2)}) %collective-permute-start.15) | collective-permute-done | bytes 8224 | tf_op jit(solution)/shard_map/ppermute | solution.py:22
  34.2 1.6 %collective-permute-start.16 = (bf16[32,256]{1,0:T(8,128)(2,1)S(1)}, bf16[32,256]{1,0:T(8,128)(2,1)S(1)}, u32[]{:S(2)}, u32[]{:S(2)}) collective-permute-start(bf16[32,256]{1,0:T(8,128)(2,1)S(1)} %shard_map.86), channel_id=1, source_target_pairs={{0,4},{2,0},{4,8},{6,2},{8,12},{10,6},{12,16},{14,10},{16,20},{18,... | collective-permute-start | bytes 49160 | tf_op jit(solution)/shard_map/ppermute | solution.py:32
  35.8 1.3 %collective-permute-done.16.refs_4_ = bf16[32,256]{1,0:T(8,128)(2,1)S(1)} collective-permute-done((bf16[32,256]{1,0:T(8,128)(2,1)S(1)}, bf16[32,256]{1,0:T(8,128)(2,1)S(1)}, u32[]{:S(2)}, u32[]{:S(2)}) %collective-permute-start.16) | collective-permute-done | bytes 16416 | tf_op jit(solution)/shard_map/ppermute | solution.py:32
  37.1 0.2 collective-permute-start.17
  37.3 2.3 %collective-permute-done.17.refs_5_ = bf16[32,256]{1,0:T(8,128)(2,1)S(1)} collective-permute-done((bf16[32,256]{1,0:T(8,128)(2,1)S(1)}, bf16[32,256]{1,0:T(8,128)(2,1)S(1)}, u32[]{:S(2)}, u32[]{:S(2)}) %collective-permute-start.17) | collective-permute-done | bytes 16416 | tf_op jit(solution)/shard_map/ppermute | solution.py:32
  39.7 3.1 %collective-permute-start.20 = (bf16[32,256]{1,0:T(8,128)(2,1)S(1)}, bf16[32,256]{1,0:T(8,128)(2,1)S(1)}, u32[]{:S(2)}, u32[]{:S(2)}) collective-permute-start(bf16[32,256]{1,0:T(8,128)(2,1)S(1)} %collective-permute-done.16.refs_4_), channel_id=1, source_target_pairs={{0,2},{2,0},{4,6},{6,4},{8,10},{10,8},{12,14},{14,12},{16,18},{18,... | collective-permute-start | bytes 49160 | tf_op jit(solution)/shard_map/ppermute | solution.py:22
  42.7 0.0 collective-permute-done.11.far_ref
  42.7 0.0 collective-permute-start.21
  42.8 1.0 %shard_map.87.refs_6_ = f32[256,256]{1,0:T(8,128)S(1)} custom-call(s32[1]{0:T(128)S(6)} %copy.8.reach_ref, bf16[272,256]{1,0:T(8,128)(2,1)S(1)} %get-tuple-element.23.refs_0_.own, bf16[272,256]{1,0:T(8,128)(2,1)S(1)} %get-tuple-element.23.refs_0_.own, bf16[272,256]{1,0:T(8,128)(2,1)S(1)} %collective-permute-done.refs_1_, ...), custom_call_target="tpu_custom_call" | custom-call | tf_op jit(solution)/shard_map/pallas_call | solution.py:331
  43.8 1.6 %shard_map.88.refs_1_ = f32[256,256]{1,0:T(8,128)S(1)} custom-call(s32[1]{0:T(128)S(6)} %copy.8.reach_ref, bf16[272,256]{1,0:T(8,128)(2,1)S(1)} %get-tuple-element.23.refs_0_.own, bf16[544,256]{1,0:T(8,128)(2,1)S(1)} %collective-permute-done.1.refs_0_, bf16[544,256]{1,0:T(8,128)(2,1)S(1)} %collective-permute-done.2.refs_1_, ...), custom_call_target="tpu_custom_call" | custom-call | tf_op jit(solution)/shard_map/pallas_call | solution.py:331
  45.4 0.0 collective-permute-done.18.refs_4_
  45.4 0.0 collective-permute-done.19.refs_5_
  45.4 0.0 collective-permute-done.20.refs_6_
  45.4 0.0 collective-permute-done.21.refs_7_
  45.4 0.0 collective-permute-done.10.got_ref
  45.5 0.0 copy-done
  45.5 1.6 %final.1 = (bf16[128,1024]{1,0:T(8,128)(2,1)}, bf16[256,256]{1,0:T(8,128)(2,1)}) custom-call(s32[1]{0:T(128)S(6)} %copy.8.reach_ref, bf16[128,256]{1,0:T(8,128)(2,1)S(1)} %get-tuple-element.36.keep_ref, bf16[128,256]{1,0:T(8,128)(2,1)S(1)} %collective-permute-done.10.got_ref, bf16[256,1024]{1,0:T(8,128)(2,1)S(1)} %copy-done, ...), custom_call_target="tpu_custom_call" | custom-call | tf_op jit(solution)/shard_map/final/pallas_call | solution.py:422
  (4 shorter events, 0.1 us)
Async XLA Ops:
  2.9 1.7 %collective-permute-start = (bf16[272,256]{1,0:T(8,128)(2,1)S(1)}, bf16[272,256]{1,0:T(8,128)(2,1)S(1)}, u32[]{:S(2)}, u32[]{:S(2)}) collective-permute-start(bf16[272,256]{1,0:T(8,128)(2,1)S(1)} %get-tuple-element.23.refs_0_.own), channel_id=1, source_target_pairs={{0,2},{2,0},{4,6},{6,4},{8,10},{10,8},{12,14},{14,12},{16,18},{18,... | collective-permute-start | bytes 417800 | tf_op jit(solution)/shard_map/ppermute | solution.py:22
  3.7 2.4 %collective-permute-start.5 = (bf16[256,256]{1,0:T(8,128)(2,1)S(1)}, bf16[256,256]{1,0:T(8,128)(2,1)S(1)}, u32[]{:S(2)}, u32[]{:S(2)}) collective-permute-start(bf16[256,256]{1,0:T(8,128)(2,1)S(1)} %get-tuple-element.26.refs_0_.refs_2_), channel_id=1, source_target_pairs={{0,2},{2,0},{4,6},{6,4},{8,10},{10,8},{12,14},{14,12},{16,18},{18,... | collective-permute-start | bytes 393224 | tf_op jit(solution)/shard_map/ppermute | solution.py:22
  4.7 8.7 %collective-permute-start.1 = (bf16[544,256]{1,0:T(8,128)(2,1)S(1)}, bf16[544,256]{1,0:T(8,128)(2,1)S(1)}, u32[]{:S(2)}, u32[]{:S(2)}) collective-permute-start(bf16[544,256]{1,0:T(8,128)(2,1)S(1)} %shard_map.77), channel_id=1, source_target_pairs={{0,4},{2,0},{4,8},{6,2},{8,12},{10,6},{12,16},{14,10},{16,20},{18,... | collective-permute-start | bytes 835592 | tf_op jit(solution)/shard_map/ppermute | solution.py:32
  5.9 8.6 %collective-permute-start.2 = (bf16[544,256]{1,0:T(8,128)(2,1)S(1)}, bf16[544,256]{1,0:T(8,128)(2,1)S(1)}, u32[]{:S(2)}, u32[]{:S(2)}) collective-permute-start(bf16[544,256]{1,0:T(8,128)(2,1)S(1)} %shard_map.77), channel_id=1, source_target_pairs={{0,8},{2,0},{4,12},{6,4},{8,16},{10,2},{12,20},{14,6},{16,24},{18,... | collective-permute-start | bytes 835592 | tf_op jit(solution)/shard_map/ppermute | solution.py:32
  6.1 13.0 %collective-permute-start.6 = (bf16[512,256]{1,0:T(8,128)(2,1)S(1)}, bf16[512,256]{1,0:T(8,128)(2,1)S(1)}, u32[]{:S(2)}, u32[]{:S(2)}) collective-permute-start(bf16[512,256]{1,0:T(8,128)(2,1)S(1)} %shard_map.78), channel_id=1, source_target_pairs={{0,4},{2,0},{4,8},{6,2},{8,12},{10,6},{12,16},{14,10},{16,20},{18,... | collective-permute-start | bytes 786440 | tf_op jit(solution)/shard_map/ppermute | solution.py:32
  6.2 13.6 %collective-permute-start.7 = (bf16[512,256]{1,0:T(8,128)(2,1)S(1)}, bf16[512,256]{1,0:T(8,128)(2,1)S(1)}, u32[]{:S(2)}, u32[]{:S(2)}) collective-permute-start(bf16[512,256]{1,0:T(8,128)(2,1)S(1)} %shard_map.78), channel_id=1, source_target_pairs={{0,8},{2,0},{4,12},{6,4},{8,16},{10,2},{12,20},{14,6},{16,24},{18,... | collective-permute-start | bytes 786440 | tf_op jit(solution)/shard_map/ppermute | solution.py:32
  8.0 1.6 %collective-permute-start.12 = (bf16[256,256]{1,0:T(8,128)(2,1)S(1)}, bf16[256,256]{1,0:T(8,128)(2,1)S(1)}, u32[]{:S(2)}, u32[]{:S(2)}) collective-permute-start(bf16[256,256]{1,0:T(8,128)(2,1)S(1)} %get-tuple-element.38.refs_0_.refs_2_), channel_id=1, source_target_pairs={{0,2},{2,0},{4,6},{6,4},{8,10},{10,8},{12,14},{14,12},{16,18},{18,... | collective-permute-start | bytes 393224 | tf_op jit(solution)/shard_map/ppermute | solution.py:22
  9.7 15.0 %collective-permute-start.13 = (bf16[512,256]{1,0:T(8,128)(2,1)S(1)}, bf16[512,256]{1,0:T(8,128)(2,1)S(1)}, u32[]{:S(2)}, u32[]{:S(2)}) collective-permute-start(bf16[512,256]{1,0:T(8,128)(2,1)S(1)} %shard_map.85), channel_id=1, source_target_pairs={{0,4},{2,0},{4,8},{6,2},{8,12},{10,6},{12,16},{14,10},{16,20},{18,... | collective-permute-start | bytes 786440 | tf_op jit(solution)/shard_map/ppermute | solution.py:32
  13.4 12.3 %collective-permute-start.14 = (bf16[512,256]{1,0:T(8,128)(2,1)S(1)}, bf16[512,256]{1,0:T(8,128)(2,1)S(1)}, u32[]{:S(2)}, u32[]{:S(2)}) collective-permute-start(bf16[512,256]{1,0:T(8,128)(2,1)S(1)} %shard_map.85), channel_id=1, source_target_pairs={{0,8},{2,0},{4,12},{6,4},{8,16},{10,2},{12,20},{14,6},{16,24},{18,... | collective-permute-start | bytes 786440 | tf_op jit(solution)/shard_map/ppermute | solution.py:32
  14.4 11.3 %collective-permute-start.3 = (bf16[544,256]{1,0:T(8,128)(2,1)S(1)}, bf16[544,256]{1,0:T(8,128)(2,1)S(1)}, u32[]{:S(2)}, u32[]{:S(2)}) collective-permute-start(bf16[544,256]{1,0:T(8,128)(2,1)S(1)} %collective-permute-done.1.refs_0_), channel_id=1, source_target_pairs={{0,2},{2,0},{4,6},{6,4},{8,10},{10,8},{12,14},{14,12},{16,18},{18,... | collective-permute-start | bytes 835592 | tf_op jit(solution)/shard_map/ppermute | solution.py:22
  19.0 7.2 %collective-permute-start.4 = (bf16[544,256]{1,0:T(8,128)(2,1)S(1)}, bf16[544,256]{1,0:T(8,128)(2,1)S(1)}, u32[]{:S(2)}, u32[]{:S(2)}) collective-permute-start(bf16[544,256]{1,0:T(8,128)(2,1)S(1)} %collective-permute-done.2.refs_1_), channel_id=1, source_target_pairs={{0,2},{2,0},{4,6},{6,4},{8,10},{10,8},{12,14},{14,12},{16,18},{18,... | collective-permute-start | bytes 835592 | tf_op jit(solution)/shard_map/ppermute | solution.py:22
  19.8 23.0 %collective-permute-start.11 = (bf16[256,1024]{1,0:T(8,128)(2,1)}, bf16[256,1024]{1,0:T(8,128)(2,1)S(1)}, u32[]{:S(2)}, u32[]{:S(2)}) collective-permute-start(bf16[256,1024]{1,0:T(8,128)(2,1)} %near_ref.1), channel_id=1, source_target_pairs={{0,1},{1,0},{2,3},{3,2},{4,5},{5,4},{6,7},{7,6},{8,9},{9,8},{10,11... | collective-permute-start | bytes 1572872 | tf_op jit(solution)/shard_map/ppermute | solution.py:36
  24.7 6.5 %collective-permute-start.8 = (bf16[512,256]{1,0:T(8,128)(2,1)S(1)}, bf16[512,256]{1,0:T(8,128)(2,1)S(1)}, u32[]{:S(2)}, u32[]{:S(2)}) collective-permute-start(bf16[512,256]{1,0:T(8,128)(2,1)S(1)} %collective-permute-done.6.refs_2_), channel_id=1, source_target_pairs={{0,2},{2,0},{4,6},{6,4},{8,10},{10,8},{12,14},{14,12},{16,18},{18,... | collective-permute-start | bytes 786440 | tf_op jit(solution)/shard_map/ppermute | solution.py:22
  25.7 5.5 %collective-permute-start.9 = (bf16[512,256]{1,0:T(8,128)(2,1)S(1)}, bf16[512,256]{1,0:T(8,128)(2,1)S(1)}, u32[]{:S(2)}, u32[]{:S(2)}) collective-permute-start(bf16[512,256]{1,0:T(8,128)(2,1)S(1)} %collective-permute-done.7.refs_3_), channel_id=1, source_target_pairs={{0,2},{2,0},{4,6},{6,4},{8,10},{10,8},{12,14},{14,12},{16,18},{18,... | collective-permute-start | bytes 786440 | tf_op jit(solution)/shard_map/ppermute | solution.py:22
  25.8 19.7 %collective-permute-start.18 = (bf16[512,256]{1,0:T(8,128)(2,1)S(1)}, bf16[512,256]{1,0:T(8,128)(2,1)S(1)}, u32[]{:S(2)}, u32[]{:S(2)}) collective-permute-start(bf16[512,256]{1,0:T(8,128)(2,1)S(1)} %collective-permute-done.13.refs_2_), channel_id=1, source_target_pairs={{0,2},{2,0},{4,6},{6,4},{8,10},{10,8},{12,14},{14,12},{16,18},{18,... | collective-permute-start | bytes 786440 | tf_op jit(solution)/shard_map/ppermute | solution.py:22
  26.3 19.2 %collective-permute-start.19 = (bf16[512,256]{1,0:T(8,128)(2,1)S(1)}, bf16[512,256]{1,0:T(8,128)(2,1)S(1)}, u32[]{:S(2)}, u32[]{:S(2)}) collective-permute-start(bf16[512,256]{1,0:T(8,128)(2,1)S(1)} %collective-permute-done.14.refs_3_), channel_id=1, source_target_pairs={{0,2},{2,0},{4,6},{6,4},{8,10},{10,8},{12,14},{14,12},{16,18},{18,... | collective-permute-start | bytes 786440 | tf_op jit(solution)/shard_map/ppermute | solution.py:22
  31.7 13.7 %copy-start = (bf16[256,1024]{1,0:T(8,128)(2,1)S(1)}, bf16[256,1024]{1,0:T(8,128)(2,1)}, u32[]{:S(2)}) copy-start(bf16[256,1024]{1,0:T(8,128)(2,1)} %near_ref.1) | copy-start | bytes 1572868
  31.8 13.7 %collective-permute-start.10 = (bf16[128,256]{1,0:T(8,128)(2,1)S(1)}, bf16[128,256]{1,0:T(8,128)(2,1)S(1)}, u32[]{:S(2)}, u32[]{:S(2)}) collective-permute-start(bf16[128,256]{1,0:T(8,128)(2,1)S(1)} %get-tuple-element.37), channel_id=1, source_target_pairs={{0,1},{1,0},{2,3},{3,2},{4,5},{5,4},{6,7},{7,6},{8,9},{9,8},{10,11... | collective-permute-start | bytes 196616 | tf_op jit(solution)/shard_map/ppermute | solution.py:36
  33.0 1.2 %collective-permute-start.15 = (bf16[16,256]{1,0:T(8,128)(2,1)S(1)}, bf16[16,256]{1,0:T(8,128)(2,1)S(1)}, u32[]{:S(2)}, u32[]{:S(2)}) collective-permute-start(bf16[16,256]{1,0:T(8,128)(2,1)S(1)} %get-tuple-element.41.refs_0_.refs_4_), channel_id=1, source_target_pairs={{0,2},{2,0},{4,6},{6,4},{8,10},{10,8},{12,14},{14,12},{16,18},{18,... | collective-permute-start | bytes 24584 | tf_op jit(solution)/shard_map/ppermute | solution.py:22
  34.2 2.9 %collective-permute-start.16 = (bf16[32,256]{1,0:T(8,128)(2,1)S(1)}, bf16[32,256]{1,0:T(8,128)(2,1)S(1)}, u32[]{:S(2)}, u32[]{:S(2)}) collective-permute-start(bf16[32,256]{1,0:T(8,128)(2,1)S(1)} %shard_map.86), channel_id=1, source_target_pairs={{0,4},{2,0},{4,8},{6,2},{8,12},{10,6},{12,16},{14,10},{16,20},{18,... | collective-permute-start | bytes 49160 | tf_op jit(solution)/shard_map/ppermute | solution.py:32
  37.1 2.6 %collective-permute-start.17 = (bf16[32,256]{1,0:T(8,128)(2,1)S(1)}, bf16[32,256]{1,0:T(8,128)(2,1)S(1)}, u32[]{:S(2)}, u32[]{:S(2)}) collective-permute-start(bf16[32,256]{1,0:T(8,128)(2,1)S(1)} %shard_map.86), channel_id=1, source_target_pairs={{0,8},{2,0},{4,12},{6,4},{8,16},{10,2},{12,20},{14,6},{16,24},{18,... | collective-permute-start | bytes 49160 | tf_op jit(solution)/shard_map/ppermute | solution.py:32
  39.7 5.7 %collective-permute-start.20 = (bf16[32,256]{1,0:T(8,128)(2,1)S(1)}, bf16[32,256]{1,0:T(8,128)(2,1)S(1)}, u32[]{:S(2)}, u32[]{:S(2)}) collective-permute-start(bf16[32,256]{1,0:T(8,128)(2,1)S(1)} %collective-permute-done.16.refs_4_), channel_id=1, source_target_pairs={{0,2},{2,0},{4,6},{6,4},{8,10},{10,8},{12,14},{14,12},{16,18},{18,... | collective-permute-start | bytes 49160 | tf_op jit(solution)/shard_map/ppermute | solution.py:22
  42.7 2.7 %collective-permute-start.21 = (bf16[32,256]{1,0:T(8,128)(2,1)S(1)}, bf16[32,256]{1,0:T(8,128)(2,1)S(1)}, u32[]{:S(2)}, u32[]{:S(2)}) collective-permute-start(bf16[32,256]{1,0:T(8,128)(2,1)S(1)} %collective-permute-done.17.refs_5_), channel_id=1, source_target_pairs={{0,2},{2,0},{4,6},{6,4},{8,10},{10,8},{12,14},{14,12},{16,18},{18,... | collective-permute-start | bytes 49160 | tf_op jit(solution)/shard_map/ppermute | solution.py:22

commit v4 on v3

v4 whole, which is shorter than its diff:
```python
from functools import partial

import jax
import jax.numpy as jnp
from jax import lax
from jax.experimental import pallas as pl
from jax.experimental.pallas import tpu as pltpu
from jax.sharding import PartitionSpec as P


HD = 64
NEGATIVE = -1e30
REACH_ROWS = 16
SHIFT_ROWS = 16
LANES = 128
F32 = jnp.float32
BF16 = jnp.bfloat16


def sibling(value):
    count = lax.axis_size("seq")
    return lax.ppermute(value, "seq", [(i, i ^ 1) for i in range(count)])


def chip_ring(value, step):
    chips = lax.axis_size("seq") // 2
    pairs = []
    for chip in range(chips):
        up, down = chip + step, chip - step
        pairs.append((2 * chip, 2 * up if up < chips else 2 * chip + 1))
        pairs.append((2 * chip + 1, 2 * down + 1 if down >= 0 else 2 * chip))
    return lax.ppermute(value, "seq", pairs)


def other_head(value):
    return lax.ppermute(value, "head", [(0, 1), (1, 0)])


def dot_nt(a, b):
    return lax.dot_general(a, b, (((1,), (1,)), ((), ())), preferred_element_type=F32)


def dot_nn(a, b):
    return lax.dot_general(a, b, (((1,), (0,)), ((), ())), preferred_element_type=F32)


def split_terms(value, count):
    terms = []
    for _ in range(count):
        terms.append(value.astype(BF16).astype(F32))
        value = value - terms[-1]
    return terms


def prepare_body(reach_ref, q_in, s_in, v_in, g_in, k_ref, v_ref, g_ref, q_ref, s_ref, sems):
    length, width = q_ref.shape
    pairs = ((q_in, q_ref), (s_in, s_ref), (v_in, v_ref), (g_in, g_ref))
    copies = [pltpu.make_async_copy(a, b, sems.at[i]) for i, (a, b) in enumerate(pairs)]
    for copy in copies:
        copy.start()
    copies[0].wait()
    copies[1].wait()
    row = lax.broadcasted_iota(jnp.int32, (LANES, LANES), 0)
    lane = lax.broadcasted_iota(jnp.int32, (LANES, LANES), 1)
    same = jnp.where(lax.div(row, HD) == lax.div(lane, HD), 1.0, 0.0).astype(BF16)
    scale_terms = split_terms(s_ref[...], 3)
    scale_terms.append(jnp.zeros((LANES - 3 * s_ref.shape[0], length), F32))
    scale_terms = jnp.transpose(jnp.concatenate(scale_terms, axis=0)).astype(BF16)
    for g in range(width // LANES):
        lanes = slice(LANES * g, LANES * g + LANES)
        q = q_ref[:, lanes].astype(F32)
        high, rest = split_terms(q * q, 2)
        total = dot_nn(high.astype(BF16), same) + dot_nn(rest.astype(BF16), same)
        head = 2 * g + lax.div(lane, HD)
        pick = jnp.where(lax.rem(row, s_ref.shape[0]) == head, 1.0, 0.0)
        pick = jnp.where(row < 3 * s_ref.shape[0], pick, 0.0).astype(BF16)
        scale = dot_nn(scale_terms, pick)
        k_ref[0:length, lanes] = ((q * lax.rsqrt(total + 1e-6)) * scale).astype(BF16)
    reach = jnp.full((REACH_ROWS, width), reach_ref[0].astype(F32), F32)
    k_ref[length:, :] = reach.astype(BF16)
    copies[2].wait()
    copies[3].wait()


def turn_body(v_ref, g_ref, vt_ref, gt_ref):
    vt_ref[...] = jnp.transpose(v_ref[...].astype(F32)).astype(BF16)
    gt_ref[...] = jnp.transpose(g_ref[...].astype(F32)).astype(BF16)


def join_body(*refs):
    *parts, out_ref = refs
    at = 0
    for ref in parts:
        out_ref[at : at + ref.shape[0], :] = ref[...]
        at += ref.shape[0]


def head_keys(k_ref, length, h):
    g = h // 2
    lane = lax.broadcasted_iota(jnp.int32, (length, LANES), 1)
    keep = (lane < HD) if h % 2 == 0 else (lane >= HD)
    rows = k_ref[0:length, LANES * g : LANES * g + LANES]
    return jnp.where(keep, rows, jnp.zeros_like(rows))


NEAR = ((0, 0, 0, None), (1, 0, 1, None))
DIRECT = ((0, 0, 2, 1), (0, 1, 1, 1), (1, 0, 4, 2), (1, 1, 3, 2))
SIBLING = ((0, 0, 1, None),)
PASSED = ((0, 0, 3, -1), (0, 1, 2, -1), (1, 1, 4, -2))


def allowed_slots(chips, reach_ref, slots, keys, length):
    place = lax.axis_index("seq")
    chip, toward = lax.div(place, 2), 2 * lax.rem(place, 2) - 1
    near = reach_ref[0].astype(F32)
    result = []
    for index, block, distance, away in slots:
        if distance == 0:
            result.append(None)
            continue
        start = block * (length + REACH_ROWS) + length
        far = jnp.max(keys[index][start : start + REACH_ROWS, 0:LANES].astype(F32))
        allowed = jnp.minimum(near, far) >= float(distance)
        if away is not None:
            other = chip + away * toward
            allowed = jnp.logical_and(allowed, jnp.logical_and(other >= 0, other < chips))
        result.append(allowed)
    return result


def off_diagonal(scores, row, column):
    rows = lax.broadcasted_iota(jnp.int32, scores.shape, 0) + row
    columns = lax.broadcasted_iota(jnp.int32, scores.shape, 1) + column
    return jnp.where(rows == columns, NEGATIVE, scores)


def stats_body(chips, slots, reach_ref, own, *refs):
    *refs, ok_ref = refs
    count = len({slot[0] for slot in slots})
    keys, rest = refs[:count], refs[count:]
    length = own.shape[0] - REACH_ROWS
    heads = own.shape[1] // HD
    last = slots is PASSED
    if last:
        near_ref, direct_ref, m_ref, w_ref, total_ref, f_ref, shift_ref = rest
    else:
        m_ref, w_ref = rest
    mine = [head_keys(own, length, h) for h in range(heads)]

    def tile(index):
        array, block, distance, _ = slots[index]
        row = block * (length + REACH_ROWS)
        products = []
        for g in range(heads // 2):
            rows = keys[array][row : row + length, LANES * g : LANES * g + LANES]
            for part in range(0, length, LANES):
                pair = [mine[h][part : part + LANES, :] for h in (2 * g, 2 * g + 1)]
                products.append((g, part, dot_nt(rows, jnp.concatenate(pair, axis=0))))
        for g, part, product in products:
            for h in (2 * g, 2 * g + 1):
                scores = product[:, LANES * (h % 2) : LANES * (h % 2) + LANES]
                if distance == 0:
                    scores = off_diagonal(scores, 0, part)
                top = jnp.max(scores, axis=0, keepdims=True)
                exponent = jnp.exp(scores - top)
                total = jnp.sum(exponent, axis=0, keepdims=True)
                lanes = slice(part, part + LANES)
                at = 2 * heads * index + h
                m_ref[at : at + 1, lanes] = top
                m_ref[at + heads : at + heads + 1, lanes] = total
                at = (index * heads + h) * length * (length // LANES) + part // LANES * length
                w_ref[at : at + length, :] = exponent.astype(BF16)

    allowed = allowed_slots(chips, reach_ref, slots, keys, length)
    for index, ok in enumerate(allowed):
        if ok is None:
            ok_ref[index] = 1
            tile(index)
            continue
        ok_ref[index] = ok.astype(jnp.int32)
        at = 2 * heads * index
        m_ref[at : at + heads, :] = jnp.full((heads, length), NEGATIVE, F32)
        m_ref[at + heads : at + 2 * heads, :] = jnp.zeros((heads, length), F32)
        pl.when(ok)(partial(tile, index))

    if last:
        parts = []
        for ref, part in ((near_ref, NEAR), (direct_ref, DIRECT), (m_ref, PASSED)):
            parts += [(ref, 2 * heads * s) for s in range(len(part))]
        tops = [ref[at : at + heads, :] for ref, at in parts]
        top = tops[0]
        for other in tops[1:]:
            top = jnp.maximum(top, other)
        total = jnp.zeros((heads, length), F32)
        for index, (ref, at) in enumerate(parts):
            factor = jnp.exp(tops[index] - top)
            total = total + factor * ref[at + heads : at + 2 * heads, :]
            f_ref[2 * heads * index : 2 * heads * index + heads, :] = factor
        terms = split_terms(top + jnp.log(total), 3)
        terms.append(jnp.zeros((SHIFT_ROWS - 3 * heads, length), F32))
        shift_ref[...] = jnp.concatenate(terms, axis=0).astype(BF16)
        total_ref[...] = total


def numerator(values, w_ref, slots, index, h, length, heads):
    array, block, _, _ = slots[index]
    at = (index * heads + h) * length * (length // LANES)
    starts = range(at, at + length * (length // LANES), length)
    weights = [w_ref[start : start + length, :] for start in starts]
    row = (block * heads + h) * HD
    return dot_nn(values[array][row : row + HD, :], jnp.concatenate(weights, axis=1))


def attend_near_body(own, sib, w_ref, *outs):
    width, length = outs[0].shape
    heads = width // HD
    for index, out in enumerate(outs):
        for h in range(heads):
            part = numerator((own, sib), w_ref, NEAR, index, h, length, heads)
            out[HD * h : HD * h + HD, :] = part


def attend_body(slots, ok_ref, *refs):
    values, refs = refs[0:2], refs[2:]
    last = slots is PASSED
    if last:
        w_ref, f_ref, total_ref, acc_in, keep_ref, send_ref, acc, rows_ref = refs
    else:
        ok_sib, values, refs = values[0], (values[1], refs[0]), refs[1:]
        w_ref, f_ref, own_in, sib_in, acc = refs
    width, length = acc.shape
    heads = width // HD
    before = len(NEAR) + (len(DIRECT) if last else 0)

    def factor(slot, h):
        at = 2 * heads * slot + h
        return f_ref[at : at + 1, :]

    def tile(index):
        for h in range(heads):
            numer = numerator(values, w_ref, slots, index, h, length, heads)
            acc[HD * h : HD * h + HD, :] += numer * factor(before + index, h)

    def near():
        for h in range(heads):
            part = slice(HD * h, HD * h + HD)
            acc[part, :] += sib_in[part, :] * factor(1, h)

    if last:
        acc[...] = acc_in[...]
    else:
        for h in range(heads):
            part = slice(HD * h, HD * h + HD)
            acc[part, :] = own_in[part, :] * factor(0, h)
        pl.when(ok_sib[1] > 0)(near)
    for index in range(len(slots)):
        pl.when(ok_ref[index] > 0)(partial(tile, index))
    if last:
        for h in range(heads):
            part = slice(HD * h, HD * h + HD)
            acc[part, :] = acc[part, :] / total_ref[h : h + 1, :]
        rows_ref[...] = jnp.transpose(acc[...])
        half = length // 2
        mine = lax.axis_index("head")
        keep_ref[...] = rows_ref[pl.ds(pl.multiple_of(mine * half, half), half), :].astype(BF16)
        other = pl.multiple_of((1 - mine) * half, half)
        send_ref[...] = rows_ref[pl.ds(other, half), :].astype(BF16)


def shifted_keys(own, length, heads):
    lane = lax.broadcasted_iota(jnp.int32, (length, LANES), 1)
    result = []
    for h in range(heads):
        term = lane - ((HD if h % 2 == 0 else 0) + h)
        one = jnp.logical_or(term == 0, jnp.logical_or(term == heads, term == 2 * heads))
        minus = jnp.where(one, -1.0, 0.0).astype(BF16)
        rows = own[0:length, LANES * (h // 2) : LANES * (h // 2) + LANES]
        result.append(jnp.where((lane < HD) if h % 2 == 0 else (lane >= HD), rows, minus))
    return result


def shift_terms(ref, block, length):
    terms = ref[block * SHIFT_ROWS : (block + 1) * SHIFT_ROWS, :].astype(F32)
    rest = jnp.zeros((HD - SHIFT_ROWS, length), F32)
    return jnp.transpose(jnp.concatenate([terms, rest, terms, rest], axis=0)).astype(BF16)


def grad_tile(mine, key, grad, terms, block, length, width, heads, acc, own):
    low = lax.broadcasted_iota(jnp.int32, (length, LANES), 1) < HD
    row = block * (length + REACH_ROWS)
    products = []
    for h in heads:
        far = key[row : row + length, LANES * (h // 2) : LANES * (h // 2) + LANES]
        far = jnp.where(low if h % 2 == 0 else ~low, far, terms)
        products.append(dot_nt(far, mine[h]))
    if own:
        products = [off_diagonal(scores, 0, 0) for scores in products]
    weights = [jnp.exp(scores).astype(BF16) for scores in products]
    for h, weight in zip(heads, weights):
        part = slice(HD * h, HD * h + HD)
        share = dot_nn(grad[block * width + HD * h : block * width + HD * h + HD, :], weight)
        if own:
            acc[part, :] = share
        else:
            acc[part, :] += share


def grad_own_body(key, grad, shift, acc):
    width, length = acc.shape
    heads = range(width // HD)
    mine = shifted_keys(key, length, width // HD)
    terms = shift_terms(shift, 0, length)
    grad_tile(mine, key, grad, terms, 0, length, width, heads, acc, True)


def grad_body(slots, ok_ref, own, *refs):
    count = len({slot[0] for slot in slots})
    keys, grads, shifts = refs[0:count], refs[count : 2 * count], refs[2 * count : 3 * count]
    acc_in, acc = refs[3 * count :]
    width, length = acc.shape
    heads = range(width // HD)
    mine = shifted_keys(own, length, width // HD)
    acc[...] = acc_in[...]

    def tile(array, block):
        terms = shift_terms(shifts[array], block, length)
        key, grad = keys[array], grads[array]
        grad_tile(mine, key, grad, terms, block, length, width, heads, acc, False)

    for index, (array, block, _, _) in enumerate(slots):
        at = index + (len(NEAR) - 1 if slots is SIBLING else 0)
        pl.when(ok_ref[at] > 0)(partial(tile, array, block))


def final_body(ok_ref, keep_ref, got_ref, near_ref, far_ref, own, acc_in, *refs):
    keys, grads, shifts, rest = refs[0:2], refs[2:4], refs[4:6], refs[6:]
    mixed_out, grad_out, acc, mixed, turned, sems = rest
    width, length = acc.shape
    total = dot_nn(keep_ref[...], near_ref[...]) + dot_nn(got_ref[...], far_ref[...])
    mixed[...] = total.astype(BF16)
    copies = [pltpu.make_async_copy(mixed, mixed_out, sems.at[0])]
    copies[0].start()
    acc[...] = acc_in[...]
    mine = shifted_keys(own, length, width // HD)

    def tile(index):
        array, block, _, _ = PASSED[index]
        heads, terms = range(width // HD), shift_terms(shifts[array], block, length)
        key, grad = keys[array], grads[array]
        grad_tile(mine, key, grad, terms, block, length, width, heads, acc, False)

    for index in range(len(PASSED)):
        pl.when(ok_ref[index] > 0)(partial(tile, index))
    for group in range(width // LANES):
        lanes = slice(LANES * group, LANES * group + LANES)
        turned[group] = jnp.transpose(acc[lanes, :]).astype(BF16)
        copy = pltpu.make_async_copy(turned.at[group], grad_out.at[:, lanes], sems.at[group + 1])
        copy.start()
        copies.append(copy)
    for copy in copies:
        copy.wait()


VMEM = pl.BlockSpec(memory_space=pltpu.VMEM)
SMEM = pl.BlockSpec(memory_space=pltpu.SMEM)
HBM = pl.BlockSpec(memory_space=pltpu.HBM)
PARAMS = pltpu.CompilerParams(vmem_limit_bytes=8 * 1024 * 1024)


def call(body, scalars, args, outs, scratch=(), flags=0):
    args = [pltpu.with_memory_space_constraint(a, pltpu.VMEM) for a in args]
    run = pl.pallas_call(
        body,
        in_specs=[SMEM] * len(scalars) + [VMEM] * len(args),
        out_specs=[VMEM] * len(outs) + [SMEM] * (flags > 0),
        out_shape=[pltpu.VMEM(shape, dtype) for shape, dtype in outs]
        + [pltpu.SMEM((flags,), jnp.int32)] * (flags > 0),
        compiler_params=PARAMS,
        scratch_shapes=[pltpu.VMEM(shape, dtype) for shape, dtype in scratch],
    )
    return list(run(*scalars, *args))


def joined(parts):
    rows, width = sum(part.shape[0] for part in parts), parts[0].shape[1]
    (both,) = call(join_body, [], parts, [((rows, width), BF16)])
    return both


def gathered(own):
    sib = sibling(own)
    return [own, sib], *rings(joined([own, sib]))


def rings(both):
    one, two = chip_ring(both, 1), chip_ring(both, 2)
    one, two = lax.optimization_barrier((one, two))
    return [one, two], [sibling(one), sibling(two)]


def compute(queries, values, scales, block_reach, out_weight, out_grad):
    length, width = queries.shape
    heads = scales.shape[1]
    chips = lax.axis_size("seq") // 2
    inputs = [queries, scales.T, values, out_grad]
    keys, *raw = pl.pallas_call(
        prepare_body,
        name="prepare",
        in_specs=[SMEM] + [HBM] * 4,
        out_specs=[VMEM] * 3,
        out_shape=[
            pltpu.VMEM((length + REACH_ROWS, width), BF16),
            pltpu.VMEM((length, width), BF16),
            pltpu.VMEM((length, width), BF16),
        ],
        compiler_params=PARAMS,
        scratch_shapes=[
            pltpu.VMEM((length, width), BF16),
            pltpu.VMEM((heads, length), F32),
            pltpu.SemaphoreType.DMA((4,)),
        ],
    )(block_reach, *(pltpu.with_memory_space_constraint(a, pltpu.HBM) for a in inputs))
    turned, grads = call(turn_body, [], raw, [((width, length), BF16)] * 2)
    stages = (NEAR, DIRECT, PASSED)
    key_set = gathered(keys)
    value_set = gathered(turned)
    grad_set = gathered(grads)
    far_weight = other_head(out_weight)

    tops, weights, allowed = [], [], []
    for index, slots in enumerate(stages):
        last = slots is PASSED
        outs = [
            ((2 * heads * len(slots), length), F32),
            ((heads * len(slots) * length * length // LANES, LANES), BF16),
        ]
        if last:
            total = sum(len(part) for part in stages)
            outs += [((heads, length), F32), ((2 * heads * total, length), F32)]
            outs += [((SHIFT_ROWS, length), BF16)]
        args = [keys, *key_set[index], *(tops if last else [])]
        body = partial(stats_body, chips, slots)
        top, weight, *rest, ok = call(body, [block_reach], args, outs, flags=len(slots))
        tops.append(top)
        weights.append(weight)
        allowed.append(ok)
    totals, factors, shifts = rest
    shift_set = gathered(shifts)

    whole = ((width, length), F32)
    near = call(attend_near_body, [], [*value_set[0], weights[0]], [whole] * 2)
    args = [*value_set[1], weights[1], factors, *near]
    (running,) = call(
        lambda ok_sib, ok, *refs: attend_body(DIRECT, ok, ok_sib, *refs),
        [allowed[0], allowed[1]],
        args,
        [whole],
    )
    args = [*value_set[2], weights[2], factors, totals, running]
    outs = [((length // 2, width), BF16)] * 2
    scratch = [whole, ((length, width), F32)]
    body = partial(attend_body, PASSED)
    keep, send = call(body, [allowed[2]], args, outs, scratch)
    got = other_head(send)

    args = [keys, grads, shifts]
    running = call(grad_own_body, [], args, [whole])
    sets = (key_set, grad_set, shift_set)
    args = [keys, *(part[0][1] for part in sets), *running]
    running = call(partial(grad_body, SIBLING), [allowed[0]], args, [whole])
    args = [keys, *key_set[1], *grad_set[1], *shift_set[1], *running]
    (running,) = call(partial(grad_body, DIRECT), [allowed[1]], args, [whole])
    half, full = length // 2, out_weight.shape[1]
    inputs = [keep, got, out_weight, far_weight, keys, running]
    inputs += [*key_set[2], *grad_set[2], *shift_set[2]]
    inputs = [pltpu.with_memory_space_constraint(a, pltpu.VMEM) for a in inputs]
    mixed, value_grad = pl.pallas_call(
        final_body,
        name="final",
        in_specs=[SMEM] + [VMEM] * len(inputs),
        out_specs=[HBM] * 2,
        out_shape=[
            jax.ShapeDtypeStruct((half, full), BF16),
            jax.ShapeDtypeStruct((length, width), BF16),
        ],
        compiler_params=PARAMS,
        scratch_shapes=[
            pltpu.VMEM((width, length), F32),
            pltpu.VMEM((half, full), BF16),
            pltpu.VMEM((width // LANES, length, LANES), BF16),
            pltpu.SemaphoreType.DMA((1 + width // LANES,)),
        ],
    )(allowed[2], *inputs)
    return (mixed, value_grad)


def solution(mesh):
    return jax.shard_map(
        compute,
        mesh=mesh,
        in_specs=(
            P("seq", "head"),
            P("seq", "head"),
            P("seq", "head"),
            P("seq"),
            P("head", None),
            P("seq", "head"),
        ),
        out_specs=(P(("seq", "head"), None), P("seq", "head")),
        check_vma=False,
    )
```

time: 47.2 us -> 46.7 us (0.989)
  Pallas kernels: 11.3 us -> 10.8 us
    pallas_call x12 -> x14, Pallas kernels: 8.07 us -> 7.94 us  [call(): return list(run(*scalars, *args))]
where the time goes in v4:
time: 46.7 us; the launch traced here: 46.5 us
  waiting for transfers between devices  18.2 us (39%)
  starting transfers between devices  16 us (34%)
  Pallas kernels  10.8 us (23%)
  between operations  1.46 us (3%)
    ppermute x8, waiting for transfers between devices, chip_ring(): return lax.ppermute(value, 'seq', pairs)  15.3 us
    pallas_call x14, Pallas kernels, call(): return list(run(*scalars, *args))  7.94 us
    ppermute x8, starting transfers between devices, chip_ring(): return lax.ppermute(value, 'seq', pairs)  7.84 us
    ppermute x12, starting transfers between devices, sibling(): return lax.ppermute(value, 'seq', [(i, i ^ 1) for i in range(count)])  5.71 us
    ppermute x12, waiting for transfers between devices, sibling(): return lax.ppermute(value, 'seq', [(i, i ^ 1) for i in range(count)])  2.89 us
    ppermute x2, starting transfers between devices, other_head(): return lax.ppermute(value, 'head', [(0, 1), (1, 0)])  2.48 us
    pallas_call x1, Pallas kernels, compute(): pl.pallas_call(final_body, name='final', in_specs=[SMEM] + [VMEM] * len(i...  1.63 us
    pallas_call x1, Pallas kernels, compute(): pl.pallas_call(prepare_body, name='prepare', in_specs=[SMEM] + [HBM] * 4,...  1.28 us
  transfers between devices with their start and end apart: 22, of which 11 were waited for; matrix products, arithmetic and copies ran while one was open for 0% of the time, Pallas kernels for 17%

profile of v4, /device:TPU:17, one launch (start us, length us, event | category | flops | bytes accessed | tf_op | source)
XLA Modules:
  0.0 46.5 jit_solution(13754370089816095957)
XLA Ops:
  0.6 0.0 copy-start
  1.3 1.3 %prepare.1 = (bf16[272,256]{1,0:T(8,128)(2,1)S(1)}, bf16[256,256]{1,0:T(8,128)(2,1)S(1)}, bf16[256,256]{1,0:T(8,128)(2,1)S(1)}) custom-call(s32[1]{0:T(128)S(6)} %copy.8.reach_ref, bf16[256,256]{1,0:T(8,128)(2,1)} %q_in.1, f32[4,256]{1,0:T(4,128)} %bitcast.1, bf16[256,256]{1,0:T(8,128)(2,1)} %v_in.1, bf16[256,256]{1,0:T(8,128)(2,1)} %g_in.1), custom_call_target="tpu_custom_call" | custom-call | tf_op jit(solution)/shard_map/prepare/pallas_call | solution.py:406
  2.6 0.7 %collective-permute-start = (bf16[272,256]{1,0:T(8,128)(2,1)S(1)}, bf16[272,256]{1,0:T(8,128)(2,1)S(1)}, u32[]{:S(2)}, u32[]{:S(2)}) collective-permute-start(bf16[272,256]{1,0:T(8,128)(2,1)S(1)} %get-tuple-element.30.refs_0_.own.key), channel_id=1, source_target_pairs={{0,2},{2,0},{4,6},{6,4},{8,10},{10,8},{12,14},{14,12},{16,18},{18,... | collective-permute-start | bytes 417800 | tf_op jit(solution)/shard_map/ppermute | solution.py:22
  3.4 0.1 shard_map.81
  3.5 0.1 collective-permute-start.5
  3.6 0.8 %collective-permute-done.refs_1_.refs_0_ = bf16[272,256]{1,0:T(8,128)(2,1)S(1)} collective-permute-done((bf16[272,256]{1,0:T(8,128)(2,1)S(1)}, bf16[272,256]{1,0:T(8,128)(2,1)S(1)}, u32[]{:S(2)}, u32[]{:S(2)}) %collective-permute-start) | collective-permute-done | bytes 139296 | tf_op jit(solution)/shard_map/ppermute | solution.py:22
  4.4 1.2 %collective-permute-start.1 = (bf16[544,256]{1,0:T(8,128)(2,1)S(1)}, bf16[544,256]{1,0:T(8,128)(2,1)S(1)}, u32[]{:S(2)}, u32[]{:S(2)}) collective-permute-start(bf16[544,256]{1,0:T(8,128)(2,1)S(1)} %shard_map.77), channel_id=1, source_target_pairs={{0,4},{2,0},{4,8},{6,2},{8,12},{10,6},{12,16},{14,10},{16,20},{18,... | collective-permute-start | bytes 835592 | tf_op jit(solution)/shard_map/ppermute | solution.py:32
  5.6 0.2 collective-permute-start.2
  5.7 0.0 collective-permute-done.5.refs_1_.sib
  5.8 0.4 collective-permute-start.6
  6.1 1.6 %collective-permute-start.7 = (bf16[512,256]{1,0:T(8,128)(2,1)S(1)}, bf16[512,256]{1,0:T(8,128)(2,1)S(1)}, u32[]{:S(2)}, u32[]{:S(2)}) collective-permute-start(bf16[512,256]{1,0:T(8,128)(2,1)S(1)} %shard_map.82), channel_id=1, source_target_pairs={{0,8},{2,0},{4,12},{6,4},{8,16},{10,2},{12,20},{14,6},{16,24},{18,... | collective-permute-start | bytes 786440 | tf_op jit(solution)/shard_map/ppermute | solution.py:32
  7.7 0.7 %collective-permute-start.12 = (bf16[256,256]{1,0:T(8,128)(2,1)S(1)}, bf16[256,256]{1,0:T(8,128)(2,1)S(1)}, u32[]{:S(2)}, u32[]{:S(2)}) collective-permute-start(bf16[256,256]{1,0:T(8,128)(2,1)S(1)} %get-tuple-element.52.refs_0_.grad), channel_id=1, source_target_pairs={{0,2},{2,0},{4,6},{6,4},{8,10},{10,8},{12,14},{14,12},{16,18},{18,... | collective-permute-start | bytes 393224 | tf_op jit(solution)/shard_map/ppermute | solution.py:22
  8.4 1.0 %collective-permute-done.12.refs_1_ = bf16[256,256]{1,0:T(8,128)(2,1)S(1)} collective-permute-done((bf16[256,256]{1,0:T(8,128)(2,1)S(1)}, bf16[256,256]{1,0:T(8,128)(2,1)S(1)}, u32[]{:S(2)}, u32[]{:S(2)}) %collective-permute-start.12) | collective-permute-done | bytes 131104 | tf_op jit(solution)/shard_map/ppermute | solution.py:22
  9.4 2.3 %collective-permute-start.13 = (bf16[512,256]{1,0:T(8,128)(2,1)S(1)}, bf16[512,256]{1,0:T(8,128)(2,1)S(1)}, u32[]{:S(2)}, u32[]{:S(2)}) collective-permute-start(bf16[512,256]{1,0:T(8,128)(2,1)S(1)} %shard_map.86), channel_id=1, source_target_pairs={{0,4},{2,0},{4,8},{6,2},{8,12},{10,6},{12,16},{14,10},{16,20},{18,... | collective-permute-start | bytes 786440 | tf_op jit(solution)/shard_map/ppermute | solution.py:32
  11.7 1.4 %collective-permute-done.1.refs_0_ = bf16[544,256]{1,0:T(8,128)(2,1)S(1)} collective-permute-done((bf16[544,256]{1,0:T(8,128)(2,1)S(1)}, bf16[544,256]{1,0:T(8,128)(2,1)S(1)}, u32[]{:S(2)}, u32[]{:S(2)}) %collective-permute-start.1) | collective-permute-done | bytes 278560 | tf_op jit(solution)/shard_map/ppermute | solution.py:32
  13.1 0.3 collective-permute-start.14
  13.4 0.7 %collective-permute-done.2.refs_1_ = bf16[544,256]{1,0:T(8,128)(2,1)S(1)} collective-permute-done((bf16[544,256]{1,0:T(8,128)(2,1)S(1)}, bf16[544,256]{1,0:T(8,128)(2,1)S(1)}, u32[]{:S(2)}, u32[]{:S(2)}) %collective-permute-start.2) | collective-permute-done | bytes 278560 | tf_op jit(solution)/shard_map/ppermute | solution.py:32
  14.1 0.0 collective-permute-start.3
  14.1 4.6 %collective-permute-done.6.refs_0_ = bf16[512,256]{1,0:T(8,128)(2,1)S(1)} collective-permute-done((bf16[512,256]{1,0:T(8,128)(2,1)S(1)}, bf16[512,256]{1,0:T(8,128)(2,1)S(1)}, u32[]{:S(2)}, u32[]{:S(2)}) %collective-permute-start.6) | collective-permute-done | bytes 262176 | tf_op jit(solution)/shard_map/ppermute | solution.py:32
  18.7 0.3 collective-permute-start.4
  19.0 0.5 %collective-permute-done.7.refs_1_ = bf16[512,256]{1,0:T(8,128)(2,1)S(1)} collective-permute-done((bf16[512,256]{1,0:T(8,128)(2,1)S(1)}, bf16[512,256]{1,0:T(8,128)(2,1)S(1)}, u32[]{:S(2)}, u32[]{:S(2)}) %collective-permute-start.7) | collective-permute-done | bytes 262176 | tf_op jit(solution)/shard_map/ppermute | solution.py:32
  19.5 0.0 copy-done
  19.5 1.2 %collective-permute-start.11 = (bf16[256,1024]{1,0:T(8,128)(2,1)S(1)}, bf16[256,1024]{1,0:T(8,128)(2,1)S(1)}, u32[]{:S(2)}, u32[]{:S(2)}) collective-permute-start(bf16[256,1024]{1,0:T(8,128)(2,1)S(1)} %copy-done), channel_id=1, source_target_pairs={{0,1},{1,0},{2,3},{3,2},{4,5},{5,4},{6,7},{7,6},{8,9},{9,8},{10,11... | collective-permute-start | bytes 1572872 | tf_op jit(solution)/shard_map/ppermute | solution.py:36
  20.7 3.7 %collective-permute-done.13.refs_2_ = bf16[512,256]{1,0:T(8,128)(2,1)S(1)} collective-permute-done((bf16[512,256]{1,0:T(8,128)(2,1)S(1)}, bf16[512,256]{1,0:T(8,128)(2,1)S(1)}, u32[]{:S(2)}, u32[]{:S(2)}) %collective-permute-start.13) | collective-permute-done | bytes 262176 | tf_op jit(solution)/shard_map/ppermute | solution.py:32
  24.4 0.3 collective-permute-start.8
  24.6 0.8 %collective-permute-done.14.refs_3_ = bf16[512,256]{1,0:T(8,128)(2,1)S(1)} collective-permute-done((bf16[512,256]{1,0:T(8,128)(2,1)S(1)}, bf16[512,256]{1,0:T(8,128)(2,1)S(1)}, u32[]{:S(2)}, u32[]{:S(2)}) %collective-permute-start.14) | collective-permute-done | bytes 262176 | tf_op jit(solution)/shard_map/ppermute | solution.py:32
  25.4 0.0 collective-permute-start.9
  25.4 0.0 collective-permute-done.3.refs_0_
  25.5 0.5 %collective-permute-start.18 = (bf16[512,256]{1,0:T(8,128)(2,1)S(1)}, bf16[512,256]{1,0:T(8,128)(2,1)S(1)}, u32[]{:S(2)}, u32[]{:S(2)}) collective-permute-start(bf16[512,256]{1,0:T(8,128)(2,1)S(1)} %collective-permute-done.13.refs_2_), channel_id=1, source_target_pairs={{0,2},{2,0},{4,6},{6,4},{8,10},{10,8},{12,14},{14,12},{16,18},{18,... | collective-permute-start | bytes 786440 | tf_op jit(solution)/shard_map/ppermute | solution.py:22
  26.0 0.0 collective-permute-done.4.refs_1_
  26.0 0.1 collective-permute-start.19
  26.0 1.0 %shard_map.78 = (f32[16,256]{1,0:T(8,128)S(1)}, bf16[4096,128]{1,0:T(8,128)(2,1)S(1)}, s32[2]{0:T(128)S(4)}) custom-call(s32[1]{0:T(128)S(6)} %copy.8.reach_ref, bf16[272,256]{1,0:T(8,128)(2,1)S(1)} %get-tuple-element.30.refs_0_.own.key, bf16[272,256]{1,0:T(8,128)(2,1)S(1)} %get-tuple-element.30.refs_0_.own.key, ...), custom_call_target="tpu_custom_call" | custom-call | tf_op jit(solution)/shard_map/pallas_call | solution.py:381
  27.0 0.3 shard_map.83
  27.3 1.5 %shard_map.79 = (f32[32,256]{1,0:T(8,128)S(1)}, bf16[8192,128]{1,0:T(8,128)(2,1)S(1)}, s32[4]{0:T(128)S(4)}) custom-call(s32[1]{0:T(128)S(6)} %copy.8.reach_ref, bf16[272,256]{1,0:T(8,128)(2,1)S(1)} %get-tuple-element.30.refs_0_.own.key, bf16[544,256]{1,0:T(8,128)(2,1)S(1)} %collective-permute-done.1.refs_0_, bf16[544,256]{1,0:T(8,128)(2,1)S(1)} %collective-permute-done.2.refs_1_), custom_call_target="tpu_custom_call" | custom-call | tf_op jit(solution)/shard_map/pallas_call | solution.py:381
  28.8 1.2 %shard_map.80 = (f32[24,256]{1,0:T(8,128)}, bf16[6144,128]{1,0:T(8,128)(2,1)S(1)}, f32[4,256]{1,0:T(4,128)S(1)}, f32[72,256]{1,0:T(8,128)S(1)}, bf16[16,256]{1,0:T(8,128)(2,1)S(1)}, /*index=5*/s32[3]{0:T(128)S(4)}) custom-call(s32[1]{0:T(128)S(6)} %copy.8.reach_ref, bf16[272,256]{1,0:T(8,128)(2,1)S(1)} %get-tuple-element.30.refs_0_.own.key, ...), custom_call_target="tpu_custom_call" | custom-call | tf_op jit(solution)/shard_map/pallas_call | solution.py:381
  30.0 0.7 %shard_map.84.refs_5_ = f32[256,256]{1,0:T(8,128)S(1)} custom-call(s32[2]{0:T(128)S(4)} %get-tuple-element.44.ok_sib.ok_ref, s32[4]{0:T(128)S(4)} %get-tuple-element.45.ok.ok_ref, bf16[512,256]{1,0:T(8,128)(2,1)S(1)} %collective-permute-done.6.refs_0_, bf16[512,256]{1,0:T(8,128)(2,1)S(1)} %collective-permute-done.7.refs_1_, ...), custom_call_target="tpu_custom_call" | custom-call | tf_op jit(solution)/shard_map/pallas_call | solution.py:381
  30.7 0.0 collective-permute-done.8.refs_0_
  30.7 0.0 collective-permute-done.9.refs_1_
  30.7 0.4 shard_map.85
  31.2 1.3 %collective-permute-start.10 = (bf16[128,256]{1,0:T(8,128)(2,1)S(1)}, bf16[128,256]{1,0:T(8,128)(2,1)S(1)}, u32[]{:S(2)}, u32[]{:S(2)}) collective-permute-start(bf16[128,256]{1,0:T(8,128)(2,1)S(1)} %get-tuple-element.51), channel_id=1, source_target_pairs={{0,1},{1,0},{2,3},{3,2},{4,5},{5,4},{6,7},{7,6},{8,9},{9,8},{10,11... | collective-permute-start | bytes 196616 | tf_op jit(solution)/shard_map/ppermute | solution.py:36
  32.4 0.1 collective-permute-start.15
  32.5 1.1 %collective-permute-done.15.refs_1_.refs_2_ = bf16[16,256]{1,0:T(8,128)(2,1)S(1)} collective-permute-done((bf16[16,256]{1,0:T(8,128)(2,1)S(1)}, bf16[16,256]{1,0:T(8,128)(2,1)S(1)}, u32[]{:S(2)}, u32[]{:S(2)}) %collective-permute-start.15) | collective-permute-done | bytes 8224 | tf_op jit(solution)/shard_map/ppermute | solution.py:22
  33.6 1.6 %collective-permute-start.16 = (bf16[32,256]{1,0:T(8,128)(2,1)S(1)}, bf16[32,256]{1,0:T(8,128)(2,1)S(1)}, u32[]{:S(2)}, u32[]{:S(2)}) collective-permute-start(bf16[32,256]{1,0:T(8,128)(2,1)S(1)} %shard_map.87), channel_id=1, source_target_pairs={{0,4},{2,0},{4,8},{6,2},{8,12},{10,6},{12,16},{14,10},{16,20},{18,... | collective-permute-start | bytes 49160 | tf_op jit(solution)/shard_map/ppermute | solution.py:32
  35.3 1.2 %collective-permute-done.16.refs_4_ = bf16[32,256]{1,0:T(8,128)(2,1)S(1)} collective-permute-done((bf16[32,256]{1,0:T(8,128)(2,1)S(1)}, bf16[32,256]{1,0:T(8,128)(2,1)S(1)}, u32[]{:S(2)}, u32[]{:S(2)}) %collective-permute-start.16) | collective-permute-done | bytes 16416 | tf_op jit(solution)/shard_map/ppermute | solution.py:32
  36.5 0.3 collective-permute-start.17
  36.8 2.3 %collective-permute-done.17.refs_5_ = bf16[32,256]{1,0:T(8,128)(2,1)S(1)} collective-permute-done((bf16[32,256]{1,0:T(8,128)(2,1)S(1)}, bf16[32,256]{1,0:T(8,128)(2,1)S(1)}, u32[]{:S(2)}, u32[]{:S(2)}) %collective-permute-start.17) | collective-permute-done | bytes 16416 | tf_op jit(solution)/shard_map/ppermute | solution.py:32
  39.1 3.1 %collective-permute-start.20 = (bf16[32,256]{1,0:T(8,128)(2,1)S(1)}, bf16[32,256]{1,0:T(8,128)(2,1)S(1)}, u32[]{:S(2)}, u32[]{:S(2)}) collective-permute-start(bf16[32,256]{1,0:T(8,128)(2,1)S(1)} %collective-permute-done.16.refs_4_), channel_id=1, source_target_pairs={{0,2},{2,0},{4,6},{6,4},{8,10},{10,8},{12,14},{14,12},{16,18},{18,... | collective-permute-start | bytes 49160 | tf_op jit(solution)/shard_map/ppermute | solution.py:22
  42.2 0.0 collective-permute-done.11.far_ref
  42.2 0.0 collective-permute-start.21
  42.2 0.5 %shard_map.88.refs_3_ = f32[256,256]{1,0:T(8,128)S(1)} custom-call(bf16[272,256]{1,0:T(8,128)(2,1)S(1)} %get-tuple-element.30.refs_0_.own.key, bf16[256,256]{1,0:T(8,128)(2,1)S(1)} %get-tuple-element.52.refs_0_.grad, bf16[16,256]{1,0:T(8,128)(2,1)S(1)} %get-tuple-element.55.refs_0_.shift), custom_call_target="tpu_custom_call" | custom-call | tf_op jit(solution)/shard_map/pallas_call | solution.py:381
  42.7 0.5 %shard_map.89.refs_6_ = f32[256,256]{1,0:T(8,128)S(1)} custom-call(s32[2]{0:T(128)S(4)} %get-tuple-element.44.ok_sib.ok_ref, bf16[272,256]{1,0:T(8,128)(2,1)S(1)} %get-tuple-element.30.refs_0_.own.key, bf16[272,256]{1,0:T(8,128)(2,1)S(1)} %collective-permute-done.refs_1_.refs_0_, bf16[256,256]{1,0:T(8,128)(2,1)S(1)} %collective-permute-done.12.refs_1_, ...), custom_call_target="tpu_custom_call" | custom-call | tf_op jit(solution)/shard_map/pallas_call | solution.py:381
  43.2 1.6 %shard_map.90.acc_in = f32[256,256]{1,0:T(8,128)S(1)} custom-call(s32[4]{0:T(128)S(4)} %get-tuple-element.45.ok.ok_ref, bf16[272,256]{1,0:T(8,128)(2,1)S(1)} %get-tuple-element.30.refs_0_.own.key, bf16[544,256]{1,0:T(8,128)(2,1)S(1)} %collective-permute-done.1.refs_0_, bf16[544,256]{1,0:T(8,128)(2,1)S(1)} %collective-permute-done.2.refs_1_, ...), custom_call_target="tpu_custom_call" | custom-call | tf_op jit(solution)/shard_map/pallas_call | solution.py:381
  44.8 0.0 collective-permute-done.18.refs_2_
  44.8 0.0 collective-permute-done.19.refs_3_
  44.8 0.0 collective-permute-done.20.refs_4_
  44.9 0.0 collective-permute-done.21.refs_5_
  44.9 0.0 collective-permute-done.10.got_ref
  44.9 1.6 %final.1 = (bf16[128,1024]{1,0:T(8,128)(2,1)}, bf16[256,256]{1,0:T(8,128)(2,1)}) custom-call(s32[3]{0:T(128)S(4)} %get-tuple-element.35.ok_ref, bf16[128,256]{1,0:T(8,128)(2,1)S(1)} %get-tuple-element.50.keep_ref, bf16[128,256]{1,0:T(8,128)(2,1)S(1)} %collective-permute-done.10.got_ref, bf16[256,1024]{1,0:T(8,128)(2,1)S(1)} %copy-done, ...), custom_call_target="tpu_custom_call" | custom-call | tf_op jit(solution)/shard_map/final/pallas_call | solution.py:477
  (4 shorter events, 0.1 us)
Async XLA Ops:
  0.6 18.9 %copy-start = (bf16[256,1024]{1,0:T(8,128)(2,1)S(1)}, bf16[256,1024]{1,0:T(8,128)(2,1)}, u32[]{:S(2)}) copy-start(bf16[256,1024]{1,0:T(8,128)(2,1)} %near_ref.1) | copy-start | bytes 1572868
  2.6 1.7 %collective-permute-start = (bf16[272,256]{1,0:T(8,128)(2,1)S(1)}, bf16[272,256]{1,0:T(8,128)(2,1)S(1)}, u32[]{:S(2)}, u32[]{:S(2)}) collective-permute-start(bf16[272,256]{1,0:T(8,128)(2,1)S(1)} %get-tuple-element.30.refs_0_.own.key), channel_id=1, source_target_pairs={{0,2},{2,0},{4,6},{6,4},{8,10},{10,8},{12,14},{14,12},{16,18},{18,... | collective-permute-start | bytes 417800 | tf_op jit(solution)/shard_map/ppermute | solution.py:22
  3.5 2.2 %collective-permute-start.5 = (bf16[256,256]{1,0:T(8,128)(2,1)S(1)}, bf16[256,256]{1,0:T(8,128)(2,1)S(1)}, u32[]{:S(2)}, u32[]{:S(2)}) collective-permute-start(bf16[256,256]{1,0:T(8,128)(2,1)S(1)} %get-tuple-element.38.refs_0_.own), channel_id=1, source_target_pairs={{0,2},{2,0},{4,6},{6,4},{8,10},{10,8},{12,14},{14,12},{16,18},{18,... | collective-permute-start | bytes 393224 | tf_op jit(solution)/shard_map/ppermute | solution.py:22
  4.4 8.7 %collective-permute-start.1 = (bf16[544,256]{1,0:T(8,128)(2,1)S(1)}, bf16[544,256]{1,0:T(8,128)(2,1)S(1)}, u32[]{:S(2)}, u32[]{:S(2)}) collective-permute-start(bf16[544,256]{1,0:T(8,128)(2,1)S(1)} %shard_map.77), channel_id=1, source_target_pairs={{0,4},{2,0},{4,8},{6,2},{8,12},{10,6},{12,16},{14,10},{16,20},{18,... | collective-permute-start | bytes 835592 | tf_op jit(solution)/shard_map/ppermute | solution.py:32
  5.6 8.6 %collective-permute-start.2 = (bf16[544,256]{1,0:T(8,128)(2,1)S(1)}, bf16[544,256]{1,0:T(8,128)(2,1)S(1)}, u32[]{:S(2)}, u32[]{:S(2)}) collective-permute-start(bf16[544,256]{1,0:T(8,128)(2,1)S(1)} %shard_map.77), channel_id=1, source_target_pairs={{0,8},{2,0},{4,12},{6,4},{8,16},{10,2},{12,20},{14,6},{16,24},{18,... | collective-permute-start | bytes 835592 | tf_op jit(solution)/shard_map/ppermute | solution.py:32
  5.8 13.0 %collective-permute-start.6 = (bf16[512,256]{1,0:T(8,128)(2,1)S(1)}, bf16[512,256]{1,0:T(8,128)(2,1)S(1)}, u32[]{:S(2)}, u32[]{:S(2)}) collective-permute-start(bf16[512,256]{1,0:T(8,128)(2,1)S(1)} %shard_map.82), channel_id=1, source_target_pairs={{0,4},{2,0},{4,8},{6,2},{8,12},{10,6},{12,16},{14,10},{16,20},{18,... | collective-permute-start | bytes 786440 | tf_op jit(solution)/shard_map/ppermute | solution.py:32
  6.1 13.4 %collective-permute-start.7 = (bf16[512,256]{1,0:T(8,128)(2,1)S(1)}, bf16[512,256]{1,0:T(8,128)(2,1)S(1)}, u32[]{:S(2)}, u32[]{:S(2)}) collective-permute-start(bf16[512,256]{1,0:T(8,128)(2,1)S(1)} %shard_map.82), channel_id=1, source_target_pairs={{0,8},{2,0},{4,12},{6,4},{8,16},{10,2},{12,20},{14,6},{16,24},{18,... | collective-permute-start | bytes 786440 | tf_op jit(solution)/shard_map/ppermute | solution.py:32
  7.7 1.6 %collective-permute-start.12 = (bf16[256,256]{1,0:T(8,128)(2,1)S(1)}, bf16[256,256]{1,0:T(8,128)(2,1)S(1)}, u32[]{:S(2)}, u32[]{:S(2)}) collective-permute-start(bf16[256,256]{1,0:T(8,128)(2,1)S(1)} %get-tuple-element.52.refs_0_.grad), channel_id=1, source_target_pairs={{0,2},{2,0},{4,6},{6,4},{8,10},{10,8},{12,14},{14,12},{16,18},{18,... | collective-permute-start | bytes 393224 | tf_op jit(solution)/shard_map/ppermute | solution.py:22
  9.4 15.0 %collective-permute-start.13 = (bf16[512,256]{1,0:T(8,128)(2,1)S(1)}, bf16[512,256]{1,0:T(8,128)(2,1)S(1)}, u32[]{:S(2)}, u32[]{:S(2)}) collective-permute-start(bf16[512,256]{1,0:T(8,128)(2,1)S(1)} %shard_map.86), channel_id=1, source_target_pairs={{0,4},{2,0},{4,8},{6,2},{8,12},{10,6},{12,16},{14,10},{16,20},{18,... | collective-permute-start | bytes 786440 | tf_op jit(solution)/shard_map/ppermute | solution.py:32
  13.1 12.3 %collective-permute-start.14 = (bf16[512,256]{1,0:T(8,128)(2,1)S(1)}, bf16[512,256]{1,0:T(8,128)(2,1)S(1)}, u32[]{:S(2)}, u32[]{:S(2)}) collective-permute-start(bf16[512,256]{1,0:T(8,128)(2,1)S(1)} %shard_map.86), channel_id=1, source_target_pairs={{0,8},{2,0},{4,12},{6,4},{8,16},{10,2},{12,20},{14,6},{16,24},{18,... | collective-permute-start | bytes 786440 | tf_op jit(solution)/shard_map/ppermute | solution.py:32
  14.1 11.3 %collective-permute-start.3 = (bf16[544,256]{1,0:T(8,128)(2,1)S(1)}, bf16[544,256]{1,0:T(8,128)(2,1)S(1)}, u32[]{:S(2)}, u32[]{:S(2)}) collective-permute-start(bf16[544,256]{1,0:T(8,128)(2,1)S(1)} %collective-permute-done.1.refs_0_), channel_id=1, source_target_pairs={{0,2},{2,0},{4,6},{6,4},{8,10},{10,8},{12,14},{14,12},{16,18},{18,... | collective-permute-start | bytes 835592 | tf_op jit(solution)/shard_map/ppermute | solution.py:22
  18.7 7.2 %collective-permute-start.4 = (bf16[544,256]{1,0:T(8,128)(2,1)S(1)}, bf16[544,256]{1,0:T(8,128)(2,1)S(1)}, u32[]{:S(2)}, u32[]{:S(2)}) collective-permute-start(bf16[544,256]{1,0:T(8,128)(2,1)S(1)} %collective-permute-done.2.refs_1_), channel_id=1, source_target_pairs={{0,2},{2,0},{4,6},{6,4},{8,10},{10,8},{12,14},{14,12},{16,18},{18,... | collective-permute-start | bytes 835592 | tf_op jit(solution)/shard_map/ppermute | solution.py:22
  19.5 22.7 %collective-permute-start.11 = (bf16[256,1024]{1,0:T(8,128)(2,1)S(1)}, bf16[256,1024]{1,0:T(8,128)(2,1)S(1)}, u32[]{:S(2)}, u32[]{:S(2)}) collective-permute-start(bf16[256,1024]{1,0:T(8,128)(2,1)S(1)} %copy-done), channel_id=1, source_target_pairs={{0,1},{1,0},{2,3},{3,2},{4,5},{5,4},{6,7},{7,6},{8,9},{9,8},{10,11... | collective-permute-start | bytes 1572872 | tf_op jit(solution)/shard_map/ppermute | solution.py:36
  24.4 6.4 %collective-permute-start.8 = (bf16[512,256]{1,0:T(8,128)(2,1)S(1)}, bf16[512,256]{1,0:T(8,128)(2,1)S(1)}, u32[]{:S(2)}, u32[]{:S(2)}) collective-permute-start(bf16[512,256]{1,0:T(8,128)(2,1)S(1)} %collective-permute-done.6.refs_0_), channel_id=1, source_target_pairs={{0,2},{2,0},{4,6},{6,4},{8,10},{10,8},{12,14},{14,12},{16,18},{18,... | collective-permute-start | bytes 786440 | tf_op jit(solution)/shard_map/ppermute | solution.py:22
  25.4 5.3 %collective-permute-start.9 = (bf16[512,256]{1,0:T(8,128)(2,1)S(1)}, bf16[512,256]{1,0:T(8,128)(2,1)S(1)}, u32[]{:S(2)}, u32[]{:S(2)}) collective-permute-start(bf16[512,256]{1,0:T(8,128)(2,1)S(1)} %collective-permute-done.7.refs_1_), channel_id=1, source_target_pairs={{0,2},{2,0},{4,6},{6,4},{8,10},{10,8},{12,14},{14,12},{16,18},{18,... | collective-permute-start | bytes 786440 | tf_op jit(solution)/shard_map/ppermute | solution.py:22
  25.5 19.4 %collective-permute-start.18 = (bf16[512,256]{1,0:T(8,128)(2,1)S(1)}, bf16[512,256]{1,0:T(8,128)(2,1)S(1)}, u32[]{:S(2)}, u32[]{:S(2)}) collective-permute-start(bf16[512,256]{1,0:T(8,128)(2,1)S(1)} %collective-permute-done.13.refs_2_), channel_id=1, source_target_pairs={{0,2},{2,0},{4,6},{6,4},{8,10},{10,8},{12,14},{14,12},{16,18},{18,... | collective-permute-start | bytes 786440 | tf_op jit(solution)/shard_map/ppermute | solution.py:22
  26.0 18.9 %collective-permute-start.19 = (bf16[512,256]{1,0:T(8,128)(2,1)S(1)}, bf16[512,256]{1,0:T(8,128)(2,1)S(1)}, u32[]{:S(2)}, u32[]{:S(2)}) collective-permute-start(bf16[512,256]{1,0:T(8,128)(2,1)S(1)} %collective-permute-done.14.refs_3_), channel_id=1, source_target_pairs={{0,2},{2,0},{4,6},{6,4},{8,10},{10,8},{12,14},{14,12},{16,18},{18,... | collective-permute-start | bytes 786440 | tf_op jit(solution)/shard_map/ppermute | solution.py:22
  31.2 13.7 %collective-permute-start.10 = (bf16[128,256]{1,0:T(8,128)(2,1)S(1)}, bf16[128,256]{1,0:T(8,128)(2,1)S(1)}, u32[]{:S(2)}, u32[]{:S(2)}) collective-permute-start(bf16[128,256]{1,0:T(8,128)(2,1)S(1)} %get-tuple-element.51), channel_id=1, source_target_pairs={{0,1},{1,0},{2,3},{3,2},{4,5},{5,4},{6,7},{7,6},{8,9},{9,8},{10,11... | collective-permute-start | bytes 196616 | tf_op jit(solution)/shard_map/ppermute | solution.py:36
  32.4 1.2 %collective-permute-start.15 = (bf16[16,256]{1,0:T(8,128)(2,1)S(1)}, bf16[16,256]{1,0:T(8,128)(2,1)S(1)}, u32[]{:S(2)}, u32[]{:S(2)}) collective-permute-start(bf16[16,256]{1,0:T(8,128)(2,1)S(1)} %get-tuple-element.55.refs_0_.shift), channel_id=1, source_target_pairs={{0,2},{2,0},{4,6},{6,4},{8,10},{10,8},{12,14},{14,12},{16,18},{18,... | collective-permute-start | bytes 24584 | tf_op jit(solution)/shard_map/ppermute | solution.py:22
  33.6 2.9 %collective-permute-start.16 = (bf16[32,256]{1,0:T(8,128)(2,1)S(1)}, bf16[32,256]{1,0:T(8,128)(2,1)S(1)}, u32[]{:S(2)}, u32[]{:S(2)}) collective-permute-start(bf16[32,256]{1,0:T(8,128)(2,1)S(1)} %shard_map.87), channel_id=1, source_target_pairs={{0,4},{2,0},{4,8},{6,2},{8,12},{10,6},{12,16},{14,10},{16,20},{18,... | collective-permute-start | bytes 49160 | tf_op jit(solution)/shard_map/ppermute | solution.py:32
  36.5 2.6 %collective-permute-start.17 = (bf16[32,256]{1,0:T(8,128)(2,1)S(1)}, bf16[32,256]{1,0:T(8,128)(2,1)S(1)}, u32[]{:S(2)}, u32[]{:S(2)}) collective-permute-start(bf16[32,256]{1,0:T(8,128)(2,1)S(1)} %shard_map.87), channel_id=1, source_target_pairs={{0,8},{2,0},{4,12},{6,4},{8,16},{10,2},{12,20},{14,6},{16,24},{18,... | collective-permute-start | bytes 49160 | tf_op jit(solution)/shard_map/ppermute | solution.py:32
  39.1 5.8 %collective-permute-start.20 = (bf16[32,256]{1,0:T(8,128)(2,1)S(1)}, bf16[32,256]{1,0:T(8,128)(2,1)S(1)}, u32[]{:S(2)}, u32[]{:S(2)}) collective-permute-start(bf16[32,256]{1,0:T(8,128)(2,1)S(1)} %collective-permute-done.16.refs_4_), channel_id=1, source_target_pairs={{0,2},{2,0},{4,6},{6,4},{8,10},{10,8},{12,14},{14,12},{16,18},{18,... | collective-permute-start | bytes 49160 | tf_op jit(solution)/shard_map/ppermute | solution.py:22
  42.2 2.7 %collective-permute-start.21 = (bf16[32,256]{1,0:T(8,128)(2,1)S(1)}, bf16[32,256]{1,0:T(8,128)(2,1)S(1)}, u32[]{:S(2)}, u32[]{:S(2)}) collective-permute-start(bf16[32,256]{1,0:T(8,128)(2,1)S(1)} %collective-permute-done.17.refs_5_), channel_id=1, source_target_pairs={{0,2},{2,0},{4,6},{6,4},{8,10},{10,8},{12,14},{14,12},{16,18},{18,... | collective-permute-start | bytes 49160 | tf_op jit(solution)/shard_map/ppermute | solution.py:22

commit v5 on v4

--- a/solution.py
+++ b/solution.py
@@ -75,16 +75,30 @@
         pick = jnp.where(lax.rem(row, s_ref.shape[0]) == head, 1.0, 0.0)
         pick = jnp.where(row < 3 * s_ref.shape[0], pick, 0.0).astype(BF16)
         scale = dot_nn(scale_terms, pick)
-        k_ref[0:length, lanes] = ((q * lax.rsqrt(total + 1e-6)) * scale).astype(BF16)
-    reach = jnp.full((REACH_ROWS, width), reach_ref[0].astype(F32), F32)
-    k_ref[length:, :] = reach.astype(BF16)
+        k_ref[g * length : g * length + length, :] = ((q * lax.rsqrt(total + 1e-6)) * scale).astype(BF16)
+    reach = jnp.full((REACH_ROWS, LANES), reach_ref[0].astype(F32), F32)
+    k_ref[width // LANES * length :, :] = reach.astype(BF16)
     copies[2].wait()
     copies[3].wait()
 
 
-def turn_body(v_ref, g_ref, vt_ref, gt_ref):
+def turn_body(k_ref, v_ref, g_ref, vt_ref, gt_ref, pair_ref, minus_ref):
+    length, width = v_ref.shape
+    heads = width // HD
     vt_ref[...] = jnp.transpose(v_ref[...].astype(F32)).astype(BF16)
     gt_ref[...] = jnp.transpose(g_ref[...].astype(F32)).astype(BF16)
+    lane = lax.broadcasted_iota(jnp.int32, (length, LANES), 1)
+    for h in range(heads):
+        rows = k_ref[h // 2 * length : h // 2 * length + length, :]
+        keep = (lane < HD) if h % 2 == 0 else (lane >= HD)
+        alone = jnp.where(keep, rows, jnp.zeros_like(rows))
+        for part in range(0, length, LANES):
+            at = h // 2 * 2 * length + 2 * part + h % 2 * LANES
+            pair_ref[at : at + LANES, :] = alone[part : part + LANES, :]
+        term = lane - ((HD if h % 2 == 0 else 0) + h)
+        one = jnp.logical_or(term == 0, jnp.logical_or(term == heads, term == 2 * heads))
+        minus = jnp.where(one, -1.0, 0.0).astype(BF16)
+        minus_ref[h * length : h * length + length, :] = jnp.where(keep, rows, minus)
 
 
 def join_body(*refs):
@@ -95,21 +109,17 @@
         at += ref.shape[0]
 
 
-def head_keys(k_ref, length, h):
-    g = h // 2
-    lane = lax.broadcasted_iota(jnp.int32, (length, LANES), 1)
-    keep = (lane < HD) if h % 2 == 0 else (lane >= HD)
-    rows = k_ref[0:length, LANES * g : LANES * g + LANES]
-    return jnp.where(keep, rows, jnp.zeros_like(rows))
-
-
 NEAR = ((0, 0, 0, None), (1, 0, 1, None))
 DIRECT = ((0, 0, 2, 1), (0, 1, 1, 1), (1, 0, 4, 2), (1, 1, 3, 2))
 SIBLING = ((0, 0, 1, None),)
 PASSED = ((0, 0, 3, -1), (0, 1, 2, -1), (1, 1, 4, -2))
 
 
-def allowed_slots(chips, reach_ref, slots, keys, length):
+def blocks(slots):
+    return 1 if slots is NEAR or slots is SIBLING else 2
+
+
+def allowed_slots(chips, reach_ref, slots, keys):
     place = lax.axis_index("seq")
     chip, toward = lax.div(place, 2), 2 * lax.rem(place, 2) - 1
     near = reach_ref[0].astype(F32)
@@ -118,7 +128,7 @@
         if distance == 0:
             result.append(None)
             continue
-        start = block * (length + REACH_ROWS) + length
+        start = (block + 1) * (keys[index].shape[0] // blocks(slots)) - REACH_ROWS
         far = jnp.max(keys[index][start : start + REACH_ROWS, 0:LANES].astype(F32))
         allowed = jnp.minimum(near, far) >= float(distance)
         if away is not None:
@@ -134,28 +144,27 @@
     return jnp.where(rows == columns, NEGATIVE, scores)
 
 
-def stats_body(chips, slots, reach_ref, own, *refs):
+def stats_body(chips, slots, reach_ref, paired, *refs):
     *refs, ok_ref = refs
     count = len({slot[0] for slot in slots})
     keys, rest = refs[:count], refs[count:]
-    length = own.shape[0] - REACH_ROWS
-    heads = own.shape[1] // HD
     last = slots is PASSED
     if last:
         near_ref, direct_ref, m_ref, w_ref, total_ref, f_ref, shift_ref = rest
     else:
         m_ref, w_ref = rest
-    mine = [head_keys(own, length, h) for h in range(heads)]
+    length = m_ref.shape[1]
+    heads = paired.shape[0] // length
 
     def tile(index):
         array, block, distance, _ = slots[index]
-        row = block * (length + REACH_ROWS)
         products = []
         for g in range(heads // 2):
-            rows = keys[array][row : row + length, LANES * g : LANES * g + LANES]
+            row = block * (heads // 2 * length + REACH_ROWS) + g * length
+            rows = keys[array][row : row + length, :]
             for part in range(0, length, LANES):
-                pair = [mine[h][part : part + LANES, :] for h in (2 * g, 2 * g + 1)]
-                products.append((g, part, dot_nt(rows, jnp.concatenate(pair, axis=0))))
+                at = 2 * (g * length + part)
+                products.append((g, part, dot_nt(rows, paired[at : at + 2 * LANES, :])))
         for g, part, product in products:
             for h in (2 * g, 2 * g + 1):
                 scores = product[:, LANES * (h % 2) : LANES * (h % 2) + LANES]
@@ -171,7 +180,7 @@
                 at = (index * heads + h) * length * (length // LANES) + part // LANES * length
                 w_ref[at : at + length, :] = exponent.astype(BF16)
 
-    allowed = allowed_slots(chips, reach_ref, slots, keys, length)
+    allowed = allowed_slots(chips, reach_ref, slots, keys)
     for index, ok in enumerate(allowed):
         if ok is None:
             ok_ref[index] = 1
@@ -267,18 +276,6 @@
         send_ref[...] = rows_ref[pl.ds(other, half), :].astype(BF16)
 
 
-def shifted_keys(own, length, heads):
-    lane = lax.broadcasted_iota(jnp.int32, (length, LANES), 1)
-    result = []
-    for h in range(heads):
-        term = lane - ((HD if h % 2 == 0 else 0) + h)
-        one = jnp.logical_or(term == 0, jnp.logical_or(term == heads, term == 2 * heads))
-        minus = jnp.where(one, -1.0, 0.0).astype(BF16)
-        rows = own[0:length, LANES * (h // 2) : LANES * (h // 2) + LANES]
-        result.append(jnp.where((lane < HD) if h % 2 == 0 else (lane >= HD), rows, minus))
-    return result
-
-
 def shift_terms(ref, block, length):
     terms = ref[block * SHIFT_ROWS : (block + 1) * SHIFT_ROWS, :].astype(F32)
     rest = jnp.zeros((HD - SHIFT_ROWS, length), F32)
@@ -287,12 +284,12 @@
 
 def grad_tile(mine, key, grad, terms, block, length, width, heads, acc, own):
     low = lax.broadcasted_iota(jnp.int32, (length, LANES), 1) < HD
-    row = block * (length + REACH_ROWS)
+    row = block * (width // LANES * length + REACH_ROWS)
     products = []
     for h in heads:
-        far = key[row : row + length, LANES * (h // 2) : LANES * (h // 2) + LANES]
+        far = key[row + h // 2 * length : row + h // 2 * length + length, :]
         far = jnp.where(low if h % 2 == 0 else ~low, far, terms)
-        products.append(dot_nt(far, mine[h]))
+        products.append(dot_nt(far, mine[h * length : h * length + length, :]))
     if own:
         products = [off_diagonal(scores, 0, 0) for scores in products]
     weights = [jnp.exp(scores).astype(BF16) for scores in products]
@@ -305,21 +302,19 @@
             acc[part, :] += share
 
 
-def grad_own_body(key, grad, shift, acc):
+def grad_own_body(mine, key, grad, shift, acc):
     width, length = acc.shape
     heads = range(width // HD)
-    mine = shifted_keys(key, length, width // HD)
     terms = shift_terms(shift, 0, length)
     grad_tile(mine, key, grad, terms, 0, length, width, heads, acc, True)
 
 
-def grad_body(slots, ok_ref, own, *refs):
+def grad_body(slots, ok_ref, mine, *refs):
     count = len({slot[0] for slot in slots})
     keys, grads, shifts = refs[0:count], refs[count : 2 * count], refs[2 * count : 3 * count]
     acc_in, acc = refs[3 * count :]
     width, length = acc.shape
     heads = range(width // HD)
-    mine = shifted_keys(own, length, width // HD)
     acc[...] = acc_in[...]
 
     def tile(array, block):
@@ -332,7 +327,7 @@
         pl.when(ok_ref[at] > 0)(partial(tile, array, block))
 
 
-def final_body(ok_ref, keep_ref, got_ref, near_ref, far_ref, own, acc_in, *refs):
+def final_body(ok_ref, keep_ref, got_ref, near_ref, far_ref, mine, acc_in, *refs):
     keys, grads, shifts, rest = refs[0:2], refs[2:4], refs[4:6], refs[6:]
     mixed_out, grad_out, acc, mixed, turned, sems = rest
     width, length = acc.shape
@@ -341,7 +336,6 @@
     copies = [pltpu.make_async_copy(mixed, mixed_out, sems.at[0])]
     copies[0].start()
     acc[...] = acc_in[...]
-    mine = shifted_keys(own, length, width // HD)
 
     def tile(index):
         array, block, _, _ = PASSED[index]
@@ -409,7 +403,7 @@
         in_specs=[SMEM] + [HBM] * 4,
         out_specs=[VMEM] * 3,
         out_shape=[
-            pltpu.VMEM((length + REACH_ROWS, width), BF16),
+            pltpu.VMEM((width // LANES * length + REACH_ROWS, LANES), BF16),
             pltpu.VMEM((length, width), BF16),
             pltpu.VMEM((length, width), BF16),
         ],
@@ -420,7 +414,8 @@
             pltpu.SemaphoreType.DMA((4,)),
         ],
     )(block_reach, *(pltpu.with_memory_space_constraint(a, pltpu.HBM) for a in inputs))
-    turned, grads = call(turn_body, [], raw, [((width, length), BF16)] * 2)
+    outs = [((width, length), BF16)] * 2 + [((heads * length, LANES), BF16)] * 2
+    turned, grads, paired, shifted = call(turn_body, [], [keys, *raw], outs)
     stages = (NEAR, DIRECT, PASSED)
     key_set = gathered(keys)
     value_set = gathered(turned)
@@ -438,7 +433,7 @@
             total = sum(len(part) for part in stages)
             outs += [((heads, length), F32), ((2 * heads * total, length), F32)]
             outs += [((SHIFT_ROWS, length), BF16)]
-        args = [keys, *key_set[index], *(tops if last else [])]
+        args = [paired, *key_set[index], *(tops if last else [])]
         body = partial(stats_body, chips, slots)
         top, weight, *rest, ok = call(body, [block_reach], args, outs, flags=len(slots))
         tops.append(top)
@@ -463,15 +458,15 @@
     keep, send = call(body, [allowed[2]], args, outs, scratch)
     got = other_head(send)
 
-    args = [keys, grads, shifts]
+    args = [shifted, keys, grads, shifts]
     running = call(grad_own_body, [], args, [whole])
     sets = (key_set, grad_set, shift_set)
-    args = [keys, *(part[0][1] for part in sets), *running]
+    args = [shifted, *(part[0][1] for part in sets), *running]
     running = call(partial(grad_body, SIBLING), [allowed[0]], args, [whole])
-    args = [keys, *key_set[1], *grad_set[1], *shift_set[1], *running]
+    args = [shifted, *key_set[1], *grad_set[1], *shift_set[1], *running]
     (running,) = call(partial(grad_body, DIRECT), [allowed[1]], args, [whole])
     half, full = length // 2, out_weight.shape[1]
-    inputs = [keep, got, out_weight, far_weight, keys, running]
+    inputs = [keep, got, out_weight, far_weight, shifted, running]
     inputs += [*key_set[2], *grad_set[2], *shift_set[2]]
     inputs = [pltpu.with_memory_space_constraint(a, pltpu.VMEM) for a in inputs]
     mixed, value_grad = pl.pallas_call(

time: 46.7 us -> 46.4 us (level)
  no operation moved by 1% of the time
where the time goes in v5:
time: 46.4 us; the launch traced here: 46.2 us
  waiting for transfers between devices  17.8 us (38%)
  starting transfers between devices  16.2 us (35%)
  Pallas kernels  10.8 us (23%)
  between operations  1.46 us (3%)
    ppermute x8, waiting for transfers between devices, chip_ring(): return lax.ppermute(value, 'seq', pairs)  14.9 us
    ppermute x8, starting transfers between devices, chip_ring(): return lax.ppermute(value, 'seq', pairs)  8 us
    pallas_call x14, Pallas kernels, call(): return list(run(*scalars, *args))  7.9 us
    ppermute x12, starting transfers between devices, sibling(): return lax.ppermute(value, 'seq', [(i, i ^ 1) for i in range(count)])  5.7 us
    ppermute x12, waiting for transfers between devices, sibling(): return lax.ppermute(value, 'seq', [(i, i ^ 1) for i in range(count)])  2.88 us
    ppermute x2, starting transfers between devices, other_head(): return lax.ppermute(value, 'head', [(0, 1), (1, 0)])  2.48 us
    pallas_call x1, Pallas kernels, compute(): pl.pallas_call(final_body, name='final', in_specs=[SMEM] + [VMEM] * len(i...  1.6 us
    pallas_call x1, Pallas kernels, compute(): pl.pallas_call(prepare_body, name='prepare', in_specs=[SMEM] + [HBM] * 4,...  1.28 us
  transfers between devices with their start and end apart: 22, of which 11 were waited for; matrix products, arithmetic and copies ran while one was open for 0% of the time, Pallas kernels for 17%

profile of v5, /device:TPU:17, one launch (start us, length us, event | category | flops | bytes accessed | tf_op | source)
XLA Modules:
  0.0 46.2 jit_solution(5119449186139513499)
XLA Ops:
  0.6 0.0 copy-start
  1.3 1.3 %prepare.1 = (bf16[528,128]{1,0:T(8,128)(2,1)S(1)}, bf16[256,256]{1,0:T(8,128)(2,1)S(1)}, bf16[256,256]{1,0:T(8,128)(2,1)S(1)}) custom-call(s32[1]{0:T(128)S(6)} %copy.8.reach_ref, bf16[256,256]{1,0:T(8,128)(2,1)} %q_in.1, f32[4,256]{1,0:T(4,128)} %bitcast.1, bf16[256,256]{1,0:T(8,128)(2,1)} %v_in.1, bf16[256,256]{1,0:T(8,128)(2,1)} %g_in.1), custom_call_target="tpu_custom_call" | custom-call | tf_op jit(solution)/shard_map/prepare/pallas_call | solution.py:400
  2.6 0.7 %collective-permute-start = (bf16[528,128]{1,0:T(8,128)(2,1)S(1)}, bf16[528,128]{1,0:T(8,128)(2,1)S(1)}, u32[]{:S(2)}, u32[]{:S(2)}) collective-permute-start(bf16[528,128]{1,0:T(8,128)(2,1)S(1)} %get-tuple-element.32.k_ref.refs_0_.key), channel_id=1, source_target_pairs={{0,2},{2,0},{4,6},{6,4},{8,10},{10,8},{12,14},{14,12},{16,18},{18,... | collective-permute-start | bytes 405512 | tf_op jit(solution)/shard_map/ppermute | solution.py:22
  3.4 0.2 shard_map.77
  3.5 0.1 collective-permute-start.5
  3.6 0.7 %collective-permute-done.refs_1_.refs_0_ = bf16[528,128]{1,0:T(8,128)(2,1)S(1)} collective-permute-done((bf16[528,128]{1,0:T(8,128)(2,1)S(1)}, bf16[528,128]{1,0:T(8,128)(2,1)S(1)}, u32[]{:S(2)}, u32[]{:S(2)}) %collective-permute-start) | collective-permute-done | bytes 135200 | tf_op jit(solution)/shard_map/ppermute | solution.py:22
  4.4 1.2 %collective-permute-start.1 = (bf16[1056,128]{1,0:T(8,128)(2,1)S(1)}, bf16[1056,128]{1,0:T(8,128)(2,1)S(1)}, u32[]{:S(2)}, u32[]{:S(2)}) collective-permute-start(bf16[1056,128]{1,0:T(8,128)(2,1)S(1)} %shard_map.78), channel_id=1, source_target_pairs={{0,4},{2,0},{4,8},{6,2},{8,12},{10,6},{12,16},{14,10},{16,20},{18,... | collective-permute-start | bytes 811016 | tf_op jit(solution)/shard_map/ppermute | solution.py:32
  5.6 0.2 collective-permute-start.2
  5.7 0.0 collective-permute-done.5.refs_1_.sib
  5.8 0.4 collective-permute-start.6
  6.2 1.5 %collective-permute-start.7 = (bf16[512,256]{1,0:T(8,128)(2,1)S(1)}, bf16[512,256]{1,0:T(8,128)(2,1)S(1)}, u32[]{:S(2)}, u32[]{:S(2)}) collective-permute-start(bf16[512,256]{1,0:T(8,128)(2,1)S(1)} %shard_map.82), channel_id=1, source_target_pairs={{0,8},{2,0},{4,12},{6,4},{8,16},{10,2},{12,20},{14,6},{16,24},{18,... | collective-permute-start | bytes 786440 | tf_op jit(solution)/shard_map/ppermute | solution.py:32
  7.7 0.7 %collective-permute-start.12 = (bf16[256,256]{1,0:T(8,128)(2,1)S(1)}, bf16[256,256]{1,0:T(8,128)(2,1)S(1)}, u32[]{:S(2)}, u32[]{:S(2)}) collective-permute-start(bf16[256,256]{1,0:T(8,128)(2,1)S(1)} %get-tuple-element.56.refs_0_.grad), channel_id=1, source_target_pairs={{0,2},{2,0},{4,6},{6,4},{8,10},{10,8},{12,14},{14,12},{16,18},{18,... | collective-permute-start | bytes 393224 | tf_op jit(solution)/shard_map/ppermute | solution.py:22
  8.4 1.0 %collective-permute-done.12.refs_1_ = bf16[256,256]{1,0:T(8,128)(2,1)S(1)} collective-permute-done((bf16[256,256]{1,0:T(8,128)(2,1)S(1)}, bf16[256,256]{1,0:T(8,128)(2,1)S(1)}, u32[]{:S(2)}, u32[]{:S(2)}) %collective-permute-start.12) | collective-permute-done | bytes 131104 | tf_op jit(solution)/shard_map/ppermute | solution.py:22
  9.4 2.3 %collective-permute-start.13 = (bf16[512,256]{1,0:T(8,128)(2,1)S(1)}, bf16[512,256]{1,0:T(8,128)(2,1)S(1)}, u32[]{:S(2)}, u32[]{:S(2)}) collective-permute-start(bf16[512,256]{1,0:T(8,128)(2,1)S(1)} %shard_map.86), channel_id=1, source_target_pairs={{0,4},{2,0},{4,8},{6,2},{8,12},{10,6},{12,16},{14,10},{16,20},{18,... | collective-permute-start | bytes 786440 | tf_op jit(solution)/shard_map/ppermute | solution.py:32
  11.7 1.2 %collective-permute-done.1.refs_0_ = bf16[1056,128]{1,0:T(8,128)(2,1)S(1)} collective-permute-done((bf16[1056,128]{1,0:T(8,128)(2,1)S(1)}, bf16[1056,128]{1,0:T(8,128)(2,1)S(1)}, u32[]{:S(2)}, u32[]{:S(2)}) %collective-permute-start.1) | collective-permute-done | bytes 270368 | tf_op jit(solution)/shard_map/ppermute | solution.py:32
  12.9 0.5 %collective-permute-start.14 = (bf16[512,256]{1,0:T(8,128)(2,1)S(1)}, bf16[512,256]{1,0:T(8,128)(2,1)S(1)}, u32[]{:S(2)}, u32[]{:S(2)}) collective-permute-start(bf16[512,256]{1,0:T(8,128)(2,1)S(1)} %shard_map.86), channel_id=1, source_target_pairs={{0,8},{2,0},{4,12},{6,4},{8,16},{10,2},{12,20},{14,6},{16,24},{18,... | collective-permute-start | bytes 786440 | tf_op jit(solution)/shard_map/ppermute | solution.py:32
  13.4 0.5 %collective-permute-done.2.refs_1_ = bf16[1056,128]{1,0:T(8,128)(2,1)S(1)} collective-permute-done((bf16[1056,128]{1,0:T(8,128)(2,1)S(1)}, bf16[1056,128]{1,0:T(8,128)(2,1)S(1)}, u32[]{:S(2)}, u32[]{:S(2)}) %collective-permute-start.2) | collective-permute-done | bytes 270368 | tf_op jit(solution)/shard_map/ppermute | solution.py:32
  13.9 0.0 copy-done
  13.9 1.2 %collective-permute-start.11 = (bf16[256,1024]{1,0:T(8,128)(2,1)S(1)}, bf16[256,1024]{1,0:T(8,128)(2,1)S(1)}, u32[]{:S(2)}, u32[]{:S(2)}) collective-permute-start(bf16[256,1024]{1,0:T(8,128)(2,1)S(1)} %copy-done), channel_id=1, source_target_pairs={{0,1},{1,0},{2,3},{3,2},{4,5},{5,4},{6,7},{7,6},{8,9},{9,8},{10,11... | collective-permute-start | bytes 1572872 | tf_op jit(solution)/shard_map/ppermute | solution.py:36
  15.2 3.4 %collective-permute-done.6.refs_0_ = bf16[512,256]{1,0:T(8,128)(2,1)S(1)} collective-permute-done((bf16[512,256]{1,0:T(8,128)(2,1)S(1)}, bf16[512,256]{1,0:T(8,128)(2,1)S(1)}, u32[]{:S(2)}, u32[]{:S(2)}) %collective-permute-start.6) | collective-permute-done | bytes 262176 | tf_op jit(solution)/shard_map/ppermute | solution.py:32
  18.6 0.3 collective-permute-start.3
  18.8 0.8 %collective-permute-done.7.refs_1_ = bf16[512,256]{1,0:T(8,128)(2,1)S(1)} collective-permute-done((bf16[512,256]{1,0:T(8,128)(2,1)S(1)}, bf16[512,256]{1,0:T(8,128)(2,1)S(1)}, u32[]{:S(2)}, u32[]{:S(2)}) %collective-permute-start.7) | collective-permute-done | bytes 262176 | tf_op jit(solution)/shard_map/ppermute | solution.py:32
  19.6 0.0 collective-permute-start.4
  19.6 4.6 %collective-permute-done.13.refs_2_ = bf16[512,256]{1,0:T(8,128)(2,1)S(1)} collective-permute-done((bf16[512,256]{1,0:T(8,128)(2,1)S(1)}, bf16[512,256]{1,0:T(8,128)(2,1)S(1)}, u32[]{:S(2)}, u32[]{:S(2)}) %collective-permute-start.13) | collective-permute-done | bytes 262176 | tf_op jit(solution)/shard_map/ppermute | solution.py:32
  24.2 0.3 collective-permute-start.8
  24.4 0.8 %collective-permute-done.14.refs_3_ = bf16[512,256]{1,0:T(8,128)(2,1)S(1)} collective-permute-done((bf16[512,256]{1,0:T(8,128)(2,1)S(1)}, bf16[512,256]{1,0:T(8,128)(2,1)S(1)}, u32[]{:S(2)}, u32[]{:S(2)}) %collective-permute-start.14) | collective-permute-done | bytes 262176 | tf_op jit(solution)/shard_map/ppermute | solution.py:32
  25.3 0.0 collective-permute-start.9
  25.3 0.0 collective-permute-done.3.refs_0_
  25.3 0.5 %collective-permute-start.18 = (bf16[512,256]{1,0:T(8,128)(2,1)S(1)}, bf16[512,256]{1,0:T(8,128)(2,1)S(1)}, u32[]{:S(2)}, u32[]{:S(2)}) collective-permute-start(bf16[512,256]{1,0:T(8,128)(2,1)S(1)} %collective-permute-done.13.refs_2_), channel_id=1, source_target_pairs={{0,2},{2,0},{4,6},{6,4},{8,10},{10,8},{12,14},{14,12},{16,18},{18,... | collective-permute-start | bytes 786440 | tf_op jit(solution)/shard_map/ppermute | solution.py:22
  25.8 0.0 collective-permute-done.4.refs_1_
  25.8 0.1 collective-permute-start.19
  25.9 1.0 %shard_map.79 = (f32[16,256]{1,0:T(8,128)S(1)}, bf16[4096,128]{1,0:T(8,128)(2,1)S(1)}, s32[2]{0:T(128)S(4)}) custom-call(s32[1]{0:T(128)S(6)} %copy.8.reach_ref, bf16[1024,128]{1,0:T(8,128)(2,1)S(1)} %get-tuple-element.35.paired, bf16[528,128]{1,0:T(8,128)(2,1)S(1)} %get-tuple-element.32.k_ref.refs_0_.key, ...), custom_call_target="tpu_custom_call" | custom-call | tf_op jit(solution)/shard_map/pallas_call | solution.py:375
  26.8 0.3 shard_map.83
  27.1 1.5 %shard_map.80 = (f32[32,256]{1,0:T(8,128)S(1)}, bf16[8192,128]{1,0:T(8,128)(2,1)S(1)}, s32[4]{0:T(128)S(4)}) custom-call(s32[1]{0:T(128)S(6)} %copy.8.reach_ref, bf16[1024,128]{1,0:T(8,128)(2,1)S(1)} %get-tuple-element.35.paired, bf16[1056,128]{1,0:T(8,128)(2,1)S(1)} %collective-permute-done.1.refs_0_, bf16[1056,128]{1,0:T(8,128)(2,1)S(1)} %collective-permute-done.2.refs_1_), custom_call_target="tpu_custom_call" | custom-call | tf_op jit(solution)/shard_map/pallas_call | solution.py:375
  28.7 1.2 %shard_map.81 = (f32[24,256]{1,0:T(8,128)}, bf16[6144,128]{1,0:T(8,128)(2,1)S(1)}, f32[4,256]{1,0:T(4,128)S(1)}, f32[72,256]{1,0:T(8,128)S(1)}, bf16[16,256]{1,0:T(8,128)(2,1)S(1)}, /*index=5*/s32[3]{0:T(128)S(4)}) custom-call(s32[1]{0:T(128)S(6)} %copy.8.reach_ref, bf16[1024,128]{1,0:T(8,128)(2,1)S(1)} %get-tuple-element.35.paired, ...), custom_call_target="tpu_custom_call" | custom-call | tf_op jit(solution)/shard_map/pallas_call | solution.py:375
  29.9 0.7 %shard_map.84.refs_5_ = f32[256,256]{1,0:T(8,128)S(1)} custom-call(s32[2]{0:T(128)S(4)} %get-tuple-element.47.ok_sib.ok_ref, s32[4]{0:T(128)S(4)} %get-tuple-element.48.ok.ok_ref, bf16[512,256]{1,0:T(8,128)(2,1)S(1)} %collective-permute-done.6.refs_0_, bf16[512,256]{1,0:T(8,128)(2,1)S(1)} %collective-permute-done.7.refs_1_, ...), custom_call_target="tpu_custom_call" | custom-call | tf_op jit(solution)/shard_map/pallas_call | solution.py:375
  30.6 0.0 collective-permute-done.8.refs_0_
  30.6 0.0 collective-permute-done.9.refs_1_
  30.6 0.4 shard_map.85
  31.0 1.3 %collective-permute-start.10 = (bf16[128,256]{1,0:T(8,128)(2,1)S(1)}, bf16[128,256]{1,0:T(8,128)(2,1)S(1)}, u32[]{:S(2)}, u32[]{:S(2)}) collective-permute-start(bf16[128,256]{1,0:T(8,128)(2,1)S(1)} %get-tuple-element.54), channel_id=1, source_target_pairs={{0,1},{1,0},{2,3},{3,2},{4,5},{5,4},{6,7},{7,6},{8,9},{9,8},{10,11... | collective-permute-start | bytes 196616 | tf_op jit(solution)/shard_map/ppermute | solution.py:36
  32.3 0.0 collective-permute-start.15
  32.3 1.1 %collective-permute-done.15.refs_1_.refs_2_ = bf16[16,256]{1,0:T(8,128)(2,1)S(1)} collective-permute-done((bf16[16,256]{1,0:T(8,128)(2,1)S(1)}, bf16[16,256]{1,0:T(8,128)(2,1)S(1)}, u32[]{:S(2)}, u32[]{:S(2)}) %collective-permute-start.15) | collective-permute-done | bytes 8224 | tf_op jit(solution)/shard_map/ppermute | solution.py:22
  33.5 1.6 %collective-permute-start.16 = (bf16[32,256]{1,0:T(8,128)(2,1)S(1)}, bf16[32,256]{1,0:T(8,128)(2,1)S(1)}, u32[]{:S(2)}, u32[]{:S(2)}) collective-permute-start(bf16[32,256]{1,0:T(8,128)(2,1)S(1)} %shard_map.87), channel_id=1, source_target_pairs={{0,4},{2,0},{4,8},{6,2},{8,12},{10,6},{12,16},{14,10},{16,20},{18,... | collective-permute-start | bytes 49160 | tf_op jit(solution)/shard_map/ppermute | solution.py:32
  35.1 1.2 %collective-permute-done.16.refs_4_ = bf16[32,256]{1,0:T(8,128)(2,1)S(1)} collective-permute-done((bf16[32,256]{1,0:T(8,128)(2,1)S(1)}, bf16[32,256]{1,0:T(8,128)(2,1)S(1)}, u32[]{:S(2)}, u32[]{:S(2)}) %collective-permute-start.16) | collective-permute-done | bytes 16416 | tf_op jit(solution)/shard_map/ppermute | solution.py:32
  36.3 0.2 collective-permute-start.17
  36.6 2.3 %collective-permute-done.17.refs_5_ = bf16[32,256]{1,0:T(8,128)(2,1)S(1)} collective-permute-done((bf16[32,256]{1,0:T(8,128)(2,1)S(1)}, bf16[32,256]{1,0:T(8,128)(2,1)S(1)}, u32[]{:S(2)}, u32[]{:S(2)}) %collective-permute-start.17) | collective-permute-done | bytes 16416 | tf_op jit(solution)/shard_map/ppermute | solution.py:32
  38.9 3.1 %collective-permute-start.20 = (bf16[32,256]{1,0:T(8,128)(2,1)S(1)}, bf16[32,256]{1,0:T(8,128)(2,1)S(1)}, u32[]{:S(2)}, u32[]{:S(2)}) collective-permute-start(bf16[32,256]{1,0:T(8,128)(2,1)S(1)} %collective-permute-done.16.refs_4_), channel_id=1, source_target_pairs={{0,2},{2,0},{4,6},{6,4},{8,10},{10,8},{12,14},{14,12},{16,18},{18,... | collective-permute-start | bytes 49160 | tf_op jit(solution)/shard_map/ppermute | solution.py:22
  42.0 0.0 collective-permute-done.11.far_ref
  42.0 0.0 collective-permute-start.21
  42.0 0.5 %shard_map.88.refs_3_ = f32[256,256]{1,0:T(8,128)S(1)} custom-call(bf16[1024,128]{1,0:T(8,128)(2,1)S(1)} %get-tuple-element.55.mine, bf16[528,128]{1,0:T(8,128)(2,1)S(1)} %get-tuple-element.32.k_ref.refs_0_.key, bf16[256,256]{1,0:T(8,128)(2,1)S(1)} %get-tuple-element.56.refs_0_.grad, bf16[16,256]{1,0:T(8,128)(2,1)S(1)} %get-tuple-element.59.refs_0_.shift), custom_call_target="tpu_custom_call" | custom-call | tf_op jit(solution)/shard_map/pallas_call | solution.py:375
  42.5 0.5 %shard_map.89.refs_6_ = f32[256,256]{1,0:T(8,128)S(1)} custom-call(s32[2]{0:T(128)S(4)} %get-tuple-element.47.ok_sib.ok_ref, bf16[1024,128]{1,0:T(8,128)(2,1)S(1)} %get-tuple-element.55.mine, bf16[528,128]{1,0:T(8,128)(2,1)S(1)} %collective-permute-done.refs_1_.refs_0_, bf16[256,256]{1,0:T(8,128)(2,1)S(1)} %collective-permute-done.12.refs_1_, ...), custom_call_target="tpu_custom_call" | custom-call | tf_op jit(solution)/shard_map/pallas_call | solution.py:375
  43.0 1.5 %shard_map.90.acc_in = f32[256,256]{1,0:T(8,128)S(1)} custom-call(s32[4]{0:T(128)S(4)} %get-tuple-element.48.ok.ok_ref, bf16[1024,128]{1,0:T(8,128)(2,1)S(1)} %get-tuple-element.55.mine, bf16[1056,128]{1,0:T(8,128)(2,1)S(1)} %collective-permute-done.1.refs_0_, bf16[1056,128]{1,0:T(8,128)(2,1)S(1)} %collective-permute-done.2.refs_1_, ...), custom_call_target="tpu_custom_call" | custom-call | tf_op jit(solution)/shard_map/pallas_call | solution.py:375
  44.6 0.0 collective-permute-done.18.refs_2_
  44.6 0.0 collective-permute-done.19.refs_3_
  44.6 0.0 collective-permute-done.20.refs_4_
  44.6 0.0 collective-permute-done.21.refs_5_
  44.6 0.0 collective-permute-done.10.got_ref
  44.6 1.6 %final.1 = (bf16[128,1024]{1,0:T(8,128)(2,1)}, bf16[256,256]{1,0:T(8,128)(2,1)}) custom-call(s32[3]{0:T(128)S(4)} %get-tuple-element.40.ok_ref, bf16[128,256]{1,0:T(8,128)(2,1)S(1)} %get-tuple-element.53.keep_ref, bf16[128,256]{1,0:T(8,128)(2,1)S(1)} %collective-permute-done.10.got_ref, bf16[256,1024]{1,0:T(8,128)(2,1)S(1)} %copy-done, ...), custom_call_target="tpu_custom_call" | custom-call | tf_op jit(solution)/shard_map/final/pallas_call | solution.py:472
  (4 shorter events, 0.1 us)
Async XLA Ops:
  0.6 13.3 %copy-start = (bf16[256,1024]{1,0:T(8,128)(2,1)S(1)}, bf16[256,1024]{1,0:T(8,128)(2,1)}, u32[]{:S(2)}) copy-start(bf16[256,1024]{1,0:T(8,128)(2,1)} %near_ref.1) | copy-start | bytes 1572868
  2.6 1.7 %collective-permute-start = (bf16[528,128]{1,0:T(8,128)(2,1)S(1)}, bf16[528,128]{1,0:T(8,128)(2,1)S(1)}, u32[]{:S(2)}, u32[]{:S(2)}) collective-permute-start(bf16[528,128]{1,0:T(8,128)(2,1)S(1)} %get-tuple-element.32.k_ref.refs_0_.key), channel_id=1, source_target_pairs={{0,2},{2,0},{4,6},{6,4},{8,10},{10,8},{12,14},{14,12},{16,18},{18,... | collective-permute-start | bytes 405512 | tf_op jit(solution)/shard_map/ppermute | solution.py:22
  3.5 2.2 %collective-permute-start.5 = (bf16[256,256]{1,0:T(8,128)(2,1)S(1)}, bf16[256,256]{1,0:T(8,128)(2,1)S(1)}, u32[]{:S(2)}, u32[]{:S(2)}) collective-permute-start(bf16[256,256]{1,0:T(8,128)(2,1)S(1)} %get-tuple-element.41.refs_0_.own), channel_id=1, source_target_pairs={{0,2},{2,0},{4,6},{6,4},{8,10},{10,8},{12,14},{14,12},{16,18},{18,... | collective-permute-start | bytes 393224 | tf_op jit(solution)/shard_map/ppermute | solution.py:22
  4.4 8.6 %collective-permute-start.1 = (bf16[1056,128]{1,0:T(8,128)(2,1)S(1)}, bf16[1056,128]{1,0:T(8,128)(2,1)S(1)}, u32[]{:S(2)}, u32[]{:S(2)}) collective-permute-start(bf16[1056,128]{1,0:T(8,128)(2,1)S(1)} %shard_map.78), channel_id=1, source_target_pairs={{0,4},{2,0},{4,8},{6,2},{8,12},{10,6},{12,16},{14,10},{16,20},{18,... | collective-permute-start | bytes 811016 | tf_op jit(solution)/shard_map/ppermute | solution.py:32
  5.6 8.4 %collective-permute-start.2 = (bf16[1056,128]{1,0:T(8,128)(2,1)S(1)}, bf16[1056,128]{1,0:T(8,128)(2,1)S(1)}, u32[]{:S(2)}, u32[]{:S(2)}) collective-permute-start(bf16[1056,128]{1,0:T(8,128)(2,1)S(1)} %shard_map.78), channel_id=1, source_target_pairs={{0,8},{2,0},{4,12},{6,4},{8,16},{10,2},{12,20},{14,6},{16,24},{18,... | collective-permute-start | bytes 811016 | tf_op jit(solution)/shard_map/ppermute | solution.py:32
  5.8 12.8 %collective-permute-start.6 = (bf16[512,256]{1,0:T(8,128)(2,1)S(1)}, bf16[512,256]{1,0:T(8,128)(2,1)S(1)}, u32[]{:S(2)}, u32[]{:S(2)}) collective-permute-start(bf16[512,256]{1,0:T(8,128)(2,1)S(1)} %shard_map.82), channel_id=1, source_target_pairs={{0,4},{2,0},{4,8},{6,2},{8,12},{10,6},{12,16},{14,10},{16,20},{18,... | collective-permute-start | bytes 786440 | tf_op jit(solution)/shard_map/ppermute | solution.py:32
  6.2 13.5 %collective-permute-start.7 = (bf16[512,256]{1,0:T(8,128)(2,1)S(1)}, bf16[512,256]{1,0:T(8,128)(2,1)S(1)}, u32[]{:S(2)}, u32[]{:S(2)}) collective-permute-start(bf16[512,256]{1,0:T(8,128)(2,1)S(1)} %shard_map.82), channel_id=1, source_target_pairs={{0,8},{2,0},{4,12},{6,4},{8,16},{10,2},{12,20},{14,6},{16,24},{18,... | collective-permute-start | bytes 786440 | tf_op jit(solution)/shard_map/ppermute | solution.py:32
  7.7 1.6 %collective-permute-start.12 = (bf16[256,256]{1,0:T(8,128)(2,1)S(1)}, bf16[256,256]{1,0:T(8,128)(2,1)S(1)}, u32[]{:S(2)}, u32[]{:S(2)}) collective-permute-start(bf16[256,256]{1,0:T(8,128)(2,1)S(1)} %get-tuple-element.56.refs_0_.grad), channel_id=1, source_target_pairs={{0,2},{2,0},{4,6},{6,4},{8,10},{10,8},{12,14},{14,12},{16,18},{18,... | collective-permute-start | bytes 393224 | tf_op jit(solution)/shard_map/ppermute | solution.py:22
  9.4 14.8 %collective-permute-start.13 = (bf16[512,256]{1,0:T(8,128)(2,1)S(1)}, bf16[512,256]{1,0:T(8,128)(2,1)S(1)}, u32[]{:S(2)}, u32[]{:S(2)}) collective-permute-start(bf16[512,256]{1,0:T(8,128)(2,1)S(1)} %shard_map.86), channel_id=1, source_target_pairs={{0,4},{2,0},{4,8},{6,2},{8,12},{10,6},{12,16},{14,10},{16,20},{18,... | collective-permute-start | bytes 786440 | tf_op jit(solution)/shard_map/ppermute | solution.py:32
  12.9 12.3 %collective-permute-start.14 = (bf16[512,256]{1,0:T(8,128)(2,1)S(1)}, bf16[512,256]{1,0:T(8,128)(2,1)S(1)}, u32[]{:S(2)}, u32[]{:S(2)}) collective-permute-start(bf16[512,256]{1,0:T(8,128)(2,1)S(1)} %shard_map.86), channel_id=1, source_target_pairs={{0,8},{2,0},{4,12},{6,4},{8,16},{10,2},{12,20},{14,6},{16,24},{18,... | collective-permute-start | bytes 786440 | tf_op jit(solution)/shard_map/ppermute | solution.py:32
  13.9 28.1 %collective-permute-start.11 = (bf16[256,1024]{1,0:T(8,128)(2,1)S(1)}, bf16[256,1024]{1,0:T(8,128)(2,1)S(1)}, u32[]{:S(2)}, u32[]{:S(2)}) collective-permute-start(bf16[256,1024]{1,0:T(8,128)(2,1)S(1)} %copy-done), channel_id=1, source_target_pairs={{0,1},{1,0},{2,3},{3,2},{4,5},{5,4},{6,7},{7,6},{8,9},{9,8},{10,11... | collective-permute-start | bytes 1572872 | tf_op jit(solution)/shard_map/ppermute | solution.py:36
  18.6 6.7 %collective-permute-start.3 = (bf16[1056,128]{1,0:T(8,128)(2,1)S(1)}, bf16[1056,128]{1,0:T(8,128)(2,1)S(1)}, u32[]{:S(2)}, u32[]{:S(2)}) collective-permute-start(bf16[1056,128]{1,0:T(8,128)(2,1)S(1)} %collective-permute-done.1.refs_0_), channel_id=1, source_target_pairs={{0,2},{2,0},{4,6},{6,4},{8,10},{10,8},{12,14},{14,12},{16,18},{18,... | collective-permute-start | bytes 811016 | tf_op jit(solution)/shard_map/ppermute | solution.py:22
  19.6 6.2 %collective-permute-start.4 = (bf16[1056,128]{1,0:T(8,128)(2,1)S(1)}, bf16[1056,128]{1,0:T(8,128)(2,1)S(1)}, u32[]{:S(2)}, u32[]{:S(2)}) collective-permute-start(bf16[1056,128]{1,0:T(8,128)(2,1)S(1)} %collective-permute-done.2.refs_1_), channel_id=1, source_target_pairs={{0,2},{2,0},{4,6},{6,4},{8,10},{10,8},{12,14},{14,12},{16,18},{18,... | collective-permute-start | bytes 811016 | tf_op jit(solution)/shard_map/ppermute | solution.py:22
  24.2 6.4 %collective-permute-start.8 = (bf16[512,256]{1,0:T(8,128)(2,1)S(1)}, bf16[512,256]{1,0:T(8,128)(2,1)S(1)}, u32[]{:S(2)}, u32[]{:S(2)}) collective-permute-start(bf16[512,256]{1,0:T(8,128)(2,1)S(1)} %collective-permute-done.6.refs_0_), channel_id=1, source_target_pairs={{0,2},{2,0},{4,6},{6,4},{8,10},{10,8},{12,14},{14,12},{16,18},{18,... | collective-permute-start | bytes 786440 | tf_op jit(solution)/shard_map/ppermute | solution.py:22
  25.3 5.3 %collective-permute-start.9 = (bf16[512,256]{1,0:T(8,128)(2,1)S(1)}, bf16[512,256]{1,0:T(8,128)(2,1)S(1)}, u32[]{:S(2)}, u32[]{:S(2)}) collective-permute-start(bf16[512,256]{1,0:T(8,128)(2,1)S(1)} %collective-permute-done.7.refs_1_), channel_id=1, source_target_pairs={{0,2},{2,0},{4,6},{6,4},{8,10},{10,8},{12,14},{14,12},{16,18},{18,... | collective-permute-start | bytes 786440 | tf_op jit(solution)/shard_map/ppermute | solution.py:22
  25.3 19.3 %collective-permute-start.18 = (bf16[512,256]{1,0:T(8,128)(2,1)S(1)}, bf16[512,256]{1,0:T(8,128)(2,1)S(1)}, u32[]{:S(2)}, u32[]{:S(2)}) collective-permute-start(bf16[512,256]{1,0:T(8,128)(2,1)S(1)} %collective-permute-done.13.refs_2_), channel_id=1, source_target_pairs={{0,2},{2,0},{4,6},{6,4},{8,10},{10,8},{12,14},{14,12},{16,18},{18,... | collective-permute-start | bytes 786440 | tf_op jit(solution)/shard_map/ppermute | solution.py:22
  25.8 18.8 %collective-permute-start.19 = (bf16[512,256]{1,0:T(8,128)(2,1)S(1)}, bf16[512,256]{1,0:T(8,128)(2,1)S(1)}, u32[]{:S(2)}, u32[]{:S(2)}) collective-permute-start(bf16[512,256]{1,0:T(8,128)(2,1)S(1)} %collective-permute-done.14.refs_3_), channel_id=1, source_target_pairs={{0,2},{2,0},{4,6},{6,4},{8,10},{10,8},{12,14},{14,12},{16,18},{18,... | collective-permute-start | bytes 786440 | tf_op jit(solution)/shard_map/ppermute | solution.py:22
  31.0 13.6 %collective-permute-start.10 = (bf16[128,256]{1,0:T(8,128)(2,1)S(1)}, bf16[128,256]{1,0:T(8,128)(2,1)S(1)}, u32[]{:S(2)}, u32[]{:S(2)}) collective-permute-start(bf16[128,256]{1,0:T(8,128)(2,1)S(1)} %get-tuple-element.54), channel_id=1, source_target_pairs={{0,1},{1,0},{2,3},{3,2},{4,5},{5,4},{6,7},{7,6},{8,9},{9,8},{10,11... | collective-permute-start | bytes 196616 | tf_op jit(solution)/shard_map/ppermute | solution.py:36
  32.3 1.2 %collective-permute-start.15 = (bf16[16,256]{1,0:T(8,128)(2,1)S(1)}, bf16[16,256]{1,0:T(8,128)(2,1)S(1)}, u32[]{:S(2)}, u32[]{:S(2)}) collective-permute-start(bf16[16,256]{1,0:T(8,128)(2,1)S(1)} %get-tuple-element.59.refs_0_.shift), channel_id=1, source_target_pairs={{0,2},{2,0},{4,6},{6,4},{8,10},{10,8},{12,14},{14,12},{16,18},{18,... | collective-permute-start | bytes 24584 | tf_op jit(solution)/shard_map/ppermute | solution.py:22
  33.5 2.9 %collective-permute-start.16 = (bf16[32,256]{1,0:T(8,128)(2,1)S(1)}, bf16[32,256]{1,0:T(8,128)(2,1)S(1)}, u32[]{:S(2)}, u32[]{:S(2)}) collective-permute-start(bf16[32,256]{1,0:T(8,128)(2,1)S(1)} %shard_map.87), channel_id=1, source_target_pairs={{0,4},{2,0},{4,8},{6,2},{8,12},{10,6},{12,16},{14,10},{16,20},{18,... | collective-permute-start | bytes 49160 | tf_op jit(solution)/shard_map/ppermute | solution.py:32
  36.3 2.6 %collective-permute-start.17 = (bf16[32,256]{1,0:T(8,128)(2,1)S(1)}, bf16[32,256]{1,0:T(8,128)(2,1)S(1)}, u32[]{:S(2)}, u32[]{:S(2)}) collective-permute-start(bf16[32,256]{1,0:T(8,128)(2,1)S(1)} %shard_map.87), channel_id=1, source_target_pairs={{0,8},{2,0},{4,12},{6,4},{8,16},{10,2},{12,20},{14,6},{16,24},{18,... | collective-permute-start | bytes 49160 | tf_op jit(solution)/shard_map/ppermute | solution.py:32
  38.9 5.7 %collective-permute-start.20 = (bf16[32,256]{1,0:T(8,128)(2,1)S(1)}, bf16[32,256]{1,0:T(8,128)(2,1)S(1)}, u32[]{:S(2)}, u32[]{:S(2)}) collective-permute-start(bf16[32,256]{1,0:T(8,128)(2,1)S(1)} %collective-permute-done.16.refs_4_), channel_id=1, source_target_pairs={{0,2},{2,0},{4,6},{6,4},{8,10},{10,8},{12,14},{14,12},{16,18},{18,... | collective-permute-start | bytes 49160 | tf_op jit(solution)/shard_map/ppermute | solution.py:22
  42.0 2.6 %collective-permute-start.21 = (bf16[32,256]{1,0:T(8,128)(2,1)S(1)}, bf16[32,256]{1,0:T(8,128)(2,1)S(1)}, u32[]{:S(2)}, u32[]{:S(2)}) collective-permute-start(bf16[32,256]{1,0:T(8,128)(2,1)S(1)} %collective-permute-done.17.refs_5_), channel_id=1, source_target_pairs={{0,2},{2,0},{4,6},{6,4},{8,10},{10,8},{12,14},{14,12},{16,18},{18,... | collective-permute-start | bytes 49160 | tf_op jit(solution)/shard_map/ppermute | solution.py:22
